TPU v7x, 32 devices: a whole 2x2x4 slice. The times are simulated.
32 devices in a mesh: rep: 8 (over z, core), shard: 4 (over y, x).
Axes of the slice: x: 2, y: 2, z: 4, core: 2. Of those that a mesh axis runs over, the one named last changes fastest.
Arguments:
- inputs: bfloat16 [32, 1024, 1024], P(('rep', 'shard')), may hold values from -6 to 6
- lengths: int32 [32], P(('rep', 'shard')), may hold values from 256 to 1024, as said below
- gain_attn: bfloat16 [1024], P('shard'), may hold values from 0.099609375 to 1.8984375
- w_query: bfloat16 [1024, 1024], P('shard'), may hold values from -0.1875 to 0.1875
- w_key: bfloat16 [1024, 512], P('shard'), may hold values from -0.1875 to 0.1875
- w_value: bfloat16 [1024, 512], P('shard'), may hold values from -0.1875 to 0.1875
- gain_query: bfloat16 [64], P('shard'), may hold values from 0.099609375 to 1.8984375
- gain_key: bfloat16 [64], P('shard'), may hold values from 0.099609375 to 1.8984375
- w_out: bfloat16 [1024, 1024], P('shard'), may hold values from -3 to 3
- gain_mlp: bfloat16 [1024], P('shard'), may hold values from 0.099609375 to 1.8984375
- w_gate: bfloat16 [1024, 4608], P('shard'), may hold values from -0.1875 to 0.1875
- w_up: bfloat16 [1024, 4608], P('shard'), may hold values from -0.1875 to 0.1875
- w_down: bfloat16 [4608, 1024], P('shard'), may hold values from -0.09375 to 0.09375
- cotangent: bfloat16 [32, 1024, 1024], P(('rep', 'shard')), may hold values from -6 to 6
Outputs:
- output: bfloat16 [32, 1024, 1024], P(('rep', 'shard'))
- input_grad: bfloat16 [32, 1024, 1024], P(('rep', 'shard'))
- grad_gain_attn: float32 [1024], P('shard')
- grad_query: float32 [1024, 1024], P('shard')
- grad_key: float32 [1024, 512], P('shard')
- grad_value: float32 [1024, 512], P('shard')
- grad_gain_query: float32 [64], P('shard')
- grad_gain_key: float32 [64], P('shard')
- grad_out: float32 [1024, 1024], P('shard')
- grad_gain_mlp: float32 [1024], P('shard')
- grad_gate: float32 [1024, 4608], P('shard')
- grad_up: float32 [1024, 4608], P('shard')
- grad_down: float32 [4608, 1024], P('shard')
- statistics: float32 [3], replicated
Inputs may be any that keep to these rules, and one draw needn't show every extreme that they name: lengths[s] counts the valid leading positions of slot s; some slot has exactly 1024 and some exactly 256.
All inputs are finite; a program needn't handle non-finite values.
Results may differ from a plain program's by a relative error of at most 0.013.
Values may be sent and summed in bfloat16 or wider, within the bound.
A program may use at most 320 MiB of HBM per device.

v0:
```python
from functools import partial
import math

import jax
import jax.numpy as jnp
from jax import lax
from jax.experimental import pallas as pl
from jax.experimental.pallas import tpu as pltpu
from jax.sharding import PartitionSpec as P

EPS = 1e-05
ROPE_BASE = 1000000.0
F32 = jnp.float32
LOW = jnp.bfloat16
LANES = 128
MESH = pl.DeviceIdType.MESH


def rope_tables(row_count, head_width):
    half_width = head_width // 2
    frequency = jnp.power(
        jnp.float32(ROPE_BASE), -jnp.arange(half_width, dtype=jnp.float32) * 2.0 / head_width
    )
    angles = jnp.arange(row_count, dtype=jnp.float32)[:, None] * frequency[None, :]
    cosine, sine = jnp.cos(angles), jnp.sin(angles)
    repeats = LANES // head_width
    return jnp.tile(cosine, (1, 2 * repeats)), jnp.tile(
        jnp.concatenate([-sine, sine], axis=1), (1, repeats)
    )


def nn(left, right):
    return jnp.dot(left, right, preferred_element_type=F32)


def nt(left, right):
    return lax.dot_general(left, right, (((1,), (1,)), ((), ())), preferred_element_type=F32)


def tn(left, right):
    return lax.dot_general(left, right, (((0,), (0,)), ((), ())), preferred_element_type=F32)


def core_swap(x):
    pairs = [(i, i ^ 1) for i in range(lax.axis_size("rep"))]
    return lax.ppermute(x, "rep", pairs)


def place():
    rep = lax.axis_index("rep")
    return lax.axis_index("shard"), lax.div(rep, 2), lax.rem(rep, 2)


def device(shard, group, core):
    return {"rep": 2 * group + core, "shard": shard}


def meet(devices):
    barrier = pltpu.get_barrier_semaphore()
    for where in devices:
        pl.semaphore_signal(barrier, inc=1, device_id=where, device_id_type=MESH)
    pl.semaphore_wait(barrier, len(devices))


def remote(source, target, send, recv, where):
    return pltpu.make_async_remote_copy(
        src_ref=source,
        dst_ref=target,
        send_sem=send,
        recv_sem=recv,
        device_id=where,
        device_id_type=MESH,
    )


def at_rows(ref, start, size):
    return ref.at[pl.ds(pl.multiple_of(start, 8), size), :]


def at(ref, row, rows, column, columns):
    return ref.at[
        pl.ds(pl.multiple_of(row, 8), rows), pl.ds(pl.multiple_of(column, LANES), columns)
    ]


class Copies:
    def __init__(self, send, recv):
        self.send, self.recv, self.used = send, recv, 0

    def __call__(self, source, target, where):
        slot = self.used
        self.used += 1
        return remote(source, target, self.send.at[slot], self.recv.at[slot], where)


def neighbours(me):
    return me + 1 - 2 * lax.rem(me, 2), me + 2 - 4 * lax.div(me, 2), 3 - me


def gather_kernel(shards, wide_parts, tall_parts, count, *refs):
    *refs, send, recv = refs
    sources, targets = refs[: count[0]], refs[count[0] :]
    me, group, core = place()
    half = shards // 2
    partner = device(me, group, 1 - core)
    meet(
        [device(lax.rem(me + k, shards), group, c) for k in range(1, shards) for c in range(2)]
        + [partner]
    )
    copies = Copies(send, recv)
    sent, due = [], []

    def go(source, target, where):
        copy = copies(source, target, where)
        copy.start()
        sent.append(copy.wait_send)
        return copy

    def passed_on(wide):
        fast, slow, _ = neighbours(me)
        later = []
        for block, first, second in wide:
            rows = block(me).shape[0] // 2
            first.wait_recv()
            later.append(go(block(fast).at[pl.ds(0, rows), :], block(fast).at[pl.ds(0, rows), :], device(slow, group, core)))
            second.wait_recv()
            later.append(go(block(slow).at[pl.ds(rows, rows), :], block(slow).at[pl.ds(rows, rows), :], device(fast, group, core)))
        return later

    wide = []
    for source, target, column, to, columns in wide_parts:
        source, target = sources[source], targets[target]
        rows = source.shape[0]
        mine = at(source, 0, rows, column(core), columns)

        def block(shard, target=target, rows=rows, to=to, columns=columns):
            return at(target, shard * rows, rows, to, columns)

        if shards == 4:
            fast, slow, _ = neighbours(me)
            wide.append(
                (
                    block,
                    go(mine, block(me), device(fast, group, core)),
                    go(mine, block(me), device(slow, group, core)),
                )
            )
        else:
            for k in range(1, shards):
                due.append(go(mine, block(me), device(lax.rem(me + k, shards), group, core)))
        due.append(go(at(source, 0, rows, column(1 - core), columns), block(me), partner))
    owner = lax.div(me, half)
    tall = []
    for source, target, row, rows in tall_parts:
        source, target = sources[source], targets[target]
        columns = source.shape[1] // 2

        def block(shard, target=target, rows=rows, columns=columns):
            return at(target, lax.rem(shard, half) * rows, rows, 0, 2 * columns)

        mine = at(source, row, rows, core * columns, columns)
        goal = at(target, lax.rem(me, half) * rows, rows, core * columns, columns)
        steps = [1, 2] if shards == 4 else list(range(1, shards))
        arrivals = []
        for k in steps:
            if shards == 4:
                to = origin = neighbours(me)[k - 1]
            else:
                to, origin = lax.rem(me + k, shards), lax.rem(me + shards - k, shards)
            pair = []
            for side in range(2):
                copy = copies(mine, goal, device(to, group, owner))
                pl.when(core == side)(copy.start)
                sent.append((core == side, copy.wait_send))
                pair.append(copy)
            arrivals.append((lax.div(origin, half) == core, pair))
        whole = copies(
            at(source, row, rows, 0, 2 * columns), block(me), partner
        )
        pl.when(owner != core)(whole.start)
        sent.append((owner != core, whole.wait_send))
        due.append((owner == core, whole))
        if shards == 4:
            tall.append((block, rows // 2, arrivals))
        else:
            for condition, pair in arrivals:
                due.extend((condition, copy) for copy in pair)
    gains, given = sources[-2:], targets[-2:]
    for k in range(1, shards):
        due.append(go(gains[0], given[0].at[me], device(lax.rem(me + k, shards), group, core)))
    due.append(go(gains[0], given[0].at[me], partner))
    due.append(go(gains[1], given[1], partner))
    if shards == 4:
        due.extend(passed_on(wide))
        fast, slow, _ = neighbours(me)
        for block, rows, arrivals in tall:
            for number, (condition, pair) in enumerate(arrivals):
                start = number * rows
                from_, to = (fast, slow) if number == 0 else (slow, fast)
                part = block(from_).at[pl.ds(start, rows), :]
                copy = copies(part, part, device(to, group, core))

                @pl.when(condition)
                def _(pair=pair, copy=copy):
                    for one in pair:
                        one.wait_recv()
                    copy.start()

                sent.append((condition, copy.wait_send))
                due.append((owner != core, copy))
    for item in sent:
        pl.when(item[0])(item[1]) if isinstance(item, tuple) else item()
    for item in due:
        pl.when(item[0])(item[1].wait_recv) if isinstance(item, tuple) else item.wait_recv()


def pack_kernel(shards, chunks, gate_ref, up_ref, down_ref, *refs):
    *packs, sems = refs
    core = lax.rem(lax.axis_index("rep"), 2)
    half = shards // 2
    total, rows = down_ref.shape[0], gate_ref.shape[0]
    piece = total // chunks
    columns = down_ref.shape[1] // 2
    copies = []
    for pack in packs:
        for row, chunk in pack[1]:
            for j, ref in enumerate((gate_ref, up_ref)):
                for i in range(half):
                    start = (core * half + i) * total + chunk * piece
                    copies.append(
                        (
                            at(ref, 0, rows, start, piece),
                            pack[0].at[pl.ds(row, rows), pl.ds((j * half + i) * piece, piece)],
                        )
                    )
            folds = 2 * half * piece // columns
            size = piece // folds
            for i in range(folds):
                copies.append(
                    (
                        at(down_ref, chunk * piece + i * size, size, core * columns, columns),
                        pack[0].at[pl.ds(row + rows, size), pl.ds(i * columns, columns)],
                    )
                )
    copies = [pltpu.make_async_copy(a, b, sems.at[k]) for k, (a, b) in enumerate(copies)]
    for copy in copies:
        copy.start()
    for copy in copies:
        copy.wait()


def add_up(parts, target, rows):
    def some(i, _):
        here = pl.ds(pl.multiple_of(i * rows, rows), rows)
        total = parts[0][here, :].astype(F32)
        for part in parts[1:]:
            total += part[here, :].astype(F32)
        target[here, :] = total.astype(target.dtype)
        return 0

    lax.fori_loop(0, target.shape[0] // rows, some, 0)


def reduce_over_plane(copies, load, shards, grad_ref, level, bufs):
    me, group, core = place()
    rows = level.shape[0]

    def block(shard, start=0, size=rows):
        return at_rows(grad_ref, shard * rows + start, size)

    own = bufs[0]
    local = pltpu.make_async_copy(block(me), own, load.at[0])
    if shards != 4:
        planes = bufs[1]
        out = [
            copies(block(lax.rem(me + k, shards)), planes.at[k - 1], device(lax.rem(me + k, shards), group, core))
            for k in range(1, shards)
        ]

        def start():
            local.start()
            for copy in out:
                copy.start()

        def end():
            local.wait()
            for copy in out:
                copy.wait_send()
                copy.wait_recv()
            add_up([own] + [planes.at[k] for k in range(shards - 1)], level, 16)

        return [start, idle, end]
    fast, slow, across = neighbours(me)
    to_fast, to_slow = device(fast, group, core), device(slow, group, core)
    half = rows // 2
    planes, met_fast, met_slow, held_fast, held_slow = bufs[1:]
    upper, lower = pl.ds(0, half), pl.ds(half, half)
    loads = [
        local,
        pltpu.make_async_copy(block(fast, half, half), held_fast, load.at[1]),
        pltpu.make_async_copy(block(slow, 0, half), held_slow, load.at[2]),
    ]
    early = [
        copies(block(across, 0, half), met_fast, to_fast),
        copies(block(across, half, half), met_slow, to_slow),
        copies(block(fast, 0, half), planes.at[0, upper, :], to_fast),
        copies(block(slow, half, half), planes.at[1, lower, :], to_slow),
    ]
    late = [
        copies(held_fast, planes.at[0, lower, :], to_fast),
        copies(held_slow, planes.at[1, upper, :], to_slow),
    ]

    def start():
        for copy in early + loads:
            copy.start()

    def merge():
        for copy in loads:
            copy.wait()
        for copy, met, held, out in (
            (early[1], met_slow, held_fast, late[0]),
            (early[0], met_fast, held_slow, late[1]),
        ):
            copy.wait_recv()
            add_up([held, met], held, 16)
            out.start()

    def end():
        for copy in early[2:] + late:
            copy.wait_recv()
        for copy in early + late:
            copy.wait_send()
        add_up([own, planes.at[0], planes.at[1]], level, 16)

    return [start, merge, end]


def plane_buffers(shards, shape):
    half = (shape[0] // 2, shape[1])
    if shards != 4:
        return [pltpu.VMEM(shape, LOW), pltpu.VMEM((shards - 1,) + shape, LOW)]
    return [pltpu.VMEM(shape, LOW), pltpu.VMEM((2,) + shape, LOW)] + [pltpu.VMEM(half, LOW)] * 4


def reduce_over_line(copies, groups, source, part, total, bufs):
    me, group, core = place()
    if groups != 4:
        (slots,) = bufs
        out = [
            copies(source, slots.at[group], device(me, lax.rem(group + k, groups), core))
            for k in range(1, groups)
        ]

        def start():
            for copy in out:
                copy.start()

        def end():
            rows = part.shape[0]

            def some(i, _):
                here = pl.ds(pl.multiple_of(i * 8, 8), 8)
                slots[group, here, :] = part[here, :]
                return 0

            lax.fori_loop(0, rows // 8, some, 0)
            for copy in out:
                copy.wait_send()
                copy.wait_recv()
            add_up([slots.at[k] for k in range(groups)], total, 8)

        return [start, idle, idle, end]
    met, summed, other = bufs
    outer = jnp.logical_or(group == 0, group == groups - 1)
    inner = jnp.logical_not(outer)
    mate = device(me, group + 1 - 2 * lax.rem(group, 2), core)
    inward = copies(source, met, mate)
    between = copies(summed, other, device(me, groups - 1 - group, core))
    back = copies(total, total, mate)

    def start():
        pl.when(outer)(inward.start)

    def exchange():
        @pl.when(inner)
        def _():
            inward.wait_recv()
            add_up([part, met], summed, 16)
            between.start()

    def give():
        @pl.when(inner)
        def _():
            between.wait_recv()
            add_up([summed, other], total, 16)
            back.start()

    def end():
        @pl.when(outer)
        def _():
            inward.wait_send()
            back.wait_recv()

        @pl.when(inner)
        def _():
            between.wait_send()
            back.wait_send()

    return [start, exchange, give, end]


def idle():
    pass


def line_buffers(groups, shape):
    if groups != 4:
        return [pltpu.VMEM((groups,) + shape, LOW)]
    return [pltpu.VMEM(shape, LOW)] * 3


PARTS = 4


class LineSum:
    def __init__(self, copies, groups, source, part, total, bufs):
        rows = part.shape[0] // PARTS
        each = len(bufs) // PARTS
        self.parts = [
            reduce_over_line(
                copies,
                groups,
                at_rows(source, i * rows, rows),
                at_rows(part, i * rows, rows),
                at_rows(total, i * rows, rows),
                bufs[i * each : (i + 1) * each],
            )
            for i in range(PARTS)
        ]

    def run(self, part, stage):
        self.parts[part][stage]()

    @staticmethod
    def buffers(groups, shape):
        return line_buffers(groups, (shape[0] // PARTS, shape[1])) * PARTS

    @staticmethod
    def copies(groups):
        return PARTS * max(3, groups - 1)


class Side:
    def __init__(self, shards, groups, plane_shapes, line_shapes, extra=0):
        self.shards, self.groups, self.extra = shards, groups, extra
        self.plane_shapes, self.line_shapes = plane_shapes, line_shapes

    def outs(self):
        return [jax.ShapeDtypeStruct(shape, LOW) for shape in self.plane_shapes + self.line_shapes]

    def scratch(self):
        groups, shards = self.groups, self.shards
        shapes = [pltpu.VMEM(shape, LOW) for shape in self.plane_shapes + self.line_shapes]
        for shape in self.plane_shapes:
            shapes += plane_buffers(shards, shape)
        for shape in self.line_shapes:
            shapes += [pltpu.VMEM(shape, LOW)] + LineSum.buffers(groups, shape)
        count = 2 * self.shards + len(self.plane_shapes) * max(6, shards - 1)
        count += len(self.line_shapes) * LineSum.copies(groups) + self.extra
        loads = 4 * len(self.plane_shapes) + 2 * len(self.line_shapes) + 1
        return shapes + [pltpu.SemaphoreType.DMA((count,))] * 2 + [pltpu.SemaphoreType.DMA((loads,))]

    def run(self, step, sources, outs, bufs):
        *bufs, send, recv, load = bufs
        totals, bufs = take(bufs, len(outs))
        me, group, core = place()
        copies = Copies(send, recv)
        shards, groups = self.shards, self.groups

        @pl.when(step == 0)
        def _():
            meet(everyone_near(shards, groups))

        planes, lines, loads = [], [], []
        for i, shape in enumerate(self.plane_shapes):
            some, bufs = take(bufs, len(plane_buffers(shards, shape)))
            planes.append(
                reduce_over_plane(
                    copies, load.at[pl.ds(3 * i, 3)], shards, sources[i], totals[i], some
                )
            )
        first = len(self.plane_shapes)
        for i, shape in enumerate(self.line_shapes):
            (own,), bufs = take(bufs, 1)
            some, bufs = take(bufs, len(LineSum.buffers(groups, shape)))
            loads.append(
                pltpu.make_async_copy(sources[first + i], own, load.at[3 * first + i])
            )
            lines.append(LineSum(copies, groups, sources[first + i], own, totals[first + i], some))

        def begin():
            for stages in planes:
                stages[0]()
            for part in range(PARTS):
                for line in lines:
                    line.run(part, 0)
            for one in loads:
                one.start()

        def load_done():
            for one in loads:
                one.wait()

        def of_lines(part, stage):
            def go():
                for line in lines:
                    line.run(part, stage)

            return go

        def merge():
            for stages in planes:
                stages[1]()

        plan = {
            0: [begin],
            2: [load_done, of_lines(0, 1)],
            3: [of_lines(1, 1), merge],
            4: [of_lines(2, 1), of_lines(0, 2)],
            5: [of_lines(3, 1), of_lines(1, 2)],
            6: [of_lines(2, 2)],
            7: [of_lines(3, 2)],
        }
        for when, stages in plan.items():

            @pl.when(step == when)
            def _(stages=stages):
                for stage in stages:
                    stage()

        count = len(outs)
        stores = [
            pltpu.make_async_copy(total, out, load.at[load.shape[0] - 1 - count + i])
            for i, (total, out) in enumerate(zip(totals, outs))
        ]

        def end():
            for stages, store in zip(planes, stores):
                stages[2]()
                store.start()
            for part in range(PARTS):
                for line in lines:
                    line.run(part, 3)
            for store in stores[len(planes) :]:
                store.start()
            for store in stores:
                store.wait()

        return copies, end


def everyone_near(shards, groups):
    me, group, core = place()
    return (
        [device(lax.rem(me + k, shards), group, core) for k in range(1, shards)]
        + [device(me, lax.rem(group + k, groups), core) for k in range(1, groups)]
        + [device(me, group, 1 - core)]
    )


def take(refs, count):
    return refs[:count], refs[count:]


def finish_kernel(shards, groups, counts, rows, length_ref, *refs):
    smalls, refs = take(refs, 1 + max(k for k, _ in rows))
    (grad_ref,), refs = take(refs, 1)
    lows, refs = take(refs, counts[0])
    ready, refs = take(refs, counts[1])
    n = counts[0] + 1
    mine, refs = take(refs, n)
    other, refs = take(refs, n + counts[1])
    (total_ref, level), refs = take(refs, 2)
    plane_bufs, refs = take(refs, len(plane_buffers(shards, (16, LANES))))
    own, refs = take(refs, counts[0])
    per_line = len(LineSum.buffers(groups, (32, LANES)))
    line_bufs = []
    for _ in range(n):
        some, refs = take(refs, per_line)
        line_bufs.append(some)
    small_a, small_b, small_c, send, recv, load = refs
    me, group, core = place()
    partner = device(me, group, 1 - core)
    plane = [device(lax.rem(me + k, shards), group, core) for k in range(1, shards)]
    line = [device(me, lax.rem(group + k, groups), core) for k in range(1, groups)]
    copies = Copies(send, recv)

    def go(source, target, where):
        copy = copies(source, target, where)
        copy.start()
        return copy

    def finish(some):
        for copy in some:
            copy.wait_send()
            copy.wait_recv()

    loads = [pltpu.make_async_copy(low, own[i], load.at[3 + i]) for i, low in enumerate(lows)]
    for copy in loads:
        copy.start()
    for i, (k, row) in enumerate(rows):
        values = smalls[k][row : row + 1, :]
        small_a[me, i : i + 1, : values.shape[1]] = values
        if values.shape[1] < small_a.shape[2]:
            rest = small_a.shape[2] - values.shape[1]
            small_a[me, i : i + 1, values.shape[1] :] = jnp.zeros((1, rest), F32)
    small_a[me, len(rows) :, :] = jnp.full(
        (small_a.shape[1] - len(rows), small_a.shape[2]), length_ref[0].astype(F32)
    )
    meet(everyone_near(shards, groups))
    stages = reduce_over_plane(copies, load.at[pl.ds(0, 3)], shards, grad_ref, level, plane_bufs)
    sums = [
        LineSum(copies, groups, low, own[i], mine[i], line_bufs[i]) for i, low in enumerate(lows)
    ]
    last = LineSum(copies, groups, level, level, mine[-1], line_bufs[-1])
    stages[0]()
    for part in range(PARTS):
        for one in sums:
            one.run(part, 0)
    swaps = [go(source, target, partner) for source, target in zip(ready, other[n:])]
    small_copies = [go(small_a.at[me], small_a.at[me], where) for where in plane]
    for copy in loads:
        copy.wait()
    finish(small_copies)
    small_b[group] = sum(small_a[k] for k in range(shards))
    small_copies = [go(small_b.at[group], small_b.at[group], where) for where in line]
    for part in range(2):
        for one in sums:
            one.run(part, 1)
    stages[1]()
    for part in range(2):
        for one in sums:
            one.run(part + 2, 1)
            one.run(part, 2)
    finish(small_copies)
    small_c[core] = sum(small_b[k] for k in range(groups))
    small_copies = [go(small_c.at[core], small_c.at[core], partner)]
    stages[2]()
    for part in range(PARTS):
        last.run(part, 0)
    for part in range(2, PARTS):
        for one in sums:
            one.run(part, 2)
        last.run(part - 2, 1)
    last.run(2, 1)
    last.run(0, 2)
    for part in range(PARTS):
        for one in sums:
            one.run(part, 3)
    swaps += [go(mine[i], other[i], partner) for i in range(counts[0])]
    last.run(3, 1)
    for part in range(1, PARTS):
        last.run(part, 2)
    for part in range(PARTS):
        last.run(part, 3)
    swaps.append(go(mine[-1], other[n - 1], partner))
    finish(small_copies)
    total_ref[...] = small_c[0] + small_c[1]
    finish(swaps)


def finish_sums(grad, length, smalls, rows, lows, ready, shards, groups):
    level = (grad.shape[0] // shards, grad.shape[1])
    shapes = [low.shape for low in lows] + [level]
    others = shapes + [one.shape for one in ready]
    vmem = pl.BlockSpec(memory_space=pltpu.VMEM)
    hbm = pl.BlockSpec(memory_space=pltpu.HBM)
    scratch = [pltpu.VMEM(level, LOW)] + plane_buffers(shards, level)
    scratch += [pltpu.VMEM(shape, LOW) for shape in shapes[:-1]]
    for shape in shapes:
        scratch += LineSum.buffers(groups, shape)
    count = 6 + 2 * shards + len(shapes) * LineSum.copies(groups) + len(others) + groups
    small = (8, max(one.shape[1] for one in smalls))
    outs = pl.pallas_call(
        partial(finish_kernel, shards, groups, (len(lows), len(ready)), rows),
        out_shape=[jax.ShapeDtypeStruct(shape, LOW) for shape in shapes + others]
        + [jax.ShapeDtypeStruct(small, F32)],
        in_specs=[pl.BlockSpec(memory_space=pltpu.SMEM)]
        + [vmem] * len(smalls)
        + [hbm] * (1 + len(lows) + len(ready)),
        out_specs=[vmem] * (len(shapes) + len(shapes)) + [hbm] * len(ready) + [vmem],
        scratch_shapes=scratch
        + [pltpu.VMEM((count,) + small, F32) for count in (shards, groups, 2)]
        + [pltpu.SemaphoreType.DMA((count,)), pltpu.SemaphoreType.DMA((count,))]
        + [pltpu.SemaphoreType.DMA((3 + len(lows),))],
        compiler_params=pltpu.CompilerParams(
            collective_id=1, has_side_effects=True, vmem_limit_bytes=56 << 20
        ),
        name="finish",
    )(length, *smalls, grad, *lows, *ready)
    n = len(shapes)
    return outs[:n], outs[n:-1], outs[-1]


def two_parts(column):
    high = column.astype(LOW)
    return high, (column - high.astype(F32)).astype(LOW)


def attend_kernel(block, width, lens_ref, q_ref, k_ref, v_ref, att_ref, qx_ref):
    rows = q_ref.shape[0]
    heads = q_ref.shape[1] // LANES
    length = lens_ref[pl.program_id(0)]
    lane = lax.broadcasted_iota(jnp.int32, (block, LANES), 1)
    keep = lax.broadcasted_iota(jnp.int32, (block, block), 1) <= lax.broadcasted_iota(
        jnp.int32, (block, block), 0
    )
    for step in range(rows // block):
        start = step * block
        here = pl.ds(start, block)

        @pl.when(start < length)
        def _():
            outs = []
            for head in range(heads):
                lanes = pl.ds(head * LANES, LANES)
                query = q_ref[here, lanes]
                probs = jnp.exp(nt(query, k_ref[here, :]))
                probs = jnp.where(keep, probs, 0.0).astype(LOW)
                total = nn(probs, v_ref[here, :])
                if step:
                    probs = jnp.exp(nt(query, k_ref[pl.ds(0, start), :])).astype(LOW)
                    total += nn(probs, v_ref[pl.ds(0, start), :])
                weight = total[:, width : width + 1]
                outs.append(total / weight)
                high, rest = two_parts(-jnp.log(weight))
                qx_ref[here, lanes] = jnp.where(
                    lane == width, high, jnp.where(lane == width + 1, rest, query)
                )
            for pair in range(heads // 2):
                att_ref[here, pl.ds(pair * LANES, LANES)] = jnp.where(
                    lane < width, outs[2 * pair], pltpu.roll(outs[2 * pair + 1], width, 1)
                ).astype(LOW)

        @pl.when(start >= length)
        def _():
            att_ref[here, :] = jnp.zeros((block, att_ref.shape[1]), LOW)
            qx_ref[here, :] = jnp.zeros((block, qx_ref.shape[1]), LOW)


def attend_back_kernel(block, width, side, q_ref, k_ref, v_ref, do_ref, *refs):
    count = len(side.plane_shapes) + len(side.line_shapes)
    sources, refs = take(refs, count)
    (dq_ref, dk_ref, dv_ref), refs = take(refs, 3)
    totals, bufs = take(refs, count)
    grid_step = pl.program_id(0) * pl.num_programs(1) + pl.program_id(1)
    _, end = side.run(grid_step, sources, totals, bufs)
    rows = q_ref.shape[0]
    heads = q_ref.shape[1] // LANES
    lane = lax.broadcasted_iota(jnp.int32, (block, LANES), 1)
    keep = lax.broadcasted_iota(jnp.int32, (block, block), 0) <= lax.broadcasted_iota(
        jnp.int32, (block, block), 1
    )
    dk_ref[...] = jnp.zeros(dk_ref.shape, F32)
    dv_ref[...] = jnp.zeros(dv_ref.shape, F32)
    for step in range(rows // block):
        start = step * block
        here = pl.ds(start, block)
        parts = []
        for head in range(heads):
            lanes = pl.ds(head * LANES, LANES)
            query = q_ref[here, lanes]
            dout = do_ref[here, lanes]

            def one(keys, masked):
                key, value = k_ref[keys, :], v_ref[keys, :]
                probs = jnp.exp(nt(key, query))
                if masked:
                    probs = jnp.where(keep, probs, 0.0)
                dscores = (probs * nt(value, dout)).astype(LOW)
                dv_ref[keys, :] += nn(probs.astype(LOW), dout)
                dk_ref[keys, :] += nn(dscores, query)
                return tn(dscores, key)

            dquery = one(here, True)
            if step:
                dquery += one(pl.ds(0, start), False)
            parts.append(dquery)
        for pair in range(heads // 2):
            dq_ref[here, pl.ds(pair * LANES, LANES)] = jnp.where(
                lane < width, parts[2 * pair], pltpu.roll(parts[2 * pair + 1], width, 1)
            )
    pl.when(grid_step == pl.num_programs(0) * pl.num_programs(1) - 1)(end)


def attention_grid(slots, groups, per_group, rows):
    wide = pl.BlockSpec((rows, per_group * LANES), lambda s, g, lens: (s, g))
    dense = pl.BlockSpec((rows, per_group * LANES // 2), lambda s, g, lens: (s, g))
    narrow = pl.BlockSpec((rows, LANES), lambda s, g, lens: (s, g))
    return (slots, groups), wide, dense, narrow


def attend(lens, queries, keys, values, rows, width, block):
    slots, groups = queries.shape[0] // rows, keys.shape[1] // LANES
    per_group = queries.shape[1] // LANES // groups
    grid, wide, dense, narrow = attention_grid(slots, groups, per_group, rows)
    flops = 4 * slots * groups * per_group * rows * rows * LANES
    return pl.pallas_call(
        partial(attend_kernel, block, width),
        out_shape=(
            jax.ShapeDtypeStruct((queries.shape[0], queries.shape[1] // 2), LOW),
            jax.ShapeDtypeStruct(queries.shape, LOW),
        ),
        grid_spec=pltpu.PrefetchScalarGridSpec(
            num_scalar_prefetch=1,
            grid=grid,
            in_specs=[wide, narrow, narrow],
            out_specs=[dense, wide],
        ),
        cost_estimate=pl.CostEstimate(flops=flops, bytes_accessed=1 << 23, transcendentals=0),
        name="attend",
    )(lens, queries, keys, values)


def attend_back(queries, keys, values, douts, rows, width, block, side, sources):
    slots, groups = queries.shape[0] // rows, keys.shape[1] // LANES
    per_group = queries.shape[1] // LANES // groups
    wide = pl.BlockSpec((rows, per_group * LANES), lambda s, g: (s, g))
    dense = pl.BlockSpec((rows, per_group * LANES // 2), lambda s, g: (s, g))
    narrow = pl.BlockSpec((rows, LANES), lambda s, g: (s, g))
    flops = 10 * slots * groups * per_group * rows * rows * LANES
    return pl.pallas_call(
        partial(attend_back_kernel, block, width, side),
        out_shape=[
            jax.ShapeDtypeStruct((queries.shape[0], queries.shape[1] // 2), F32),
            jax.ShapeDtypeStruct(keys.shape, F32),
            jax.ShapeDtypeStruct(keys.shape, F32),
        ]
        + side.outs(),
        grid=(slots, groups),
        in_specs=[wide, narrow, narrow, wide]
        + [pl.BlockSpec(memory_space=pltpu.HBM)] * len(sources),
        out_specs=[dense, narrow, narrow]
        + [pl.BlockSpec(memory_space=pltpu.HBM)] * len(side.outs()),
        scratch_shapes=side.scratch(),
        cost_estimate=pl.CostEstimate(flops=flops, bytes_accessed=1 << 24, transcendentals=0),
        compiler_params=pltpu.CompilerParams(
            collective_id=5, has_side_effects=True, vmem_limit_bytes=56 << 20
        ),
        name="attend_back",
    )(queries, keys, values, douts, *sources)


def swap_halves(values, width):
    lane = lax.broadcasted_iota(jnp.int32, values.shape, 1)
    half = width // 2
    return jnp.where(
        lane % width < half, pltpu.roll(values, LANES - half, 1), pltpu.roll(values, half, 1)
    )


def head_sum(values, width):
    same = lax.broadcasted_iota(jnp.int32, (LANES, LANES), 0) // width
    same = (same == lax.broadcasted_iota(jnp.int32, (LANES, LANES), 1) // width).astype(LOW)
    high, rest = two_parts(values)
    return nn(high, same) + nn(rest, same)


def row_rsqrt(values):
    return lax.rsqrt(jnp.mean(values * values, axis=1, keepdims=True) + EPS)


def is_live(lens_ref, step, per_slot, block):
    return lax.rem(step, per_slot) * block < lens_ref[lax.div(step, per_slot)]


def qkv_kernel(
    per_slot, counts, width, scale, lens_ref, own_ref, other_ref, w_ref, ga_ref, gh_ref, cos_ref, sin_ref,
    normed_ref, raw_ref, q_ref, k_ref, v_ref,
):
    step = pl.program_id(0)
    block = own_ref.shape[0]
    q_tiles, kv_tiles = counts

    @pl.when(is_live(lens_ref, step, per_slot, block))
    def _():
        x = jnp.where(step < per_slot, own_ref[...], other_ref[...]).astype(F32)
        normed = (x * row_rsqrt(x) * ga_ref[...]).astype(LOW)
        normed_ref[...] = normed
        lane = lax.broadcasted_iota(jnp.int32, (block, LANES), 1)
        zero = jnp.zeros((block, LANES), F32)
        ones = jnp.where(lane < width + 2, 1.0, 0.0)
        cosine, sine = cos_ref[...], sin_ref[...]

        def put(ref, tile, values, rest):
            ref[:, pl.ds(2 * tile * LANES, LANES)] = jnp.where(lane < width, values, rest).astype(LOW)
            ref[:, pl.ds((2 * tile + 1) * LANES, LANES)] = jnp.where(
                lane < width, pltpu.roll(values, width, 1), rest
            ).astype(LOW)

        for tile in range(q_tiles + 2 * kv_tiles):
            lanes = pl.ds(tile * LANES, LANES)
            if tile % 2 == 0:
                pair = nn(normed, w_ref[:, pl.ds(tile * LANES, 2 * LANES)])
            values = pair[:, (tile % 2) * LANES : (tile % 2 + 1) * LANES]
            if tile >= q_tiles + kv_tiles:
                put(v_ref, tile - q_tiles - kv_tiles, values, ones)
                continue
            raw_ref[:, lanes] = values
            is_query = tile < q_tiles
            gain = gh_ref[0:1, :] if is_query else gh_ref[1:2, :]
            values *= lax.rsqrt(head_sum(values * values, width) * (1.0 / width) + EPS) * gain
            values = values * cosine + swap_halves(values, width) * sine
            if is_query:
                put(q_ref, tile, values * scale, zero)
            else:
                put(k_ref, tile - q_tiles, values, ones)

    @pl.when(jnp.logical_not(is_live(lens_ref, step, per_slot, block)))
    def _():
        for ref in (normed_ref, raw_ref, q_ref, k_ref, v_ref):
            ref[...] = jnp.zeros(ref.shape, ref.dtype)


def out_kernel(per_slot, lens_ref, att_ref, w_ref, own_ref, other_ref):
    step = pl.program_id(0)
    block = att_ref.shape[0]

    @pl.when(step < per_slot)
    def _():
        other_ref[...] = nn(att_ref[...], w_ref[...]).astype(LOW)

    @pl.when(step >= per_slot)
    def _():
        own_ref[...] = nn(att_ref[...], w_ref[...])


def resid_kernel(lens_ref, x_ref, part_ref, got_ref, gain_ref, resid_ref, normed_ref, sums_ref):
    step = pl.program_id(0)
    block = x_ref.shape[0]
    valid = lax.broadcasted_iota(jnp.int32, (block, 1), 0) + step * block < lens_ref[0]
    attn_out = part_ref[...] + got_ref[...].astype(F32)
    resid = x_ref[...].astype(F32) + attn_out
    resid_ref[...] = resid
    normed_ref[...] = (resid * row_rsqrt(resid) * gain_ref[...]).astype(LOW)

    @pl.when(step == 0)
    def _():
        sums_ref[...] = jnp.zeros(sums_ref.shape, F32)

    for row, values in ((0, resid), (1, attn_out)):
        sums_ref[row : row + 1, :] += jnp.sum(
            jnp.where(valid, values * values, 0.0), axis=0, keepdims=True
        )


def ffn_kernel(
    per_slot, shards, chained, last, side, offset, x_own, x_other, g_own, g_other, gathered_ref, *refs
):
    if chained:
        (mlp_in, db_in), refs = take(refs, 2)
    count = len(side.plane_shapes) + len(side.line_shapes)
    sources, refs = take(refs, count)
    (mlp_own, db_own), refs = take(refs, 2)
    if last:
        (mlp_other, db_other), refs = take(refs, 2)
    (grad_out,), refs = take(refs, 1)
    totals, refs = take(refs, count)
    (acc_ref, accd_ref, given_ref, w_ref, wd_ref, grad_ref, load), bufs = take(refs, 7)
    step = pl.program_id(0)
    copies, end = side.run(step, sources, totals, bufs)
    own = step < per_slot
    units, depth = wd_ref.shape
    me, group, core = place()
    partner = device(me, group, 1 - core)
    half, columns, d_rows = shards // 2, depth // 2, depth // shards
    packed = grad_ref.shape[0] // shards
    size = packed - d_rows
    folds = grad_ref.shape[1] // columns

    def folded(ref, shard, fold):
        return ref.at[shard, pl.ds(offset + d_rows, size), pl.ds(fold * columns, columns)]

    def unfolded(i, fold):
        return at(wd_ref, (i * folds + fold) * size, size, core * columns, columns)

    tiles = [(i, fold) for i in range(half) for fold in range(folds)]
    given = [
        copies(folded(gathered_ref, (1 - core) * half + i, fold), unfolded(i, fold), partner)
        for i, fold in tiles
    ]
    loads = [
        pltpu.make_async_copy(
            gathered_ref.at[shard, pl.ds(offset, d_rows), :],
            w_ref.at[pl.ds(shard * d_rows, d_rows), :],
            load.at[shard],
        )
        for shard in range(shards)
    ] + [
        pltpu.make_async_copy(
            folded(gathered_ref, core * half + i, fold), unfolded(i, fold), load.at[shards + k]
        )
        for k, (i, fold) in enumerate(tiles)
    ]

    @pl.when(step == 0)
    def _():
        for copy in given + loads:
            copy.start()
        acc_ref[...] = jnp.zeros(acc_ref.shape, F32)
        accd_ref[...] = jnp.zeros(accd_ref.shape, F32)
        for copy in loads:
            copy.wait()
        for copy in given:
            copy.wait_send()
            copy.wait_recv()

    x = jnp.where(own, x_own[...], x_other[...])
    g = jnp.where(own, g_own[...], g_other[...])
    gate = nn(x, w_ref[:, :units])
    up = nn(x, w_ref[:, units:])
    d_hidden = nt(g, wd_ref[...])
    sig = jax.nn.sigmoid(gate)
    silu = gate * sig
    hidden = (silu * up).astype(LOW)
    d_gate = (d_hidden * up * (sig * (1.0 + gate * (1.0 - sig)))).astype(LOW)
    d_up = (d_hidden * silu).astype(LOW)
    mlp = nn(hidden, wd_ref[...])
    d_b = nt(d_gate, w_ref[:, :units]) + nt(d_up, w_ref[:, units:])
    if chained:
        mlp += mlp_in[...]
        d_b += db_in[...]
    if last:

        @pl.when(own)
        def _():
            mlp_own[...] = mlp
            db_own[...] = d_b

        @pl.when(jnp.logical_not(own))
        def _():
            mlp_other[...] = mlp.astype(LOW)
            db_other[...] = d_b.astype(LOW)

    else:
        mlp_own[...] = mlp
        db_own[...] = d_b
    acc_ref[:, :units] += tn(x, d_gate)
    acc_ref[:, units:] += tn(x, d_up)
    accd_ref[...] += tn(hidden, g)

    @pl.when(step == pl.num_programs(0) - 1)
    def _():
        mine = pl.ds(pl.multiple_of(core * columns, columns), columns)
        theirs = pl.ds(pl.multiple_of((1 - core) * columns, columns), columns)
        given_ref[...] = accd_ref[:, theirs].astype(LOW)
        for shard in range(shards):
            grad_ref[pl.ds(shard * packed, d_rows), :] = acc_ref[
                pl.ds(shard * d_rows, d_rows), :
            ].astype(LOW)
        out = []
        for i in range(half):
            for fold in range(folds):
                row = i * folds * size + fold * size
                to = pl.ds(
                    pl.multiple_of((core * half + i) * packed + d_rows, 8), size
                )
                lanes = pl.ds(fold * columns, columns)
                out.append(
                    copies(
                        given_ref.at[pl.ds(row, size), :],
                        grad_ref.at[to, lanes],
                        partner,
                    )
                )
                out[-1].start()
                grad_ref[to, lanes] = accd_ref[pl.ds(row, size), mine].astype(LOW)
        for copy in out:
            copy.wait_send()
            copy.wait_recv()
        store = pltpu.make_async_copy(grad_ref, grad_out, load.at[0])
        store.start()
        end()
        store.wait()


def norm_back(values, dy, gain):
    inverse = row_rsqrt(values)
    scaled = dy * gain
    inner = jnp.mean(values * scaled, axis=1, keepdims=True)
    return inverse * scaled - values * (inverse * inverse * inverse * inner), dy * values * inverse


def resid_back_kernel(
    lens_ref, resid_ref, mlp_ref, mlp_got, db_ref, db_got, g_ref, gain_ref,
    out_ref, dresid_ref, dattn_ref, sums_ref,
):
    step = pl.program_id(0)
    block = resid_ref.shape[0]
    valid = lax.broadcasted_iota(jnp.int32, (block, 1), 0) + step * block < lens_ref[0]
    resid = resid_ref[...]
    mlp_out = mlp_ref[...] + mlp_got[...].astype(F32)
    out_ref[...] = jnp.where(valid, resid + mlp_out, 0.0).astype(LOW)
    d_norm, d_gain = norm_back(resid, db_ref[...] + db_got[...].astype(F32), gain_ref[...])
    d_resid = jnp.where(valid, g_ref[...].astype(F32) + d_norm, 0.0)
    dresid_ref[...] = d_resid
    dattn_ref[...] = d_resid.astype(LOW)

    @pl.when(step == 0)
    def _():
        sums_ref[...] = jnp.zeros(sums_ref.shape, F32)

    for row, values in ((0, mlp_out * mlp_out), (1, d_gain)):
        sums_ref[row : row + 1, :] += jnp.sum(
            jnp.where(valid, values, 0.0), axis=0, keepdims=True
        )


def dout_kernel(
    per_slot, width, lens_ref, own_ref, other_ref, att_ref, w_ref, do_ref, grad_ref, acc_ref
):
    step = pl.program_id(0)
    block = own_ref.shape[0]

    @pl.when(step == 0)
    def _():
        acc_ref[...] = jnp.zeros(acc_ref.shape, F32)

    @pl.when(is_live(lens_ref, step, per_slot, block))
    def _():
        d_attn = jnp.where(step < per_slot, own_ref[...], other_ref[...])
        lane = lax.broadcasted_iota(jnp.int32, (block, LANES), 1)
        att = att_ref[...]
        acc_ref[...] += tn(att, d_attn)
        for tile in range(att.shape[1] // LANES):
            lanes = slice(tile * LANES, (tile + 1) * LANES)
            if tile % 2 == 0:
                pair = nt(d_attn, w_ref[tile * LANES : (tile + 2) * LANES, :])
            dout = pair[:, (tile % 2) * LANES : (tile % 2 + 1) * LANES].astype(LOW).astype(F32)
            delta = -head_sum(dout * att[:, lanes].astype(F32), width)
            for head, (values, column) in enumerate(
                ((dout, pltpu.roll(delta, width, 1)), (pltpu.roll(dout, width, 1), delta))
            ):
                high, rest = two_parts(column)
                column = jnp.where(
                    lane == width, high, jnp.where(lane == width + 1, rest, jnp.zeros_like(rest))
                )
                do_ref[:, pl.ds((2 * tile + head) * LANES, LANES)] = jnp.where(
                    lane < width, values.astype(LOW), column
                )

    @pl.when(jnp.logical_not(is_live(lens_ref, step, per_slot, block)))
    def _():
        do_ref[...] = jnp.zeros(do_ref.shape, LOW)

    @pl.when(step == pl.num_programs(0) - 1)
    def _():
        grad_ref[...] = acc_ref[...].astype(LOW)


def qkv_back_kernel(
    per_slot, counts, width, scale, lens_ref, dq_ref, dk_ref, dv_ref, raw_ref, normed_ref, w_ref, gh_ref,
    cos_ref, sin_ref, own_ref, other_ref, grad_ref, gain_ref, acc_ref, low_ref,
):
    step = pl.program_id(0)
    block = dq_ref.shape[0]
    q_tiles, kv_tiles = counts
    slot_step = lax.rem(step + per_slot, 2 * per_slot)

    @pl.when(step == 0)
    def _():
        acc_ref[...] = jnp.zeros(acc_ref.shape, F32)
        gain_ref[...] = jnp.zeros(gain_ref.shape, F32)

    live = is_live(lens_ref, slot_step, per_slot, block)

    def put(d_a):
        @pl.when(step < per_slot)
        def _():
            other_ref[...] = d_a.astype(LOW)

        @pl.when(step >= per_slot)
        def _():
            own_ref[...] = d_a

    @pl.when(live)
    def _():
        lane = lax.broadcasted_iota(jnp.int32, (block, LANES), 1)
        cosine, sine = cos_ref[...], sin_ref[...]

        def pair(ref, tile):
            return jnp.where(
                lane < width,
                ref[:, pl.ds(2 * tile * LANES, LANES)],
                pltpu.roll(ref[:, pl.ds((2 * tile + 1) * LANES, LANES)], width, 1),
            )

        for tile in range(q_tiles + 2 * kv_tiles):
            lanes = pl.ds(tile * LANES, LANES)
            if tile >= q_tiles + kv_tiles:
                low_ref[:, lanes] = pair(dv_ref, tile - q_tiles - kv_tiles).astype(LOW)
                continue
            is_query = tile < q_tiles
            if is_query:
                turned, row = dq_ref[:, lanes] * scale, 0
            else:
                turned, row = pair(dk_ref, tile - q_tiles), 1
            gain = gh_ref[row : row + 1, :]
            dy = turned * cosine + swap_halves(turned * sine, width)
            values = raw_ref[:, lanes]
            inverse = lax.rsqrt(head_sum(values * values, width) * (1.0 / width) + EPS)
            scaled = dy * gain
            inner = head_sum(values * scaled, width) * (1.0 / width)
            low_ref[:, lanes] = (
                inverse * scaled - values * (inverse * inverse * inverse * inner)
            ).astype(LOW)
            gain_ref[row : row + 1, :] += jnp.sum(dy * values * inverse, axis=0, keepdims=True)
        low = low_ref[...]
        acc_ref[...] += tn(normed_ref[...], low)
        put(nt(low, w_ref[...]))

    @pl.when(jnp.logical_not(live))
    def _():
        put(jnp.zeros(own_ref.shape, F32))

    @pl.when(step == pl.num_programs(0) - 1)
    def _():
        grad_ref[...] = acc_ref[...].astype(LOW)


def input_back_kernel(lens_ref, x_ref, part_ref, got_ref, dresid_ref, gain_ref, out_ref, sums_ref):
    step = pl.program_id(0)
    d_norm, d_gain = norm_back(
        x_ref[...].astype(F32), part_ref[...] + got_ref[...].astype(F32), gain_ref[...]
    )
    out_ref[...] = (dresid_ref[...] + d_norm).astype(LOW)

    @pl.when(step == 0)
    def _():
        sums_ref[...] = jnp.zeros(sums_ref.shape, F32)

    sums_ref[0:1, :] += jnp.sum(d_gain, axis=0, keepdims=True)


def assemble_kernel(chunks, half, folds, widths, *refs):
    parts, refs = take(refs, 4 * chunks)
    pairs, (gate_ref, up_ref, down_ref, *outs) = take(refs, 4)
    first = lax.rem(lax.axis_index("rep"), 2) == 0

    def sides(mine, other):
        return [jnp.where(first, mine, other), jnp.where(first, other, mine)]

    units = parts[0].shape[1] // 2
    piece = units // half
    for chunk in range(chunks):
        top, low, other_top, other_low = parts[4 * chunk : 4 * chunk + 4]
        for side, values in enumerate(sides(top[...], other_top[...])):
            for j, ref in enumerate((gate_ref, up_ref)):
                for i in range(half):
                    to = ((side * half + i) * chunks + chunk) * piece
                    start = j * units + i * piece
                    ref[:, to : to + piece] = values[:, start : start + piece].astype(F32)
        columns = down_ref.shape[2] // 2
        for side, values in enumerate(sides(low[...], other_low[...])):
            for fold in range(folds):
                down_ref[chunk * folds + fold, :, side * columns : (side + 1) * columns] = values[
                    :, fold * columns : (fold + 1) * columns
                ].astype(F32)
    columns = [pairs[0].shape[1], widths[0], widths[1], widths[1]]
    starts = [0, 0, widths[0], widths[0] + widths[1]]
    for ref, width, start, k in zip(outs, columns, starts, (0, 2, 2, 2)):
        mine, other = (one[:, start : start + width] for one in pairs[k : k + 2])
        for side, values in enumerate(sides(mine, other)):
            ref[:, side * width : (side + 1) * width] = values.astype(F32)


class Rows:
    def __init__(self, lens, rows, block):
        self.lens, self.block, self.per_slot = lens, block, rows // block

    def both(self, width):
        return pl.BlockSpec((self.block, width), lambda i, lens: (i, 0))

    def both_other_first(self, width):
        n = self.per_slot
        return pl.BlockSpec((self.block, width), lambda i, lens: (lax.rem(i + n, 2 * n), 0))

    def early(self, width):
        n = self.per_slot
        return pl.BlockSpec((self.block, width), lambda i, lens: (jnp.minimum(i, n - 1), 0))

    def late(self, width):
        n = self.per_slot
        return pl.BlockSpec((self.block, width), lambda i, lens: (jnp.maximum(i - n, 0), 0))

    def repeated(self, width):
        n = self.per_slot
        return pl.BlockSpec((self.block, width), lambda i, lens: (lax.rem(i, n), 0))

    def fixed(self, shape):
        return pl.BlockSpec(shape, lambda i, lens: (0, 0), pipeline_mode=pl.Buffered(1))

    def call(self, name, kernel, slots, in_specs, out_specs, outs, scratch, flops, *args):
        return pl.pallas_call(
            kernel,
            out_shape=[jax.ShapeDtypeStruct(shape, kind) for shape, kind in outs],
            grid_spec=pltpu.PrefetchScalarGridSpec(
                num_scalar_prefetch=1,
                grid=(slots * self.per_slot,),
                in_specs=in_specs,
                out_specs=out_specs,
                scratch_shapes=scratch,
            ),
            cost_estimate=pl.CostEstimate(
                flops=flops, bytes_accessed=1 << 24, transcendentals=0
            ),
            compiler_params=pltpu.CompilerParams(vmem_limit_bytes=60 << 20),
            name=name,
        )(self.lens, *args)


def local(
    inputs,
    lengths,
    gain_attn,
    w_query,
    w_key,
    w_value,
    gain_query,
    gain_key,
    w_out,
    gain_mlp,
    w_gate,
    w_up,
    w_down,
    cotangent,
):
    shards = lax.axis_size("shard")
    core = lax.axis_index("rep") % 2
    first = core == 0
    rows, width_all = inputs.shape[1], inputs.shape[2]
    head_width = gain_query.shape[0] * shards
    q_half, kv_half = w_query.shape[1] // 2, w_key.shape[1] // 2
    d_half = width_all // 2
    d_rows, ff_rows = w_query.shape[0], w_down.shape[0]
    block = min(256, rows)
    scale = 1.0 / math.sqrt(head_width)
    counts = (q_half // LANES, kv_half // LANES)

    def ordered(mine, other, axis):
        return jnp.where(
            first,
            jnp.concatenate([mine, other], axis=axis),
            jnp.concatenate([other, mine], axis=axis),
        )

    half_shards = shards // 2
    groups = lax.axis_size("rep") // 2
    chunks = 3
    piece = ff_rows // chunks
    units = half_shards * piece
    folds = 2 * units // d_half
    head_rows = gain_query.shape[0]

    def fold(part):
        return jnp.concatenate(jnp.split(part, folds, axis=-2), axis=-1)

    def unfold(part):
        return jnp.concatenate(jnp.split(part, folds, axis=-1), axis=-2)

    packed_rows = d_rows + piece // folds
    hbm = pl.BlockSpec(memory_space=pltpu.HBM)
    vmem = pl.BlockSpec(memory_space=pltpu.VMEM)
    chunk_sets = [list(range(chunks - 1)), [chunks - 1]]

    def pack(*refs):
        *refs, pack_a, pack_b, sems = refs
        packs = [
            (ref, [(i * packed_rows, chunk) for i, chunk in enumerate(some)])
            for ref, some in zip((pack_a, pack_b), chunk_sets)
        ]
        pack_kernel(shards, chunks, *refs, *packs, sems)

    if piece % LANES == 0:
        packs = pl.pallas_call(
            pack,
            out_shape=[
                jax.ShapeDtypeStruct((len(some) * packed_rows, 2 * units), LOW) for some in chunk_sets
            ],
            in_specs=[hbm] * 3,
            out_specs=[vmem] * 2,
            scratch_shapes=[pltpu.SemaphoreType.DMA((chunks * (2 * half_shards + folds),))],
            compiler_params=pltpu.CompilerParams(vmem_limit_bytes=32 << 20),
            name="pack",
        )(w_gate, w_up, w_down)
    else:

        def my_half(weight):
            half = weight.shape[1] // 2
            return jnp.where(first, weight[:, :half], weight[:, half:])

        def chunk_of(weight, chunk):
            columns = weight.reshape(d_rows, shards, chunks, piece)[:, :, chunk]
            return my_half(columns.reshape(d_rows, shards * piece))

        def packed_chunk(chunk):
            tall = fold(my_half(w_down)[chunk * piece : (chunk + 1) * piece])
            wide = jnp.concatenate([chunk_of(w_gate, chunk), chunk_of(w_up, chunk)], axis=1)
            return jnp.concatenate([wide, tall])

        packs = [jnp.concatenate([packed_chunk(k) for k in some]) for some in chunk_sets]
    gathered = [lax.all_gather(packs[0], "shard", axis=0)]
    later, _ = lax.optimization_barrier((packs[1], gathered[0]))
    gathered.append(lax.all_gather(later, "shard", axis=0))

    def gain_row(*gains):
        flat = jnp.concatenate(gains)
        return jnp.pad(flat, (0, max(d_rows, LANES) - flat.shape[0]))[None]

    gain_rows = jnp.pad(
        jnp.concatenate(
            [gain_row(gain_attn), gain_row(gain_mlp), gain_row(gain_query, gain_key)]
        ),
        ((0, 13), (0, 0)),
    )

    def half_of(width):
        return lambda core: core * width

    wide_parts = [
        (0, 0, half_of(q_half), 0, q_half),
        (1, 0, half_of(kv_half), q_half, kv_half),
        (2, 0, half_of(kv_half), q_half + kv_half, kv_half),
    ]
    tall_parts = [(3, 1, 0, w_out.shape[0])]
    copies = len(wide_parts) * (shards + 2) + len(tall_parts) * (2 * shards + 3) + shards + 1
    w_qkv, w_o, gains, x_other = pl.pallas_call(
        partial(gather_kernel, shards, wide_parts, tall_parts, (6, copies)),
        out_shape=[
            jax.ShapeDtypeStruct(shape, LOW)
            for shape in (
                (width_all, q_half + 2 * kv_half),
                (half_shards * w_out.shape[0], width_all),
                (shards,) + gain_rows.shape,
                inputs.shape[1:],
            )
        ],
        in_specs=[hbm] * 6,
        out_specs=[hbm] * 4,
        scratch_shapes=[pltpu.SemaphoreType.DMA((copies,)), pltpu.SemaphoreType.DMA((copies,))],
        compiler_params=pltpu.CompilerParams(collective_id=0, has_side_effects=True),
        name="gather",
    )(w_query, w_key, w_value, w_out, gain_rows, inputs[0])
    gain_a = gains[:, 0, :d_rows].reshape(1, -1).astype(F32)
    gain_m = gains[:, 1, :d_rows].reshape(1, -1).astype(F32)
    gain_q = gains[:, 2, :head_rows].reshape(1, -1).astype(F32)
    gain_k = gains[:, 2, head_rows : 2 * head_rows].reshape(1, -1).astype(F32)
    gain_h = jnp.tile(jnp.concatenate([gain_q, gain_k]), (4, LANES // head_width))

    lens = jnp.concatenate([lengths, core_swap(lengths)])
    valid = (jnp.arange(rows) < lengths[0])[:, None]
    x_own = inputs[0]
    g_own = jnp.where(valid, cotangent[0], jnp.zeros((), LOW))
    g_other = core_swap(g_own)
    over = Rows(lens, rows, block)
    cosine, sine = rope_tables(rows, head_width)
    full, total = 2 * rows, w_qkv.shape[1]
    qk = q_half + kv_half

    normed_a, raw, queries, keys, values = over.call(
        "qkv",
        partial(qkv_kernel, over.per_slot, counts, head_width, scale),
        2,
        [over.early(width_all), over.late(width_all), over.fixed(w_qkv.shape)]
        + [over.fixed(gain_a.shape), over.fixed(gain_h.shape)]
        + [over.repeated(LANES), over.repeated(LANES)],
        [over.both(width_all), over.both(qk), over.both(2 * q_half), over.both(2 * kv_half)]
        + [over.both(2 * kv_half)],
        [((full, width_all), LOW), ((full, qk), F32), ((full, 2 * q_half), LOW)]
        + [((full, 2 * kv_half), LOW)] * 2,
        [],
        2 * full * width_all * total,
        x_own, x_other, w_qkv, gain_a, gain_h, cosine, sine,
    )
    attended, queries = attend(lens, queries, keys, values, rows, head_width, block)
    part, send = over.call(
        "out",
        partial(out_kernel, over.per_slot),
        2,
        [over.both_other_first(q_half), over.fixed(w_o.shape)],
        [over.late(width_all), over.early(width_all)],
        [((rows, width_all), F32), ((rows, width_all), LOW)],
        [],
        2 * full * q_half * width_all,
        attended, w_o,
    )
    wide, slim = over.both(width_all), over.fixed(gain_m.shape)
    eight = (8, width_all)
    resid, normed_b, sums_a = over.call(
        "resid",
        resid_kernel,
        1,
        [wide, wide, wide, slim],
        [wide, wide, pl.BlockSpec(eight, lambda i, lens: (0, 0))],
        [((rows, width_all), F32), ((rows, width_all), LOW), (eight, F32)],
        [],
        1 << 24,
        x_own, part, core_swap(send), gain_m,
    )
    normed_b_other = core_swap(normed_b)

    def across(grad_rows):
        half = grad_rows.shape[1] // 2
        mine = lax.dynamic_slice_in_dim(grad_rows, core * half, half, axis=1)
        other = core_swap(lax.dynamic_slice_in_dim(grad_rows, (1 - core) * half, half, axis=1))
        return ordered(mine, other, 0)

    n = over.per_slot
    sums = []
    ff_grads, ff_levels, ff_totals = [], [], []
    packed_shape = (shards * packed_rows, 2 * units)
    level_shape = (packed_rows, 2 * units)
    first_rows = pl.BlockSpec((block, width_all), lambda i: (jnp.minimum(i, n - 1), 0))
    last_rows = pl.BlockSpec((block, width_all), lambda i: (jnp.maximum(i - n, 0), 0))
    all_rows = pl.BlockSpec((block, width_all), lambda i: (i, 0))

    wide_shape, tall_shape = (width_all, 2 * units), (units, width_all)
    for chunk in range(chunks):
        last = chunk == chunks - 1
        side = Side(
            shards,
            groups,
            [level_shape] if chunk >= 1 else [],
            [level_shape] if chunk >= 2 else [],
            2 * half_shards * folds,
        )
        late = chunk == chunks - 1
        sources = ff_grads[-1:] + ff_levels[-1:]
        ends = [first_rows] * 2 + [last_rows] * 2 if last else [all_rows] * 2
        end_shapes = [jax.ShapeDtypeStruct((full, width_all), F32)] * 2
        if last:
            end_shapes = [jax.ShapeDtypeStruct((rows, width_all), F32)] * 2 + [
                jax.ShapeDtypeStruct((rows, width_all), LOW)
            ] * 2
        outs = pl.pallas_call(
            partial(
                ffn_kernel, n, shards, bool(sums), last, side, 0 if late else chunk * packed_rows
            ),
            out_shape=end_shapes + [jax.ShapeDtypeStruct(packed_shape, LOW)] + side.outs(),
            grid=(2 * n,),
            in_specs=[first_rows, last_rows] * 2
            + [hbm]
            + [all_rows] * len(sums)
            + [hbm] * len(sources),
            out_specs=ends + [hbm] * (1 + len(side.outs())),
            scratch_shapes=[pltpu.VMEM(wide_shape, F32), pltpu.VMEM(tall_shape, F32)]
            + [pltpu.VMEM((units, d_half), LOW)]
            + [pltpu.VMEM(wide_shape, LOW), pltpu.VMEM(tall_shape, LOW)]
            + [pltpu.VMEM(packed_shape, LOW)]
            + [pltpu.SemaphoreType.DMA((shards + half_shards * folds,))]
            + side.scratch(),
            cost_estimate=pl.CostEstimate(
                flops=18 * full * width_all * units, bytes_accessed=1 << 25, transcendentals=0
            ),
            compiler_params=pltpu.CompilerParams(
                collective_id=2 + chunk, has_side_effects=True, vmem_limit_bytes=62 << 20
            ),
            name="ffn",
        )(normed_b, normed_b_other, g_own, g_other, gathered[late], *sums, *sources)
        sums = outs[: len(end_shapes)]
        ff_grads.append(outs[len(end_shapes)])
        rest = outs[len(end_shapes) + 1 :]
        ff_levels += rest[:1]
        ff_totals += rest[1:]
    mlp_part, db_part, mlp_send, db_send = sums
    db_got = core_swap(db_send)
    mlp_got = core_swap(mlp_send)
    output, d_resid, d_attn, sums_b = over.call(
        "resid_back",
        resid_back_kernel,
        1,
        [wide] * 6 + [slim],
        [wide, wide, wide, pl.BlockSpec(eight, lambda i, lens: (0, 0))],
        [((rows, width_all), LOW), ((rows, width_all), F32), ((rows, width_all), LOW)]
        + [(eight, F32)],
        [],
        1 << 24,
        resid, mlp_part, mlp_got, db_part, db_got, g_own, gain_m,
    )

    d_attn_other = core_swap(d_attn)
    d_heads, grad_out = over.call(
        "dout",
        partial(dout_kernel, over.per_slot, head_width),
        2,
        [over.early(width_all), over.late(width_all), over.both(q_half), over.fixed(w_o.shape)],
        [over.both(2 * q_half), over.fixed(w_o.shape)],
        [((full, 2 * q_half), LOW), (w_o.shape, LOW)],
        [pltpu.VMEM(w_o.shape, F32)],
        4 * full * q_half * width_all,
        d_attn, d_attn_other, attended, w_o,
    )
    grad_out = across(grad_out)
    o_level = (d_rows, d_half)
    d_query, d_key, d_value, ff_level, out_level, ff_total = attend_back(
        queries,
        keys,
        values,
        d_heads,
        rows,
        head_width,
        block,
        Side(shards, groups, [level_shape, o_level], [level_shape]),
        [ff_grads[-1], grad_out, ff_levels[-1]],
    )
    ff_totals.append(ff_total)
    turned = pl.BlockSpec((block, LANES), lambda i, lens: (lax.rem(i, n), 0))
    part, send, grad_qkv, gain_sums = over.call(
        "qkv_back",
        partial(qkv_back_kernel, over.per_slot, counts, head_width, scale),
        2,
        [over.both_other_first(q_half)]
        + [over.both_other_first(2 * kv_half)] * 2
        + [over.both_other_first(qk), over.both_other_first(width_all)]
        + [over.fixed(w_qkv.shape), over.fixed(gain_h.shape), turned, turned],
        [over.late(width_all), over.early(width_all), over.fixed(w_qkv.shape)]
        + [pl.BlockSpec((8, LANES), lambda i, lens: (0, 0))],
        [((rows, width_all), F32), ((rows, width_all), LOW), (w_qkv.shape, LOW)]
        + [((8, LANES), F32)],
        [pltpu.VMEM(w_qkv.shape, F32), pltpu.VMEM((block, total), LOW)],
        4 * full * width_all * total,
        d_query, d_key, d_value, raw, normed_a, w_qkv, gain_h, cosine, sine,
    )
    input_grad, sums_c = over.call(
        "input_back",
        input_back_kernel,
        1,
        [wide] * 4 + [slim],
        [wide, pl.BlockSpec(eight, lambda i, lens: (0, 0))],
        [((rows, width_all), LOW), (eight, F32)],
        [],
        1 << 24,
        x_own, part, core_swap(send), d_resid, gain_a,
    )
    mine, other, small = finish_sums(
        grad_qkv,
        lengths,
        [sums_a, sums_b, sums_c, gain_sums],
        [(2, 0), (1, 1), (0, 0), (0, 1), (1, 0), (3, 0), (3, 1)],
        [ff_level, out_level],
        ff_totals,
        shards,
        groups,
    )
    total_ga, total_gm = small[0], small[1]
    total_gh = small[5:7, :LANES].reshape(2, -1, head_width).sum(1)
    totals = jnp.concatenate([small[2:5].sum(1), small[7, :1]])
    statistics = jnp.sqrt(totals[:3] / (totals[3] * width_all))
    me = lax.axis_index("shard")

    def own_piece(vector):
        size = vector.shape[0] // shards
        return lax.dynamic_slice_in_dim(vector, me * size, size)

    ff_mine = ff_totals + [mine[0]]
    ff_other = list(other[3:]) + [other[0]]

    wide = (d_rows, shards * ff_rows)
    shapes = [wide, wide, (chunks * folds, piece // folds, width_all)]
    shapes += [w.shape for w in (w_out, w_query, w_key, w_value)]
    top = d_rows // 8
    low_rows = piece // folds // 8

    def blocks(part):
        return [
            pl.BlockSpec((top, part.shape[1]), lambda i: (i, 0)),
            pl.BlockSpec((low_rows, part.shape[1]), lambda i: (8 * top // low_rows + i, 0)),
        ]

    def whole(part):
        return pl.BlockSpec((top, part.shape[1]), lambda i: (i, 0))

    parts = [one for pair in zip(ff_mine, ff_other) for one in pair for _ in range(2)]
    specs = [one for pair in zip(ff_mine, ff_other) for part in pair for one in blocks(part)]
    pairs = [mine[1], other[1], mine[2], other[2]]
    grad_gate, grad_up, grad_down, grad_out, grad_query, grad_key, grad_value = pl.pallas_call(
        partial(assemble_kernel, chunks, half_shards, folds, (q_half, kv_half)),
        out_shape=[jax.ShapeDtypeStruct(shape, F32) for shape in shapes],
        grid=(8,),
        in_specs=specs + [whole(part) for part in pairs],
        out_specs=[pl.BlockSpec((top, shape[1]), lambda i: (i, 0)) for shape in shapes[:2]]
        + [pl.BlockSpec((shapes[2][0], low_rows, width_all), lambda i: (0, i, 0))]
        + [pl.BlockSpec((top, shape[1]), lambda i: (i, 0)) for shape in shapes[3:]],
        compiler_params=pltpu.CompilerParams(vmem_limit_bytes=48 << 20),
        name="assemble",
    )(*parts, *pairs)
    return (
        output[None],
        input_grad[None],
        own_piece(total_ga),
        grad_query,
        grad_key,
        grad_value,
        own_piece(total_gh[0]),
        own_piece(total_gh[1]),
        grad_out,
        own_piece(total_gm),
        grad_gate,
        grad_up,
        grad_down.reshape(w_down.shape),
        statistics,
    )


def solution(mesh):
    in_specs = (
        P(("rep", "shard"), None, None),
        P(("rep", "shard")),
        P("shard"),
        P("shard", None),
        P("shard", None),
        P("shard", None),
        P("shard"),
        P("shard"),
        P("shard", None),
        P("shard"),
        P("shard", None),
        P("shard", None),
        P("shard", None),
        P(("rep", "shard"), None, None),
    )
    out_specs = (
        P(("rep", "shard"), None, None),
        P(("rep", "shard"), None, None),
        P("shard"),
        P("shard", None),
        P("shard", None),
        P("shard", None),
        P("shard"),
        P("shard"),
        P("shard", None),
        P("shard"),
        P("shard", None),
        P("shard", None),
        P("shard", None),
        P(),
    )
    return jax.shard_map(local, mesh=mesh, in_specs=in_specs, out_specs=out_specs, check_vma=False)
```

profile of v0, /device:TPU:0, one launch (start us, length us, event | category | flops | bytes accessed | tf_op | source)
XLA Modules:
  0.0 553.0 jit_solution(2520476842627909030)
XLA Ops:
  7.2 1.7 copy-done.3
  8.9 1.7 copy-done.4
  10.6 1.7 copy-done.5
  12.2 2.5 pack.1
  16.1 0.6 fusion.7.refs_4_
  16.7 52.4 %gather.1 = (bf16[1024,1024]{1,0:T(8,128)(2,1)}, bf16[512,1024]{1,0:T(8,128)(2,1)}, bf16[4,16,256]{2,1,0:T(8,128)(2,1)}, bf16[1024,1024]{1,0:T(8,128)(2,1)}) custom-call(bf16[256,1024]{1,0:T(8,128)(2,1)} %refs_0_.2, bf16[256,512]{1,0:T(8,128)(2,1)} %refs_1_.2, bf16[256,512]{1,0:T(8,128)(2,1)} %refs_2_.2, bf16[256,1024]{1,0:T(8,128)(2,1)} %refs_3_.1, ...), custom_call_target="tpu_custom_call" | custom-call | tf_op jit(solution)/shard_map/gather/pallas_call | solution.py:1438
  69.1 0.9 slice_reduce_fusion.2
  70.2 0.7 tile.32.gh_ref
  70.9 0.8 fusion.14
  72.9 1.0 copy.29.sin_ref
  74.0 1.0 copy.28.cos_ref
  75.0 1.3 pad_add_fusion.lens_ref
  76.2 19.8 %qkv.1 = (bf16[2048,1024]{1,0:T(8,128)(2,1)}, f32[2048,768]{1,0:T(8,128)}, bf16[2048,1024]{1,0:T(8,128)(2,1)}, bf16[2048,512]{1,0:T(8,128)(2,1)}, bf16[2048,512]{1,0:T(8,128)(2,1)}) custom-call(s32[2]{0:T(128)} %pad_add_fusion.lens_ref, bf16[1024,1024]{1,0:T(8,128)(2,1)} %bitcast.24, bf16[1024,1024]{1,0:T(8,128)(2,1)} %get-tuple-element.81.other_ref, ...), custom_call_target="tpu_custom_call" | custom-call | flops 4294967296 | bytes 16777216 | tf_op jit(solution)/shard_map/qkv/pallas_call | solution.py:1305
  96.1 28.8 %attend.1 = (bf16[2048,512]{1,0:T(8,128)(2,1)}, bf16[2048,1024]{1,0:T(8,128)(2,1)}) custom-call(s32[2]{0:T(128)} %pad_add_fusion.lens_ref, bf16[2048,1024]{1,0:T(8,128)(2,1)} %get-tuple-element.84.q_ref, bf16[2048,512]{1,0:T(8,128)(2,1)} %get-tuple-element.85.k_ref, bf16[2048,512]{1,0:T(8,128)(2,1)} %get-tuple-element.86.v_ref), custom_call_target="tpu_custom_call" | custom-call | flops 8589934592 | bytes 8388608 | tf_op jit(solution)/shard_map/attend/pallas_call | solution.py:809
  124.9 9.2 %out.1 = (f32[1024,1024]{1,0:T(8,128)}, bf16[1024,1024]{1,0:T(8,128)(2,1)}) custom-call(s32[2]{0:T(128)} %pad_add_fusion.lens_ref, bf16[2048,512]{1,0:T(8,128)(2,1)} %get-tuple-element.87.att_ref, bf16[512,1024]{1,0:T(8,128)(2,1)} %get-tuple-element.88.w_ref), custom_call_target="tpu_custom_call" | custom-call | flops 2147483648 | bytes 16777216 | tf_op jit(solution)/shard_map/out/pallas_call | solution.py:1305
  134.1 1.8 bitcast_select_fusion.g_own.g_ref
  136.5 0.7 convert.6.gain_ref
  137.2 1.4 collective-permute-done.1.got_ref
  138.6 7.4 %resid.1 = (f32[1024,1024]{1,0:T(8,128)}, bf16[1024,1024]{1,0:T(8,128)(2,1)}, f32[8,1024]{1,0:T(8,128)}) custom-call(s32[2]{0:T(128)} %pad_add_fusion.lens_ref, bf16[1024,1024]{1,0:T(8,128)(2,1)} %bitcast.25, f32[1024,1024]{1,0:T(8,128)} %get-tuple-element.89.part_ref, bf16[1024,1024]{1,0:T(8,128)(2,1)} %collective-permute-done.1.got_ref, ...), custom_call_target="tpu_custom_call" | custom-call | flops 16777216 | bytes 16777216 | tf_op jit(solution)/shard_map/resid/pallas_call | solution.py:1305
  146.2 4.3 collective-permute-done.2.x_other
  150.6 42.1 %ffn.3 = (f32[2048,1024]{1,0:T(8,128)}, f32[2048,1024]{1,0:T(8,128)}, bf16[1536,1536]{1,0:T(8,128)(2,1)}) custom-call(bf16[1024,1024]{1,0:T(8,128)(2,1)} %get-tuple-element.92.x_own, bf16[1024,1024]{1,0:T(8,128)(2,1)} %collective-permute-done.2.x_other, bf16[1024,1024]{1,0:T(8,128)(2,1)} %copy-done.10, bf16[1024,1024]{1,0:T(8,128)(2,1)} %collective-permute-done.3.g_other, ...), custom_call_target="tpu_custom_call" | custom-call | flops 28991029248 | bytes 33554432 | tf_op jit(solution)/shard_map/ffn/pallas_call | solution.py:1546
  192.7 50.9 %ffn.4 = (f32[2048,1024]{1,0:T(8,128)}, f32[2048,1024]{1,0:T(8,128)}, bf16[1536,1536]{1,0:T(8,128)(2,1)}, bf16[384,1536]{1,0:T(8,128)(2,1)}) custom-call(bf16[1024,1024]{1,0:T(8,128)(2,1)} %get-tuple-element.92.x_own, bf16[1024,1024]{1,0:T(8,128)(2,1)} %collective-permute-done.2.x_other, bf16[1024,1024]{1,0:T(8,128)(2,1)} %copy-done.10, ...), custom_call_target="tpu_custom_call" | custom-call | flops 28991029248 | bytes 33554432 | tf_op jit(solution)/shard_map/ffn/pallas_call | solution.py:1546
  243.7 56.8 %ffn.5 = (f32[1024,1024]{1,0:T(8,128)}, f32[1024,1024]{1,0:T(8,128)}, bf16[1024,1024]{1,0:T(8,128)(2,1)}, bf16[1024,1024]{1,0:T(8,128)(2,1)}, bf16[1536,1536]{1,...) custom-call(bf16[1024,1024]{1,0:T(8,128)(2,1)} %get-tuple-element.92.x_own, ...), custom_call_target="tpu_custom_call" | custom-call | flops 28991029248 | bytes 33554432 | tf_op jit(solution)/shard_map/ffn/pallas_call | solution.py:1546
  301.0 6.1 %collective-permute-done.4.mlp_got = bf16[1024,1024]{1,0:T(8,128)(2,1)S(1)} collective-permute-done((bf16[1024,1024]{1,0:T(8,128)(2,1)}, bf16[1024,1024]{1,0:T(8,128)(2,1)S(1)}, u32[]{:S(2)}, u32[]{:S(2)}) %collective-permute-start.4) | collective-permute-done | bytes 2097184 | tf_op jit(solution)/shard_map/ppermute | solution.py:46
  307.1 0.9 collective-permute-done.5.db_got
  308.4 11.7 %resid_back.1 = (bf16[1024,1024]{1,0:T(8,128)(2,1)}, f32[1024,1024]{1,0:T(8,128)}, bf16[1024,1024]{1,0:T(8,128)(2,1)}, f32[8,1024]{1,0:T(8,128)}) custom-call(s32[2]{0:T(128)} %pad_add_fusion.lens_ref, f32[1024,1024]{1,0:T(8,128)} %get-tuple-element.91.resid_ref, f32[1024,1024]{1,0:T(8,128)} %get-tuple-element.103.mlp_ref, bf16[1024,1024]{1,0:T(8,128)(2,1)} %copy-done.11, ...), custom_call_target="tpu_custom_call" | custom-call | flops 16777216 | bytes 16777216 | tf_op jit(solution)/shard_map/resid_back/pallas_call | solution.py:1305
  320.3 4.2 collective-permute-done.6.other_ref
  324.6 1.3 copy-done.13
  325.9 17.0 %dout.1 = (bf16[2048,1024]{1,0:T(8,128)(2,1)}, bf16[512,1024]{1,0:T(8,128)(2,1)}) custom-call(s32[2]{0:T(128)} %pad_add_fusion.lens_ref, bf16[1024,1024]{1,0:T(8,128)(2,1)} %get-tuple-element.109.own_ref, bf16[1024,1024]{1,0:T(8,128)(2,1)} %copy-done.13, bf16[2048,512]{1,0:T(8,128)(2,1)} %get-tuple-element.87.att_ref, bf16[512,1024]{1,0:T(8,128)(2,1)} %get-tuple-element.88.w_ref), custom_call_target="tpu_custom_call" | custom-call | flops 4294967296 | bytes 16777216 | tf_op jit(solution)/shard_map/dout/pallas_call | solution.py:1305
  342.9 1.3 constant_dynamic-slice_fusion.5
  344.4 1.8 collective-permute-done.7
  346.1 1.4 maximum_select_fusion.refs_1_
  347.6 65.4 %attend_back.1 = (f32[2048,512]{1,0:T(8,128)}, f32[2048,512]{1,0:T(8,128)}, f32[2048,512]{1,0:T(8,128)}, bf16[384,1536]{1,0:T(8,128)(2,1)}, bf16[256,512]{1,0:T(8,128)(2,1)}, /*index=5*/bf16[384,1536]{1,0:T(8,128)(2,1)}) custom-call(bf16[2048,1024]{1,0:T(8,128)(2,1)} %get-tuple-element.108.q_ref, bf16[2048,512]{1,0:T(8,128)(2,1)} %get-tuple-element.85.k_ref, ...), custom_call_target="tpu_custom_call" | custom-call | flops 21474836480 | bytes 16777216 | tf_op jit(solution)/shard_map/attend_back/pallas_call | solution.py:833
  413.0 24.6 %qkv_back.1 = (f32[1024,1024]{1,0:T(8,128)}, bf16[1024,1024]{1,0:T(8,128)(2,1)}, bf16[1024,1024]{1,0:T(8,128)(2,1)}, f32[8,128]{1,0:T(8,128)}) custom-call(s32[2]{0:T(128)} %pad_add_fusion.lens_ref, f32[2048,512]{1,0:T(8,128)} %get-tuple-element.114.dq_ref, f32[2048,512]{1,0:T(8,128)} %get-tuple-element.115.dk_ref, f32[2048,512]{1,0:T(8,128)} %get-tuple-element.116.dv_ref, ...), custom_call_target="tpu_custom_call" | custom-call | flops 8589934592 | bytes 16777216 | tf_op jit(solution)/shard_map/qkv_back/pallas_call | solution.py:1305
  437.6 4.4 collective-permute-done.8.got_ref
  442.0 1.3 copy-done.12
  443.3 8.0 %input_back.1 = (bf16[1024,1024]{1,0:T(8,128)(2,1)}, f32[8,1024]{1,0:T(8,128)}) custom-call(s32[2]{0:T(128)} %pad_add_fusion.lens_ref, bf16[1024,1024]{1,0:T(8,128)(2,1)} %bitcast.26, f32[1024,1024]{1,0:T(8,128)} %get-tuple-element.119.part_ref, bf16[1024,1024]{1,0:T(8,128)(2,1)} %copy-done.12, f32[1024,1024]{1,0:T(8,128)} %get-tuple-element.121.dresid_ref, ...), custom_call_target="tpu_custom_call" | custom-call | flops 16777216 | bytes 16777216 | tf_op jit(solution)/shard_map/input_back/pallas_call | solution.py:1305
  451.4 74.7 %finish.1 = (bf16[384,1536]{1,0:T(8,128)(2,1)}, bf16[256,512]{1,0:T(8,128)(2,1)}, bf16[256,1024]{1,0:T(8,128)(2,1)}, bf16[384,1536]{1,0:T(8,128)(2,1)}, bf16[256...) custom-call(s32[1]{0:T(128)} %copy.32.length_ref, ...), custom_call_target="tpu_custom_call" | custom-call | tf_op jit(solution)/shard_map/finish/pallas_call | solution.py:685
  526.0 1.2 slice.43
  527.2 0.9 slice_reduce_fusion
  528.1 0.7 slice.38
  528.8 0.8 fusion.13
  532.1 1.3 copy-done.2
  533.4 1.0 copy-done.6
  534.4 1.0 copy-done.7
  535.4 0.9 copy-done.8
  536.4 0.9 copy-done.9
  537.3 8.7 %assemble.1 = (f32[256,4608]{1,0:T(8,128)}, f32[256,4608]{1,0:T(8,128)}, f32[9,128,1024]{2,1,0:T(8,128)}, f32[256,1024]{1,0:T(8,128)}, f32[256,1024]{1,0:T(8,128...) custom-call(bf16[384,1536]{1,0:T(8,128)(2,1)S(1)} %copy-done, bf16[384,1536]{1,0:T(8,128)(2,1)S(1)} %copy-done, ...), custom_call_target="tpu_custom_call" | custom-call | tf_op jit(solution)/shard_map/assemble/pallas_call | solution.py:1687
  (64 shorter events, 6.2 us)
Async XLA Ops:
  7.2 139.0 %all-gather.5.cloned.1.call-start = ((), (), s32[]{:S(2)}) async-start(), calls=%async_computation | async-start | bytes 11796480 | tf_op jit(solution)/shard_map/all_gather | solution.py:1413
  7.2 1.7 copy-start.3
  8.9 1.7 copy-start.4
  10.6 1.7 copy-start.5
  14.7 1.3 copy-start.14
  14.7 1.3 copy-start.15
  14.7 1.4 copy-start.16
  14.7 1.4 copy-start.17
  14.8 228.9 %all-gather.7.cloned.1.call-start = ((), (), s32[]{:S(2)}) async-start(), calls=%async_computation.1 | async-start | bytes 5898240 | tf_op jit(solution)/shard_map/all_gather | solution.py:1415
  14.8 60.1 %collective-permute-start = (s32[1]{0:T(128)}, s32[1]{0:T(128)}, u32[]{:S(2)}, u32[]{:S(2)}) collective-permute-start(s32[1]{0:T(128)} %param.15), channel_id=1, source_target_pairs={{0,4},{4,0},{8,12},{12,8},{16,20},{20,16},{24,28},{28,24},{1,5},{5... | collective-permute-start | bytes 20 | tf_op jit(solution)/shard_map/ppermute | solution.py:46
  134.1 4.5 collective-permute-start.1
  135.9 10.1 %copy-start.10 = (bf16[1024,1024]{1,0:T(8,128)(2,1)}, bf16[1024,1024]{1,0:T(8,128)(2,1)S(1)}, u32[]{:S(2)}) copy-start(bf16[1024,1024]{1,0:T(8,128)(2,1)S(1)} %bitcast_select_fusion.g_own.g_ref) | copy-start | bytes 6291460
  135.9 10.3 %collective-permute-start.3 = (bf16[1024,1024]{1,0:T(8,128)(2,1)S(1)}, bf16[1024,1024]{1,0:T(8,128)(2,1)}, u32[]{:S(2)}, u32[]{:S(2)}) collective-permute-start(bf16[1024,1024]{1,0:T(8,128)(2,1)S(1)} %bitcast_select_fusion.g_own.g_ref), channel_id=1, source_target_pairs={{0,4},{4,0},{8,12},{12,8},{16,20},{20,16},{24,28},{28,24},{1,5},{5... | collective-permute-start | bytes 6291464 | tf_op jit(solution)/shard_map/ppermute | solution.py:46
  146.0 4.6 collective-permute-start.2
  300.5 6.7 %collective-permute-start.4 = (bf16[1024,1024]{1,0:T(8,128)(2,1)}, bf16[1024,1024]{1,0:T(8,128)(2,1)S(1)}, u32[]{:S(2)}, u32[]{:S(2)}) collective-permute-start(bf16[1024,1024]{1,0:T(8,128)(2,1)} %get-tuple-element.104), channel_id=1, source_target_pairs={{0,4},{4,0},{8,12},{12,8},{16,20},{20,16},{24,28},{28,24},{1,5},{5... | collective-permute-start | bytes 6291464 | tf_op jit(solution)/shard_map/ppermute | solution.py:46
  300.5 7.5 %collective-permute-start.5 = (bf16[1024,1024]{1,0:T(8,128)(2,1)}, bf16[1024,1024]{1,0:T(8,128)(2,1)}, u32[]{:S(2)}, u32[]{:S(2)}) collective-permute-start(bf16[1024,1024]{1,0:T(8,128)(2,1)} %get-tuple-element.106), channel_id=1, source_target_pairs={{0,4},{4,0},{8,12},{12,8},{16,20},{20,16},{24,28},{28,24},{1,5},{5... | collective-permute-start | bytes 6291464 | tf_op jit(solution)/shard_map/ppermute | solution.py:46
  307.1 1.3 copy-start.11
  320.1 4.4 collective-permute-start.6
  324.6 1.3 copy-start.13
  344.2 2.0 collective-permute-start.7
  437.6 4.4 collective-permute-start.8
  442.0 1.3 copy-start.12
  451.4 80.7 %copy-start = (bf16[384,1536]{1,0:T(8,128)(2,1)S(1)}, bf16[384,1536]{1,0:T(8,128)(2,1)}, u32[]{:S(2)}) copy-start(bf16[384,1536]{1,0:T(8,128)(2,1)} %get-tuple-element.130.refs_7_.refs_0_.refs_1_) | copy-start | bytes 3538948
  451.4 80.7 %copy-start.1 = (bf16[384,1536]{1,0:T(8,128)(2,1)S(1)}, bf16[384,1536]{1,0:T(8,128)(2,1)}, u32[]{:S(2)}) copy-start(bf16[384,1536]{1,0:T(8,128)(2,1)} %get-tuple-element.131.refs_8_.refs_4_.refs_5_) | copy-start | bytes 3538948
  532.1 1.3 copy-start.2
  533.3 1.0 copy-start.6
  534.4 1.0 copy-start.7
  535.4 0.9 copy-start.8
  536.4 0.9 copy-start.9
Sparse Core Ops, SparseCore 0:
  14.9 116.9 all-gather.4
  146.4 53.2 all-gather.6
where the time goes:
time: 558 us; the launch traced here: 553 us
  Pallas kernels  480 us (86%)
  local copies, waits for them, and re-layouts  23.1 us (4%)
  waiting for transfers between devices  23.1 us (4%)
  between operations  15.8 us (3%)
  other arithmetic  8.51 us (2%)
    pallas_call x3, Pallas kernels, local(): pl.pallas_call(partial(ffn_kernel, n, shards, bool(sums), last, side, 0 i...  150 us
    pallas_call x7, Pallas kernels, call(): pl.pallas_call(kernel, out_shape=[jax.ShapeDtypeStruct(shape, kind) for s...  97.8 us
    pallas_call x1, Pallas kernels, finish_sums(): pl.pallas_call(partial(finish_kernel, shards, groups, (len(lows), len(rea...  74.7 us
    pallas_call x1, Pallas kernels, attend_back(): pl.pallas_call(partial(attend_back_kernel, block, width, side), out_shape...  65.4 us
    pallas_call x1, Pallas kernels, local(): pl.pallas_call(partial(gather_kernel, shards, wide_parts, tall_parts, (6,...  52.4 us
    pallas_call x1, Pallas kernels, attend(): pl.pallas_call(partial(attend_kernel, block, width), out_shape=(jax.Shape...  28.8 us
    ppermute x9, waiting for transfers between devices, core_swap(): return lax.ppermute(x, 'rep', pairs)  23.1 us
    unnamed x36, local copies, waits for them, and re-layouts  13.3 us
  transfers between devices with their start and end apart: 11, of which 7 were waited for; matrix products, arithmetic and copies ran while one was open for 2% of the time, Pallas kernels for 38%

commit v1 on v0

--- a/solution.py
+++ b/solution.py
@@ -249,7 +249,10 @@
         copy.wait()
 
 
-def add_up(parts, target, rows):
+def add_up(parts, target, least):
+    total_rows = target.shape[0]
+    rows = max(k for k in range(least, 97, least) if total_rows % k == 0)
+
     def some(i, _):
         here = pl.ds(pl.multiple_of(i * rows, rows), rows)
         total = parts[0][here, :].astype(F32)
@@ -258,7 +261,7 @@
         target[here, :] = total.astype(target.dtype)
         return 0
 
-    lax.fori_loop(0, target.shape[0] // rows, some, 0)
+    lax.fori_loop(0, total_rows // rows, some, 0)
 
 
 def reduce_over_plane(copies, load, shards, grad_ref, level, bufs):
@@ -289,7 +292,7 @@
                 copy.wait_recv()
             add_up([own] + [planes.at[k] for k in range(shards - 1)], level, 16)
 
-        return [start, idle, end]
+        return [start, idle, idle, end]
     fast, slow, across = neighbours(me)
     to_fast, to_slow = device(fast, group, core), device(slow, group, core)
     half = rows // 2
@@ -312,7 +315,11 @@
     ]
 
     def start():
-        for copy in early + loads:
+        for copy in early[:2] + loads:
+            copy.start()
+
+    def direct():
+        for copy in early[2:]:
             copy.start()
 
     def merge():
@@ -333,7 +340,7 @@
             copy.wait_send()
         add_up([own, planes.at[0], planes.at[1]], level, 16)
 
-    return [start, merge, end]
+    return [start, direct, merge, end]
 
 
 def plane_buffers(shards, shape):
@@ -420,7 +427,7 @@
     return [pltpu.VMEM(shape, LOW)] * 3
 
 
-PARTS = 4
+PARTS = 8
 
 
 class LineSum:
@@ -502,6 +509,8 @@
         def begin():
             for stages in planes:
                 stages[0]()
+            for stages in planes:
+                stages[1]()
             for part in range(PARTS):
                 for line in lines:
                     line.run(part, 0)
@@ -521,16 +530,17 @@
 
         def merge():
             for stages in planes:
-                stages[1]()
+                stages[2]()
 
         plan = {
             0: [begin],
-            2: [load_done, of_lines(0, 1)],
-            3: [of_lines(1, 1), merge],
-            4: [of_lines(2, 1), of_lines(0, 2)],
-            5: [of_lines(3, 1), of_lines(1, 2)],
-            6: [of_lines(2, 2)],
-            7: [of_lines(3, 2)],
+            1: [load_done, of_lines(0, 1)],
+            2: [of_lines(1, 1)],
+            3: [of_lines(2, 1), of_lines(3, 1), merge, of_lines(0, 2), of_lines(1, 2)],
+            4: [of_lines(4, 1), of_lines(2, 2), of_lines(3, 2)],
+            5: [of_lines(5, 1), of_lines(6, 1), of_lines(4, 2)],
+            6: [of_lines(7, 1), of_lines(5, 2), of_lines(6, 2)],
+            7: [of_lines(7, 2)],
         }
         for when, stages in plan.items():
 
@@ -547,7 +557,7 @@
 
         def end():
             for stages, store in zip(planes, stores):
-                stages[2]()
+                stages[3]()
                 store.start()
             for part in range(PARTS):
                 for line in lines:
@@ -558,6 +568,48 @@
                 store.wait()
 
         return copies, end
+
+
+class Blocks:
+    def __init__(self, copies, partner, count, block, held, got):
+        self.count, self.block = count, block
+        self.copies = [
+            copies(
+                held.at[pl.ds(k % (held.shape[0] // block) * block, block), :],
+                got.at[pl.ds(k * block, block), :],
+                partner,
+            )
+            for k in range(count)
+        ]
+        self.slots = held.shape[0] // block
+        self.held, self.got = held, got
+
+    def begin(self, step, first):
+        for k in range(self.count):
+
+            @pl.when(step == first + k + 1)
+            def _(k=k):
+                self.copies[k].start()
+                if k + 1 >= self.slots and k + 1 < self.count:
+                    self.copies[k + 1 - self.slots].wait_send()
+
+    def put(self, number, values):
+        self.held[pl.ds(lax.rem(number, self.slots) * self.block, self.block), :] = values
+
+    def take(self, step, first):
+        for k in range(self.count):
+            pl.when(step == first + k)(self.copies[k].wait_recv)
+        start = jnp.clip(step - first, 0, self.count - 1) * self.block
+        return self.got[pl.ds(pl.multiple_of(start, self.block), self.block), :]
+
+    def end(self, sent_last, received):
+        if sent_last:
+            self.copies[-1].start()
+        for k in range(max(0, self.count - self.slots), self.count):
+            self.copies[k].wait_send()
+        if received:
+            for copy in self.copies:
+                copy.wait_recv()
 
 
 def everyone_near(shards, groups):
@@ -625,6 +677,7 @@
     ]
     last = LineSum(copies, groups, level, level, mine[-1], line_bufs[-1])
     stages[0]()
+    stages[1]()
     for part in range(PARTS):
         for one in sums:
             one.run(part, 0)
@@ -635,33 +688,33 @@
     finish(small_copies)
     small_b[group] = sum(small_a[k] for k in range(shards))
     small_copies = [go(small_b.at[group], small_b.at[group], where) for where in line]
-    for part in range(2):
+    for part in range(PARTS // 2):
         for one in sums:
             one.run(part, 1)
-    stages[1]()
-    for part in range(2):
+    stages[2]()
+    for part in range(PARTS // 2):
         for one in sums:
-            one.run(part + 2, 1)
+            one.run(part + PARTS // 2, 1)
             one.run(part, 2)
     finish(small_copies)
     small_c[core] = sum(small_b[k] for k in range(groups))
     small_copies = [go(small_c.at[core], small_c.at[core], partner)]
-    stages[2]()
+    stages[3]()
     for part in range(PARTS):
         last.run(part, 0)
-    for part in range(2, PARTS):
+    for part in range(PARTS // 2, PARTS):
         for one in sums:
             one.run(part, 2)
-        last.run(part - 2, 1)
-    last.run(2, 1)
-    last.run(0, 2)
+    for part in range(PARTS):
+        last.run(part, 1)
+        if part >= 2:
+            last.run(part - 2, 2)
+    for part in range(PARTS - 2, PARTS):
+        last.run(part, 2)
     for part in range(PARTS):
         for one in sums:
             one.run(part, 3)
     swaps += [go(mine[i], other[i], partner) for i in range(counts[0])]
-    last.run(3, 1)
-    for part in range(1, PARTS):
-        last.run(part, 2)
     for part in range(PARTS):
         last.run(part, 3)
     swaps.append(go(mine[-1], other[n - 1], partner))
@@ -923,36 +976,53 @@
             ref[...] = jnp.zeros(ref.shape, ref.dtype)
 
 
-def out_kernel(per_slot, lens_ref, att_ref, w_ref, own_ref, other_ref):
+def out_kernel(
+    per_slot, length_ref, att_ref, w_ref, x_ref, gain_ref, resid_ref, normed_ref, sums_ref,
+    other_out, give, got, hold, other, send, recv, store,
+):
     step = pl.program_id(0)
     block = att_ref.shape[0]
+    me, group, core = place()
+    partner = device(me, group, 1 - core)
+    copies = Copies(send, recv)
+    parts = Blocks(copies, partner, per_slot, block, give, got)
+    normed_parts = Blocks(copies, partner, per_slot, block, hold, other)
+
+    @pl.when(step == 0)
+    def _():
+        meet([partner])
+        sums_ref[...] = jnp.zeros(sums_ref.shape, F32)
+
+    parts.begin(step, 0)
+    normed_parts.begin(step, per_slot)
+    product = nn(att_ref[...], w_ref[...])
 
     @pl.when(step < per_slot)
     def _():
-        other_ref[...] = nn(att_ref[...], w_ref[...]).astype(LOW)
+        parts.put(step, product.astype(LOW))
 
     @pl.when(step >= per_slot)
     def _():
-        own_ref[...] = nn(att_ref[...], w_ref[...])
-
-
-def resid_kernel(lens_ref, x_ref, part_ref, got_ref, gain_ref, resid_ref, normed_ref, sums_ref):
-    step = pl.program_id(0)
-    block = x_ref.shape[0]
-    valid = lax.broadcasted_iota(jnp.int32, (block, 1), 0) + step * block < lens_ref[0]
-    attn_out = part_ref[...] + got_ref[...].astype(F32)
-    resid = x_ref[...].astype(F32) + attn_out
-    resid_ref[...] = resid
-    normed_ref[...] = (resid * row_rsqrt(resid) * gain_ref[...]).astype(LOW)
-
-    @pl.when(step == 0)
+        number = step - per_slot
+        valid = lax.broadcasted_iota(jnp.int32, (block, 1), 0) + number * block < length_ref[0]
+        attn_out = product + parts.take(step, per_slot).astype(F32)
+        resid = x_ref[...].astype(F32) + attn_out
+        resid_ref[...] = resid
+        normed = (resid * row_rsqrt(resid) * gain_ref[...]).astype(LOW)
+        normed_ref[...] = normed
+        normed_parts.put(number, normed)
+        for row, values in ((0, resid), (1, attn_out)):
+            sums_ref[row : row + 1, :] += jnp.sum(
+                jnp.where(valid, values * values, 0.0), axis=0, keepdims=True
+            )
+
+    @pl.when(step == 2 * per_slot - 1)
     def _():
-        sums_ref[...] = jnp.zeros(sums_ref.shape, F32)
-
-    for row, values in ((0, resid), (1, attn_out)):
-        sums_ref[row : row + 1, :] += jnp.sum(
-            jnp.where(valid, values * values, 0.0), axis=0, keepdims=True
-        )
+        parts.end(False, False)
+        normed_parts.end(True, True)
+        copy = pltpu.make_async_copy(other, other_out, store.at[0])
+        copy.start()
+        copy.wait()
 
 
 def ffn_kernel(
@@ -960,18 +1030,23 @@
 ):
     if chained:
         (mlp_in, db_in), refs = take(refs, 2)
+    if last:
+        (length_ref, resid_ref, gain_ref), refs = take(refs, 3)
     count = len(side.plane_shapes) + len(side.line_shapes)
     sources, refs = take(refs, count)
-    (mlp_own, db_own), refs = take(refs, 2)
     if last:
-        (mlp_other, db_other), refs = take(refs, 2)
+        (out_ref, dresid_ref, dattn_ref, sums_ref, dattn_out), refs = take(refs, 5)
+    else:
+        (mlp_ref, db_ref), refs = take(refs, 2)
     (grad_out,), refs = take(refs, 1)
     totals, refs = take(refs, count)
-    (acc_ref, accd_ref, given_ref, w_ref, wd_ref, grad_ref, load), bufs = take(refs, 7)
+    (acc_ref, accd_ref, given_ref, w_ref, wd_ref, grad_ref, load), refs = take(refs, 7)
+    exchange, bufs = take(refs, 6 if last else 0)
     step = pl.program_id(0)
     copies, end = side.run(step, sources, totals, bufs)
-    own = step < per_slot
+    own = step >= per_slot if last else step < per_slot
     units, depth = wd_ref.shape
+    block = x_own.shape[0]
     me, group, core = place()
     partner = device(me, group, 1 - core)
     half, columns, d_rows = shards // 2, depth // 2, depth // shards
@@ -1004,8 +1079,19 @@
         for k, (i, fold) in enumerate(tiles)
     ]
 
+    if last:
+        give_mlp, got_mlp, give_db, got_db, hold, other = exchange
+        mlp_parts = Blocks(copies, partner, per_slot, block, give_mlp, got_mlp)
+        db_parts = Blocks(copies, partner, per_slot, block, give_db, got_db)
+        attn_parts = Blocks(copies, partner, per_slot, block, hold, other)
+        mlp_parts.begin(step, 0)
+        db_parts.begin(step, 0)
+        attn_parts.begin(step, per_slot)
+
     @pl.when(step == 0)
     def _():
+        if last:
+            sums_ref[...] = jnp.zeros(sums_ref.shape, F32)
         for copy in given + loads:
             copy.start()
         acc_ref[...] = jnp.zeros(acc_ref.shape, F32)
@@ -1033,19 +1119,34 @@
         d_b += db_in[...]
     if last:
 
-        @pl.when(own)
+        @pl.when(step < per_slot)
         def _():
-            mlp_own[...] = mlp
-            db_own[...] = d_b
-
-        @pl.when(jnp.logical_not(own))
+            mlp_parts.put(step, mlp.astype(LOW))
+            db_parts.put(step, d_b.astype(LOW))
+
+        @pl.when(step >= per_slot)
         def _():
-            mlp_other[...] = mlp.astype(LOW)
-            db_other[...] = d_b.astype(LOW)
+            number = step - per_slot
+            valid = lax.broadcasted_iota(jnp.int32, (block, 1), 0) + number * block < length_ref[0]
+            resid = resid_ref[...]
+            mlp_out = mlp + mlp_parts.take(step, per_slot).astype(F32)
+            out_ref[...] = jnp.where(valid, resid + mlp_out, 0.0).astype(LOW)
+            d_norm, d_gain = norm_back(
+                resid, d_b + db_parts.take(step, per_slot).astype(F32), gain_ref[...]
+            )
+            d_resid = jnp.where(valid, g.astype(F32) + d_norm, 0.0)
+            dresid_ref[...] = d_resid
+            d_attn = d_resid.astype(LOW)
+            dattn_ref[...] = d_attn
+            attn_parts.put(number, d_attn)
+            for row, values in ((0, mlp_out * mlp_out), (1, d_gain)):
+                sums_ref[row : row + 1, :] += jnp.sum(
+                    jnp.where(valid, values, 0.0), axis=0, keepdims=True
+                )
 
     else:
-        mlp_own[...] = mlp
-        db_own[...] = d_b
+        mlp_ref[...] = mlp
+        db_ref[...] = d_b
     acc_ref[:, :units] += tn(x, d_gate)
     acc_ref[:, units:] += tn(x, d_up)
     accd_ref[...] += tn(hidden, g)
@@ -1079,10 +1180,17 @@
         for copy in out:
             copy.wait_send()
             copy.wait_recv()
-        store = pltpu.make_async_copy(grad_ref, grad_out, load.at[0])
-        store.start()
+        stores = [pltpu.make_async_copy(grad_ref, grad_out, load.at[0])]
+        stores[0].start()
+        if last:
+            mlp_parts.end(False, False)
+            db_parts.end(False, False)
+            attn_parts.end(True, True)
+            stores.append(pltpu.make_async_copy(other, dattn_out, load.at[1]))
+            stores[1].start()
         end()
-        store.wait()
+        for store in stores:
+            store.wait()
 
 
 def norm_back(values, dy, gain):
@@ -1090,31 +1198,6 @@
     scaled = dy * gain
     inner = jnp.mean(values * scaled, axis=1, keepdims=True)
     return inverse * scaled - values * (inverse * inverse * inverse * inner), dy * values * inverse
-
-
-def resid_back_kernel(
-    lens_ref, resid_ref, mlp_ref, mlp_got, db_ref, db_got, g_ref, gain_ref,
-    out_ref, dresid_ref, dattn_ref, sums_ref,
-):
-    step = pl.program_id(0)
-    block = resid_ref.shape[0]
-    valid = lax.broadcasted_iota(jnp.int32, (block, 1), 0) + step * block < lens_ref[0]
-    resid = resid_ref[...]
-    mlp_out = mlp_ref[...] + mlp_got[...].astype(F32)
-    out_ref[...] = jnp.where(valid, resid + mlp_out, 0.0).astype(LOW)
-    d_norm, d_gain = norm_back(resid, db_ref[...] + db_got[...].astype(F32), gain_ref[...])
-    d_resid = jnp.where(valid, g_ref[...].astype(F32) + d_norm, 0.0)
-    dresid_ref[...] = d_resid
-    dattn_ref[...] = d_resid.astype(LOW)
-
-    @pl.when(step == 0)
-    def _():
-        sums_ref[...] = jnp.zeros(sums_ref.shape, F32)
-
-    for row, values in ((0, mlp_out * mlp_out), (1, d_gain)):
-        sums_ref[row : row + 1, :] += jnp.sum(
-            jnp.where(valid, values, 0.0), axis=0, keepdims=True
-        )
 
 
 def dout_kernel(
@@ -1160,87 +1243,74 @@
 
 
 def qkv_back_kernel(
-    per_slot, counts, width, scale, lens_ref, dq_ref, dk_ref, dv_ref, raw_ref, normed_ref, w_ref, gh_ref,
-    cos_ref, sin_ref, own_ref, other_ref, grad_ref, gain_ref, acc_ref, low_ref,
+    per_slot, counts, width, scale, dq_ref, dk_ref, dv_ref, raw_ref, normed_ref, w_ref, gh_ref,
+    cos_ref, sin_ref, x_ref, dresid_ref, ga_ref, out_ref, grad_ref, gain_ref, sums_ref,
+    acc_ref, low_ref, give, got, send, recv,
 ):
     step = pl.program_id(0)
     block = dq_ref.shape[0]
     q_tiles, kv_tiles = counts
-    slot_step = lax.rem(step + per_slot, 2 * per_slot)
+    me, group, core = place()
+    partner = device(me, group, 1 - core)
+    parts = Blocks(Copies(send, recv), partner, per_slot, block, give, got)
 
     @pl.when(step == 0)
     def _():
+        meet([partner])
         acc_ref[...] = jnp.zeros(acc_ref.shape, F32)
         gain_ref[...] = jnp.zeros(gain_ref.shape, F32)
-
-    live = is_live(lens_ref, slot_step, per_slot, block)
-
-    def put(d_a):
-        @pl.when(step < per_slot)
-        def _():
-            other_ref[...] = d_a.astype(LOW)
-
-        @pl.when(step >= per_slot)
-        def _():
-            own_ref[...] = d_a
-
-    @pl.when(live)
+        sums_ref[...] = jnp.zeros(sums_ref.shape, F32)
+
+    parts.begin(step, 0)
+    lane = lax.broadcasted_iota(jnp.int32, (block, LANES), 1)
+    cosine, sine = cos_ref[...], sin_ref[...]
+
+    def pair(ref, tile):
+        return jnp.where(
+            lane < width,
+            ref[:, pl.ds(2 * tile * LANES, LANES)],
+            pltpu.roll(ref[:, pl.ds((2 * tile + 1) * LANES, LANES)], width, 1),
+        )
+
+    for tile in range(q_tiles + 2 * kv_tiles):
+        lanes = pl.ds(tile * LANES, LANES)
+        if tile >= q_tiles + kv_tiles:
+            low_ref[:, lanes] = pair(dv_ref, tile - q_tiles - kv_tiles).astype(LOW)
+            continue
+        if tile < q_tiles:
+            turned, row = dq_ref[:, lanes] * scale, 0
+        else:
+            turned, row = pair(dk_ref, tile - q_tiles), 1
+        gain = gh_ref[row : row + 1, :]
+        dy = turned * cosine + swap_halves(turned * sine, width)
+        values = raw_ref[:, lanes]
+        inverse = lax.rsqrt(head_sum(values * values, width) * (1.0 / width) + EPS)
+        scaled = dy * gain
+        inner = head_sum(values * scaled, width) * (1.0 / width)
+        low_ref[:, lanes] = (
+            inverse * scaled - values * (inverse * inverse * inverse * inner)
+        ).astype(LOW)
+        gain_ref[row : row + 1, :] += jnp.sum(dy * values * inverse, axis=0, keepdims=True)
+    low = low_ref[...]
+    acc_ref[...] += tn(normed_ref[...], low)
+    d_a = nt(low, w_ref[...])
+
+    @pl.when(step < per_slot)
     def _():
-        lane = lax.broadcasted_iota(jnp.int32, (block, LANES), 1)
-        cosine, sine = cos_ref[...], sin_ref[...]
-
-        def pair(ref, tile):
-            return jnp.where(
-                lane < width,
-                ref[:, pl.ds(2 * tile * LANES, LANES)],
-                pltpu.roll(ref[:, pl.ds((2 * tile + 1) * LANES, LANES)], width, 1),
-            )
-
-        for tile in range(q_tiles + 2 * kv_tiles):
-            lanes = pl.ds(tile * LANES, LANES)
-            if tile >= q_tiles + kv_tiles:
-                low_ref[:, lanes] = pair(dv_ref, tile - q_tiles - kv_tiles).astype(LOW)
-                continue
-            is_query = tile < q_tiles
-            if is_query:
-                turned, row = dq_ref[:, lanes] * scale, 0
-            else:
-                turned, row = pair(dk_ref, tile - q_tiles), 1
-            gain = gh_ref[row : row + 1, :]
-            dy = turned * cosine + swap_halves(turned * sine, width)
-            values = raw_ref[:, lanes]
-            inverse = lax.rsqrt(head_sum(values * values, width) * (1.0 / width) + EPS)
-            scaled = dy * gain
-            inner = head_sum(values * scaled, width) * (1.0 / width)
-            low_ref[:, lanes] = (
-                inverse * scaled - values * (inverse * inverse * inverse * inner)
-            ).astype(LOW)
-            gain_ref[row : row + 1, :] += jnp.sum(dy * values * inverse, axis=0, keepdims=True)
-        low = low_ref[...]
-        acc_ref[...] += tn(normed_ref[...], low)
-        put(nt(low, w_ref[...]))
-
-    @pl.when(jnp.logical_not(live))
+        parts.put(step, d_a.astype(LOW))
+
+    @pl.when(step >= per_slot)
     def _():
-        put(jnp.zeros(own_ref.shape, F32))
-
-    @pl.when(step == pl.num_programs(0) - 1)
+        d_norm, d_gain = norm_back(
+            x_ref[...].astype(F32), d_a + parts.take(step, per_slot).astype(F32), ga_ref[...]
+        )
+        out_ref[...] = (dresid_ref[...] + d_norm).astype(LOW)
+        sums_ref[0:1, :] += jnp.sum(d_gain, axis=0, keepdims=True)
+
+    @pl.when(step == 2 * per_slot - 1)
     def _():
         grad_ref[...] = acc_ref[...].astype(LOW)
-
-
-def input_back_kernel(lens_ref, x_ref, part_ref, got_ref, dresid_ref, gain_ref, out_ref, sums_ref):
-    step = pl.program_id(0)
-    d_norm, d_gain = norm_back(
-        x_ref[...].astype(F32), part_ref[...] + got_ref[...].astype(F32), gain_ref[...]
-    )
-    out_ref[...] = (dresid_ref[...] + d_norm).astype(LOW)
-
-    @pl.when(step == 0)
-    def _():
-        sums_ref[...] = jnp.zeros(sums_ref.shape, F32)
-
-    sums_ref[0:1, :] += jnp.sum(d_gain, axis=0, keepdims=True)
+        parts.end(False, False)
 
 
 def assemble_kernel(chunks, half, folds, widths, *refs):
@@ -1411,8 +1481,6 @@
 
         packs = [jnp.concatenate([packed_chunk(k) for k in some]) for some in chunk_sets]
     gathered = [lax.all_gather(packs[0], "shard", axis=0)]
-    later, _ = lax.optimization_barrier((packs[1], gathered[0]))
-    gathered.append(lax.all_gather(later, "shard", axis=0))
 
     def gain_row(*gains):
         flat = jnp.concatenate(gains)
@@ -1484,31 +1552,45 @@
         x_own, x_other, w_qkv, gain_a, gain_h, cosine, sine,
     )
     attended, queries = attend(lens, queries, keys, values, rows, head_width, block)
-    part, send = over.call(
-        "out",
-        partial(out_kernel, over.per_slot),
-        2,
-        [over.both_other_first(q_half), over.fixed(w_o.shape)],
-        [over.late(width_all), over.early(width_all)],
-        [((rows, width_all), F32), ((rows, width_all), LOW)],
-        [],
-        2 * full * q_half * width_all,
-        attended, w_o,
-    )
-    wide, slim = over.both(width_all), over.fixed(gain_m.shape)
+    later, attended = lax.optimization_barrier((packs[1], attended))
+    gathered.append(lax.all_gather(later, "shard", axis=0))
+    n = over.per_slot
     eight = (8, width_all)
-    resid, normed_b, sums_a = over.call(
-        "resid",
-        resid_kernel,
-        1,
-        [wide, wide, wide, slim],
-        [wide, wide, pl.BlockSpec(eight, lambda i, lens: (0, 0))],
-        [((rows, width_all), F32), ((rows, width_all), LOW), (eight, F32)],
-        [],
-        1 << 24,
-        x_own, part, core_swap(send), gain_m,
-    )
-    normed_b_other = core_swap(normed_b)
+    first_rows = pl.BlockSpec((block, width_all), lambda i: (jnp.minimum(i, n - 1), 0))
+    last_rows = pl.BlockSpec((block, width_all), lambda i: (jnp.maximum(i - n, 0), 0))
+    all_rows = pl.BlockSpec((block, width_all), lambda i: (i, 0))
+    smem = pl.BlockSpec(memory_space=pltpu.SMEM)
+
+    def other_first(width):
+        return pl.BlockSpec((block, width), lambda i: (lax.rem(i + n, 2 * n), 0))
+
+    def held(shape):
+        return pl.BlockSpec(shape, lambda i: (0, 0), pipeline_mode=pl.Buffered(1))
+
+    sums_spec = pl.BlockSpec(eight, lambda i: (0, 0))
+    slot_rows = pltpu.VMEM((rows, width_all), LOW)
+    resid, normed_b, sums_a, normed_b_other = pl.pallas_call(
+        partial(out_kernel, n),
+        out_shape=[
+            jax.ShapeDtypeStruct((rows, width_all), F32),
+            jax.ShapeDtypeStruct((rows, width_all), LOW),
+            jax.ShapeDtypeStruct(eight, F32),
+            jax.ShapeDtypeStruct((rows, width_all), LOW),
+        ],
+        grid=(2 * n,),
+        in_specs=[smem, other_first(q_half), held(w_o.shape), last_rows, held(gain_m.shape)],
+        out_specs=[last_rows, last_rows, sums_spec, hbm],
+        scratch_shapes=[pltpu.VMEM((2 * block, width_all), LOW), slot_rows, slot_rows, slot_rows]
+        + [pltpu.SemaphoreType.DMA((2 * n,))] * 2
+        + [pltpu.SemaphoreType.DMA((1,))],
+        cost_estimate=pl.CostEstimate(
+            flops=2 * full * q_half * width_all, bytes_accessed=1 << 24, transcendentals=0
+        ),
+        compiler_params=pltpu.CompilerParams(
+            collective_id=6, has_side_effects=True, vmem_limit_bytes=40 << 20
+        ),
+        name="out",
+    )(lengths, attended, w_o, x_own, gain_m)
 
     def across(grad_rows):
         half = grad_rows.shape[1] // 2
@@ -1516,15 +1598,10 @@
         other = core_swap(lax.dynamic_slice_in_dim(grad_rows, (1 - core) * half, half, axis=1))
         return ordered(mine, other, 0)
 
-    n = over.per_slot
     sums = []
     ff_grads, ff_levels, ff_totals = [], [], []
     packed_shape = (shards * packed_rows, 2 * units)
     level_shape = (packed_rows, 2 * units)
-    first_rows = pl.BlockSpec((block, width_all), lambda i: (jnp.minimum(i, n - 1), 0))
-    last_rows = pl.BlockSpec((block, width_all), lambda i: (jnp.maximum(i - n, 0), 0))
-    all_rows = pl.BlockSpec((block, width_all), lambda i: (i, 0))
-
     wide_shape, tall_shape = (width_all, 2 * units), (units, width_all)
     for chunk in range(chunks):
         last = chunk == chunks - 1
@@ -1533,25 +1610,38 @@
             groups,
             [level_shape] if chunk >= 1 else [],
             [level_shape] if chunk >= 2 else [],
-            2 * half_shards * folds,
+            2 * half_shards * folds + 3 * n,
         )
         late = chunk == chunks - 1
         sources = ff_grads[-1:] + ff_levels[-1:]
-        ends = [first_rows] * 2 + [last_rows] * 2 if last else [all_rows] * 2
+        ends = [all_rows] * 2
         end_shapes = [jax.ShapeDtypeStruct((full, width_all), F32)] * 2
+        own_rows, other_rows, sum_rows, more, more_specs, exchange = (
+            first_rows, last_rows, all_rows, [], [], []
+        )
         if last:
-            end_shapes = [jax.ShapeDtypeStruct((rows, width_all), F32)] * 2 + [
-                jax.ShapeDtypeStruct((rows, width_all), LOW)
-            ] * 2
+            own_rows, other_rows, sum_rows = last_rows, first_rows, other_first(width_all)
+            more = [lengths, resid, gain_m]
+            more_specs = [smem, last_rows, held(gain_m.shape)]
+            ends = [last_rows] * 3 + [sums_spec, hbm]
+            end_shapes = [
+                jax.ShapeDtypeStruct((rows, width_all), LOW),
+                jax.ShapeDtypeStruct((rows, width_all), F32),
+                jax.ShapeDtypeStruct((rows, width_all), LOW),
+                jax.ShapeDtypeStruct(eight, F32),
+                jax.ShapeDtypeStruct((rows, width_all), LOW),
+            ]
+            exchange = [pltpu.VMEM((2 * block, width_all), LOW), slot_rows] * 3
         outs = pl.pallas_call(
             partial(
                 ffn_kernel, n, shards, bool(sums), last, side, 0 if late else chunk * packed_rows
             ),
             out_shape=end_shapes + [jax.ShapeDtypeStruct(packed_shape, LOW)] + side.outs(),
             grid=(2 * n,),
-            in_specs=[first_rows, last_rows] * 2
+            in_specs=[own_rows, other_rows] * 2
             + [hbm]
-            + [all_rows] * len(sums)
+            + [sum_rows] * len(sums)
+            + more_specs
             + [hbm] * len(sources),
             out_specs=ends + [hbm] * (1 + len(side.outs())),
             scratch_shapes=[pltpu.VMEM(wide_shape, F32), pltpu.VMEM(tall_shape, F32)]
@@ -1559,37 +1649,23 @@
             + [pltpu.VMEM(wide_shape, LOW), pltpu.VMEM(tall_shape, LOW)]
             + [pltpu.VMEM(packed_shape, LOW)]
             + [pltpu.SemaphoreType.DMA((shards + half_shards * folds,))]
+            + exchange
             + side.scratch(),
             cost_estimate=pl.CostEstimate(
                 flops=18 * full * width_all * units, bytes_accessed=1 << 25, transcendentals=0
             ),
             compiler_params=pltpu.CompilerParams(
-                collective_id=2 + chunk, has_side_effects=True, vmem_limit_bytes=62 << 20
+                collective_id=2 + chunk, has_side_effects=True, vmem_limit_bytes=67043328
             ),
             name="ffn",
-        )(normed_b, normed_b_other, g_own, g_other, gathered[late], *sums, *sources)
+        )(normed_b, normed_b_other, g_own, g_other, gathered[late], *sums, *more, *sources)
         sums = outs[: len(end_shapes)]
         ff_grads.append(outs[len(end_shapes)])
         rest = outs[len(end_shapes) + 1 :]
         ff_levels += rest[:1]
         ff_totals += rest[1:]
-    mlp_part, db_part, mlp_send, db_send = sums
-    db_got = core_swap(db_send)
-    mlp_got = core_swap(mlp_send)
-    output, d_resid, d_attn, sums_b = over.call(
-        "resid_back",
-        resid_back_kernel,
-        1,
-        [wide] * 6 + [slim],
-        [wide, wide, wide, pl.BlockSpec(eight, lambda i, lens: (0, 0))],
-        [((rows, width_all), LOW), ((rows, width_all), F32), ((rows, width_all), LOW)]
-        + [(eight, F32)],
-        [],
-        1 << 24,
-        resid, mlp_part, mlp_got, db_part, db_got, g_own, gain_m,
-    )
-
-    d_attn_other = core_swap(d_attn)
+    output, d_resid, d_attn, sums_b, d_attn_other = sums
+
     d_heads, grad_out = over.call(
         "dout",
         partial(dout_kernel, over.per_slot, head_width),
@@ -1615,33 +1691,33 @@
         [ff_grads[-1], grad_out, ff_levels[-1]],
     )
     ff_totals.append(ff_total)
-    turned = pl.BlockSpec((block, LANES), lambda i, lens: (lax.rem(i, n), 0))
-    part, send, grad_qkv, gain_sums = over.call(
-        "qkv_back",
-        partial(qkv_back_kernel, over.per_slot, counts, head_width, scale),
-        2,
-        [over.both_other_first(q_half)]
-        + [over.both_other_first(2 * kv_half)] * 2
-        + [over.both_other_first(qk), over.both_other_first(width_all)]
-        + [over.fixed(w_qkv.shape), over.fixed(gain_h.shape), turned, turned],
-        [over.late(width_all), over.early(width_all), over.fixed(w_qkv.shape)]
-        + [pl.BlockSpec((8, LANES), lambda i, lens: (0, 0))],
-        [((rows, width_all), F32), ((rows, width_all), LOW), (w_qkv.shape, LOW)]
-        + [((8, LANES), F32)],
-        [pltpu.VMEM(w_qkv.shape, F32), pltpu.VMEM((block, total), LOW)],
-        4 * full * width_all * total,
-        d_query, d_key, d_value, raw, normed_a, w_qkv, gain_h, cosine, sine,
-    )
-    input_grad, sums_c = over.call(
-        "input_back",
-        input_back_kernel,
-        1,
-        [wide] * 4 + [slim],
-        [wide, pl.BlockSpec(eight, lambda i, lens: (0, 0))],
-        [((rows, width_all), LOW), (eight, F32)],
-        [],
-        1 << 24,
-        x_own, part, core_swap(send), d_resid, gain_a,
+    turned = pl.BlockSpec((block, LANES), lambda i: (lax.rem(i, n), 0))
+    input_grad, grad_qkv, gain_sums, sums_c = pl.pallas_call(
+        partial(qkv_back_kernel, n, counts, head_width, scale),
+        out_shape=[
+            jax.ShapeDtypeStruct((rows, width_all), LOW),
+            jax.ShapeDtypeStruct(w_qkv.shape, LOW),
+            jax.ShapeDtypeStruct((8, LANES), F32),
+            jax.ShapeDtypeStruct(eight, F32),
+        ],
+        grid=(2 * n,),
+        in_specs=[other_first(q_half), other_first(2 * kv_half), other_first(2 * kv_half)]
+        + [other_first(qk), other_first(width_all), held(w_qkv.shape), held(gain_h.shape)]
+        + [turned, turned, last_rows, last_rows, held(gain_a.shape)],
+        out_specs=[last_rows, held(w_qkv.shape)]
+        + [pl.BlockSpec((8, LANES), lambda i: (0, 0)), sums_spec],
+        scratch_shapes=[pltpu.VMEM(w_qkv.shape, F32), pltpu.VMEM((block, total), LOW)]
+        + [pltpu.VMEM((2 * block, width_all), LOW), slot_rows]
+        + [pltpu.SemaphoreType.DMA((n,))] * 2,
+        cost_estimate=pl.CostEstimate(
+            flops=4 * full * width_all * total, bytes_accessed=1 << 24, transcendentals=0
+        ),
+        compiler_params=pltpu.CompilerParams(
+            collective_id=7, has_side_effects=True, vmem_limit_bytes=48 << 20
+        ),
+        name="qkv_back",
+    )(
+        d_query, d_key, d_value, raw, normed_a, w_qkv, gain_h, cosine, sine, x_own, d_resid, gain_a
     )
     mine, other, small = finish_sums(
         grad_qkv,

time: 558 us -> 526 us (0.943)
  Pallas kernels: 480 us -> 455 us
  waiting for transfers between devices: 23.1 us -> 1.95 us
  local copies, waits for them, and re-layouts: 23.1 us -> 34.8 us
    pallas_call x7 -> x2, Pallas kernels: 97.8 us -> 36.5 us  [call(): pl.pallas_call(kernel, out_shape=[jax.ShapeDtypeStruct(shape, kind) for s...]
    pallas_call x0 -> x2, Pallas kernels: none -> 35 us  [the longest x1 24.7 us: local(): pl.pallas_call(partial(qkv_back_kernel, n, counts, head_width, scale), ou...]
    ppermute x9 -> x3, waiting for transfers between devices: 23.1 us -> 1.89 us  [core_swap(): return lax.ppermute(x, 'rep', pairs)]
    unnamed x36 -> x68, local copies, waits for them, and re-layouts: 13.3 us -> 25 us
    pallas_call x3, Pallas kernels: 150 us -> 157 us  [local(): pl.pallas_call(partial(ffn_kernel, n, shards, bool(sums), last, side, 0 i...]
  transfers between devices with their start and end apart: 11 -> 5, of which waited for: 7 -> 1; matrix products, arithmetic and copies ran while one was open for 2% -> 2% of each run, Pallas kernels for 38% -> 41%
where the time goes in v1:
time: 526 us; the launch traced here: 516 us
  Pallas kernels  455 us (87%)
  local copies, waits for them, and re-layouts  34.8 us (7%)
  between operations  16 us (3%)
  other arithmetic  7.43 us (1%)
    pallas_call x3, Pallas kernels, local(): pl.pallas_call(partial(ffn_kernel, n, shards, bool(sums), last, side, 0 i...  157 us
    pallas_call x1, Pallas kernels, finish_sums(): pl.pallas_call(partial(finish_kernel, shards, groups, (len(lows), len(rea...  74.1 us
    pallas_call x1, Pallas kernels, attend_back(): pl.pallas_call(partial(attend_back_kernel, block, width, side), out_shape...  60.5 us
    pallas_call x1, Pallas kernels, local(): pl.pallas_call(partial(gather_kernel, shards, wide_parts, tall_parts, (6,...  54.8 us
    pallas_call x2, Pallas kernels, call(): pl.pallas_call(kernel, out_shape=[jax.ShapeDtypeStruct(shape, kind) for s...  36.5 us
    pallas_call x1, Pallas kernels, attend(): pl.pallas_call(partial(attend_kernel, block, width), out_shape=(jax.Shape...  25.4 us
    unnamed x68, local copies, waits for them, and re-layouts  25 us
    pallas_call x1, Pallas kernels, local(): pl.pallas_call(partial(qkv_back_kernel, n, counts, head_width, scale), ou...  24.7 us
  transfers between devices with their start and end apart: 5, of which 1 were waited for; matrix products, arithmetic and copies ran while one was open for 2% of the time, Pallas kernels for 41%

profile of v1, /device:TPU:0, one launch (start us, length us, event | category | flops | bytes accessed | tf_op | source)
XLA Modules:
  0.0 515.8 jit_solution(6845851925906139223)
XLA Ops:
  7.2 1.7 copy-done.4
  8.9 1.7 copy-done.5
  10.6 1.7 copy-done.6
  12.2 2.4 pack.1
  16.3 1.5 bitcast_select_fusion.g_own
  18.4 0.6 fusion.7.refs_4_
  19.0 54.8 %gather.1 = (bf16[1024,1024]{1,0:T(8,128)(2,1)}, bf16[512,1024]{1,0:T(8,128)(2,1)}, bf16[4,16,256]{2,1,0:T(8,128)(2,1)}, bf16[1024,1024]{1,0:T(8,128)(2,1)}) custom-call(bf16[256,1024]{1,0:T(8,128)(2,1)} %refs_0_.3, bf16[256,512]{1,0:T(8,128)(2,1)} %refs_1_.3, bf16[256,512]{1,0:T(8,128)(2,1)} %refs_2_.4, bf16[256,1024]{1,0:T(8,128)(2,1)} %refs_3_.1, ...), custom_call_target="tpu_custom_call" | custom-call | tf_op jit(solution)/shard_map/gather/pallas_call | solution.py:1506
  73.8 0.9 slice_reduce_fusion.2
  74.8 0.7 tile.32.gh_ref
  75.5 0.8 fusion.14
  77.5 1.0 copy.29.sin_ref
  78.6 1.0 copy.28.cos_ref
  79.6 1.2 pad_add_fusion.lens_ref
  80.7 20.1 %qkv.1 = (bf16[2048,1024]{1,0:T(8,128)(2,1)}, f32[2048,768]{1,0:T(8,128)}, bf16[2048,1024]{1,0:T(8,128)(2,1)}, bf16[2048,512]{1,0:T(8,128)(2,1)}, bf16[2048,512]{1,0:T(8,128)(2,1)}) custom-call(s32[2]{0:T(128)} %pad_add_fusion.lens_ref, bf16[1024,1024]{1,0:T(8,128)(2,1)} %bitcast.24, bf16[1024,1024]{1,0:T(8,128)(2,1)} %get-tuple-element.77.other_ref, ...), custom_call_target="tpu_custom_call" | custom-call | flops 4294967296 | bytes 16777216 | tf_op jit(solution)/shard_map/qkv/pallas_call | solution.py:1375
  100.9 25.4 %attend.1 = (bf16[2048,512]{1,0:T(8,128)(2,1)}, bf16[2048,1024]{1,0:T(8,128)(2,1)}) custom-call(s32[2]{0:T(128)} %pad_add_fusion.lens_ref, bf16[2048,1024]{1,0:T(8,128)(2,1)} %get-tuple-element.80.q_ref, bf16[2048,512]{1,0:T(8,128)(2,1)} %get-tuple-element.81.k_ref, bf16[2048,512]{1,0:T(8,128)(2,1)} %get-tuple-element.82.v_ref), custom_call_target="tpu_custom_call" | custom-call | flops 8589934592 | bytes 8388608 | tf_op jit(solution)/shard_map/attend/pallas_call | solution.py:862
  126.4 1.6 copy-done.24
  128.0 10.3 %out.1 = (f32[1024,1024]{1,0:T(8,128)S(1)}, bf16[1024,1024]{1,0:T(8,128)(2,1)S(1)}, f32[8,1024]{1,0:T(8,128)S(1)}, bf16[1024,1024]{1,0:T(8,128)(2,1)S(1)}) custom-call(s32[1]{0:T(128)} %copy.34.length_ref.refs_2_, bf16[2048,512]{1,0:T(8,128)(2,1)S(1)} %copy-done.24, bf16[512,1024]{1,0:T(8,128)(2,1)S(1)} %copy-done.22, bf16[1024,1024]{1,0:T(8,128)(2,1)S(1)} %bitcast.26, ...), custom_call_target="tpu_custom_call" | custom-call | flops 2147483648 | bytes 16777216 | tf_op jit(solution)/shard_map/out/pallas_call | solution.py:1572
  138.4 0.6 copy-done.16
  139.0 2.0 copy-done.23
  141.0 1.3 copy-done.25
  142.3 1.4 copy-done.26
  143.7 44.0 %ffn.3 = (f32[2048,1024]{1,0:T(8,128)}, f32[2048,1024]{1,0:T(8,128)}, bf16[1536,1536]{1,0:T(8,128)(2,1)}) custom-call(bf16[1024,1024]{1,0:T(8,128)(2,1)} %copy-done.25, bf16[1024,1024]{1,0:T(8,128)(2,1)} %copy-done.26, bf16[1024,1024]{1,0:T(8,128)(2,1)} %bitcast_select_fusion.g_own, bf16[1024,1024]{1,0:T(8,128)(2,1)} %collective-permute-done.1.g_other, ...), custom_call_target="tpu_custom_call" | custom-call | flops 28991029248 | bytes 33554432 | tf_op jit(solution)/shard_map/ffn/pallas_call | solution.py:1635
  187.7 54.3 %ffn.4 = (f32[2048,1024]{1,0:T(8,128)}, f32[2048,1024]{1,0:T(8,128)}, bf16[1536,1536]{1,0:T(8,128)(2,1)}, bf16[384,1536]{1,0:T(8,128)(2,1)}) custom-call(bf16[1024,1024]{1,0:T(8,128)(2,1)} %copy-done.25, bf16[1024,1024]{1,0:T(8,128)(2,1)} %copy-done.26, bf16[1024,1024]{1,0:T(8,128)(2,1)} %bitcast_select_fusion.g_own, ...), custom_call_target="tpu_custom_call" | custom-call | flops 28991029248 | bytes 33554432 | tf_op jit(solution)/shard_map/ffn/pallas_call | solution.py:1635
  242.0 58.7 %ffn.5 = (bf16[1024,1024]{1,0:T(8,128)(2,1)}, f32[1024,1024]{1,0:T(8,128)}, bf16[1024,1024]{1,0:T(8,128)(2,1)}, f32[8,1024]{1,0:T(8,128)}, bf16[1024,1024]{1,0:T...) custom-call(bf16[1024,1024]{1,0:T(8,128)(2,1)} %copy-done.25, ...), custom_call_target="tpu_custom_call" | custom-call | flops 28991029248 | bytes 33554432 | tf_op jit(solution)/shard_map/ffn/pallas_call | solution.py:1635
  300.7 16.4 %dout.1 = (bf16[2048,1024]{1,0:T(8,128)(2,1)}, bf16[512,1024]{1,0:T(8,128)(2,1)}) custom-call(s32[2]{0:T(128)} %pad_add_fusion.lens_ref, bf16[1024,1024]{1,0:T(8,128)(2,1)} %get-tuple-element.100.own_ref, bf16[1024,1024]{1,0:T(8,128)(2,1)} %get-tuple-element.101.other_ref, bf16[2048,512]{1,0:T(8,128)(2,1)} %get-tuple-element.84.att_ref, ...), custom_call_target="tpu_custom_call" | custom-call | flops 4294967296 | bytes 16777216 | tf_op jit(solution)/shard_map/dout/pallas_call | solution.py:1375
  317.1 1.3 constant_dynamic-slice_fusion.5
  318.5 1.9 collective-permute-done.2
  320.4 1.4 maximum_select_fusion.refs_1_
  321.8 60.5 %attend_back.1 = (f32[2048,512]{1,0:T(8,128)}, f32[2048,512]{1,0:T(8,128)}, f32[2048,512]{1,0:T(8,128)}, bf16[384,1536]{1,0:T(8,128)(2,1)}, bf16[256,512]{1,0:T(8,128)(2,1)}, /*index=5*/bf16[384,1536]{1,0:T(8,128)(2,1)}) custom-call(bf16[2048,1024]{1,0:T(8,128)(2,1)} %get-tuple-element.99.q_ref, bf16[2048,512]{1,0:T(8,128)(2,1)} %get-tuple-element.81.k_ref, ...), custom_call_target="tpu_custom_call" | custom-call | flops 21474836480 | bytes 16777216 | tf_op jit(solution)/shard_map/attend_back/pallas_call | solution.py:886
  382.4 24.7 %qkv_back.1 = (bf16[1024,1024]{1,0:T(8,128)(2,1)S(1)}, bf16[1024,1024]{1,0:T(8,128)(2,1)S(1)}, f32[8,128]{1,0:T(8,128)S(1)}, f32[8,1024]{1,0:T(8,128)S(1)}) custom-call(f32[2048,512]{1,0:T(8,128)} %get-tuple-element.106.dq_ref, f32[2048,512]{1,0:T(8,128)} %get-tuple-element.107.dk_ref, f32[2048,512]{1,0:T(8,128)} %get-tuple-element.108.dv_ref, ...), custom_call_target="tpu_custom_call" | custom-call | flops 8589934592 | bytes 16777216 | tf_op jit(solution)/shard_map/qkv_back/pallas_call | solution.py:1695
  407.1 1.3 copy-done.9
  408.4 1.3 copy-done.11
  409.7 0.6 copy-done.17
  410.3 0.6 copy-done.21
  410.9 74.1 %finish.1 = (bf16[384,1536]{1,0:T(8,128)(2,1)}, bf16[256,512]{1,0:T(8,128)(2,1)}, bf16[256,1024]{1,0:T(8,128)(2,1)}, bf16[384,1536]{1,0:T(8,128)(2,1)}, bf16[256...) custom-call(s32[1]{0:T(128)} %copy.34.length_ref.refs_2_, ...), custom_call_target="tpu_custom_call" | custom-call | tf_op jit(solution)/shard_map/finish/pallas_call | solution.py:738
  485.0 1.2 slice.43
  486.2 0.9 slice_reduce_fusion
  487.1 0.7 slice.38
  487.8 0.8 fusion.13
  491.1 1.3 copy-done.3
  492.3 1.0 copy-done.12
  493.4 1.0 copy-done.13
  494.4 0.9 copy-done.14
  495.4 0.9 copy-done.15
  496.3 8.8 %assemble.1 = (f32[256,4608]{1,0:T(8,128)}, f32[256,4608]{1,0:T(8,128)}, f32[9,128,1024]{2,1,0:T(8,128)}, f32[256,1024]{1,0:T(8,128)}, f32[256,1024]{1,0:T(8,128...) custom-call(bf16[384,1536]{1,0:T(8,128)(2,1)S(1)} %copy-done, bf16[384,1536]{1,0:T(8,128)(2,1)S(1)} %copy-done, ...), custom_call_target="tpu_custom_call" | custom-call | tf_op jit(solution)/shard_map/assemble/pallas_call | solution.py:1763
  505.1 1.3 copy.35
  506.5 1.0 copy-done.10
  507.5 1.3 copy.36
  (81 shorter events, 4.9 us)
Async XLA Ops:
  7.2 136.5 %all-gather.7.cloned.1.call-start = ((), (), s32[]{:S(2)}) async-start(), calls=%async_computation.1 | async-start | bytes 11796480 | tf_op jit(solution)/shard_map/all_gather | solution.py:1483
  7.2 1.7 copy-start.4
  8.9 1.7 copy-start.5
  10.6 1.7 copy-start.6
  14.7 1.6 copy-start.27
  14.7 227.3 %all-gather.5.cloned.1.call-start = ((), (), s32[]{:S(2)}) async-start(), calls=%async_computation | async-start | bytes 5898240 | tf_op jit(solution)/shard_map/all_gather | solution.py:1556
  14.7 64.8 %collective-permute-start = (s32[1]{0:T(128)}, s32[1]{0:T(128)}, u32[]{:S(2)}, u32[]{:S(2)}) collective-permute-start(s32[1]{0:T(128)} %param.15), channel_id=1, source_target_pairs={{0,4},{4,0},{8,12},{12,8},{16,20},{20,16},{24,28},{28,24},{1,5},{5... | collective-permute-start | bytes 20 | tf_op jit(solution)/shard_map/ppermute | solution.py:46
  16.3 2.0 copy-start.29
  16.3 2.0 copy-start.30
  16.3 2.1 copy-start.31
  16.3 2.1 copy-start.32
  17.8 125.8 %collective-permute-start.1 = (bf16[1024,1024]{1,0:T(8,128)(2,1)}, bf16[1024,1024]{1,0:T(8,128)(2,1)}, u32[]{:S(2)}, u32[]{:S(2)}) collective-permute-start(bf16[1024,1024]{1,0:T(8,128)(2,1)} %bitcast_select_fusion.g_own), channel_id=1, source_target_pairs={{0,4},{4,0},{8,12},{12,8},{16,20},{20,16},{24,28},{28,24},{1,5},{5... | collective-permute-start | bytes 6291464 | tf_op jit(solution)/shard_map/ppermute | solution.py:46
  100.9 25.5 %copy-start.2 = (bf16[1,1024,1024]{2,1,0:T(8,128)(2,1)S(1)}, bf16[1,1024,1024]{2,1,0:T(8,128)(2,1)}, u32[]{:S(2)}) copy-start(bf16[1,1024,1024]{2,1,0:T(8,128)(2,1)} %param.14) | copy-start | bytes 6291460
  100.9 25.5 %copy-start.22 = (bf16[512,1024]{1,0:T(8,128)(2,1)S(1)}, bf16[512,1024]{1,0:T(8,128)(2,1)}, u32[]{:S(2)}) copy-start(bf16[512,1024]{1,0:T(8,128)(2,1)} %get-tuple-element.85.w_ref) | copy-start | bytes 3145732
  126.3 12.0 %copy-start.20 = (f32[1,1024]{1,0:T(1,128)}, f32[1,1024]{1,0:T(1,128)S(1)}, u32[]{:S(2)}) copy-start(f32[1,1024]{1,0:T(1,128)S(1)} %convert.6.gain_ref.refs_4_) | copy-start | bytes 12292
  126.4 1.6 copy-start.24
  138.3 0.6 copy-start.16
  139.0 2.0 copy-start.23
  141.0 1.3 copy-start.25
  142.3 1.4 copy-start.26
  318.4 2.0 collective-permute-start.2
  321.8 60.6 %copy-start.7 = (f32[1024,128]{1,0:T(8,128)S(1)}, f32[1024,128]{1,0:T(8,128)}, u32[]{:S(2)}) copy-start(f32[1024,128]{1,0:T(8,128)} %copy.29.sin_ref) | copy-start | bytes 1572868
  321.8 60.6 %copy-start.8 = (f32[1024,128]{1,0:T(8,128)S(1)}, f32[1024,128]{1,0:T(8,128)}, u32[]{:S(2)}) copy-start(f32[1024,128]{1,0:T(8,128)} %copy.28.cos_ref) | copy-start | bytes 1572868
  321.8 60.6 %copy-start.18 = (f32[8,128]{1,0:T(8,128)S(1)}, f32[8,128]{1,0:T(8,128)}, u32[]{:S(2)}) copy-start(f32[8,128]{1,0:T(8,128)} %tile.32.gh_ref) | copy-start | bytes 12292
  321.8 60.6 %copy-start.19 = (f32[1,1024]{1,0:T(1,128)S(1)}, f32[1,1024]{1,0:T(1,128)}, u32[]{:S(2)}) copy-start(f32[1,1024]{1,0:T(1,128)} %convert.5.ga_ref) | copy-start | bytes 12292
  407.1 1.3 copy-start.9
  408.4 1.3 copy-start.11
  409.7 0.6 copy-start.17
  410.3 0.6 copy-start.21
  410.9 80.1 %copy-start = (bf16[384,1536]{1,0:T(8,128)(2,1)S(1)}, bf16[384,1536]{1,0:T(8,128)(2,1)}, u32[]{:S(2)}) copy-start(bf16[384,1536]{1,0:T(8,128)(2,1)} %get-tuple-element.120.refs_7_.refs_0_.refs_1_) | copy-start | bytes 3538948
  410.9 80.1 %copy-start.1 = (bf16[384,1536]{1,0:T(8,128)(2,1)S(1)}, bf16[384,1536]{1,0:T(8,128)(2,1)}, u32[]{:S(2)}) copy-start(bf16[384,1536]{1,0:T(8,128)(2,1)} %get-tuple-element.121.refs_8_.refs_4_.refs_5_) | copy-start | bytes 3538948
  491.1 1.3 copy-start.3
  492.3 1.0 copy-start.12
  493.4 1.0 copy-start.13
  494.4 0.9 copy-start.14
  495.4 0.9 copy-start.15
  496.3 8.8 %copy-start.28 = (bf16[1024,1024]{1,0:T(8,128)(2,1)S(1)}, bf16[1024,1024]{1,0:T(8,128)(2,1)}, u32[]{:S(2)}) copy-start(bf16[1024,1024]{1,0:T(8,128)(2,1)} %get-tuple-element.98) | copy-start | bytes 6291460
  505.1 2.4 copy-start.10
Sparse Core Ops, SparseCore 0:
  14.8 119.2 all-gather.6
  135.9 57.0 all-gather.4

commit v2 on v1

--- a/solution.py
+++ b/solution.py
@@ -430,10 +430,15 @@
 PARTS = 8
 
 
+def parts_of(shape):
+    return PARTS if shape[0] * shape[1] >= 1 << 18 else PARTS // 2
+
+
 class LineSum:
     def __init__(self, copies, groups, source, part, total, bufs):
-        rows = part.shape[0] // PARTS
-        each = len(bufs) // PARTS
+        self.count = parts_of(part.shape)
+        rows = part.shape[0] // self.count
+        each = len(bufs) // self.count
         self.parts = [
             reduce_over_line(
                 copies,
@@ -443,19 +448,25 @@
                 at_rows(total, i * rows, rows),
                 bufs[i * each : (i + 1) * each],
             )
-            for i in range(PARTS)
+            for i in range(self.count)
         ]
 
     def run(self, part, stage):
-        self.parts[part][stage]()
+        if part < self.count:
+            self.parts[part][stage]()
+
+    def all(self, stage, first=0, last=None):
+        for part in self.parts[first:last]:
+            part[stage]()
 
     @staticmethod
     def buffers(groups, shape):
-        return line_buffers(groups, (shape[0] // PARTS, shape[1])) * PARTS
+        count = parts_of(shape)
+        return line_buffers(groups, (shape[0] // count, shape[1])) * count
 
     @staticmethod
-    def copies(groups):
-        return PARTS * max(3, groups - 1)
+    def copies(groups, shape):
+        return parts_of(shape) * max(3, groups - 1)
 
 
 class Side:
@@ -474,7 +485,7 @@
         for shape in self.line_shapes:
             shapes += [pltpu.VMEM(shape, LOW)] + LineSum.buffers(groups, shape)
         count = 2 * self.shards + len(self.plane_shapes) * max(6, shards - 1)
-        count += len(self.line_shapes) * LineSum.copies(groups) + self.extra
+        count += sum(LineSum.copies(groups, shape) for shape in self.line_shapes) + self.extra
         loads = 4 * len(self.plane_shapes) + 2 * len(self.line_shapes) + 1
         return shapes + [pltpu.SemaphoreType.DMA((count,))] * 2 + [pltpu.SemaphoreType.DMA((loads,))]
 
@@ -501,10 +512,9 @@
         for i, shape in enumerate(self.line_shapes):
             (own,), bufs = take(bufs, 1)
             some, bufs = take(bufs, len(LineSum.buffers(groups, shape)))
-            loads.append(
-                pltpu.make_async_copy(sources[first + i], own, load.at[3 * first + i])
-            )
-            lines.append(LineSum(copies, groups, sources[first + i], own, totals[first + i], some))
+            source = at_rows(sources[first + i], 0, shape[0])
+            loads.append(pltpu.make_async_copy(source, own, load.at[3 * first + i]))
+            lines.append(LineSum(copies, groups, source, own, totals[first + i], some))
 
         def begin():
             for stages in planes:
@@ -625,21 +635,25 @@
     return refs[:count], refs[count:]
 
 
-def finish_kernel(shards, groups, counts, rows, length_ref, *refs):
+def finish_kernel(shards, groups, counts, rows, skip, length_ref, *refs):
     smalls, refs = take(refs, 1 + max(k for k, _ in rows))
     (grad_ref,), refs = take(refs, 1)
     lows, refs = take(refs, counts[0])
     ready, refs = take(refs, counts[1])
-    n = counts[0] + 1
+    n = counts[0] + 2
+    mine_out, refs = take(refs, n)
+    other, refs = take(refs, n + counts[1])
+    (total_ref,), refs = take(refs, 1)
     mine, refs = take(refs, n)
-    other, refs = take(refs, n + counts[1])
-    (total_ref, level), refs = take(refs, 2)
-    plane_bufs, refs = take(refs, len(plane_buffers(shards, (16, LANES))))
+    levels, refs = take(refs, 2)
     own, refs = take(refs, counts[0])
-    per_line = len(LineSum.buffers(groups, (32, LANES)))
+    plane_bufs = []
+    for level in levels:
+        some, refs = take(refs, len(plane_buffers(shards, level.shape)))
+        plane_bufs.append(some)
     line_bufs = []
-    for _ in range(n):
-        some, refs = take(refs, per_line)
+    for one in mine:
+        some, refs = take(refs, len(LineSum.buffers(groups, one.shape)))
         line_bufs.append(some)
     small_a, small_b, small_c, send, recv, load = refs
     me, group, core = place()
@@ -658,7 +672,10 @@
             copy.wait_send()
             copy.wait_recv()
 
-    loads = [pltpu.make_async_copy(low, own[i], load.at[3 + i]) for i, low in enumerate(lows)]
+    parts = [
+        at_rows(low, 0 if i else skip, one.shape[0]) for i, (low, one) in enumerate(zip(lows, own))
+    ]
+    loads = [pltpu.make_async_copy(low, own[i], load.at[6 + i]) for i, low in enumerate(parts)]
     for copy in loads:
         copy.start()
     for i, (k, row) in enumerate(rows):
@@ -671,84 +688,103 @@
         (small_a.shape[1] - len(rows), small_a.shape[2]), length_ref[0].astype(F32)
     )
     meet(everyone_near(shards, groups))
-    stages = reduce_over_plane(copies, load.at[pl.ds(0, 3)], shards, grad_ref, level, plane_bufs)
+    columns = levels[0].shape[1]
+    planes = [
+        reduce_over_plane(
+            copies,
+            load.at[pl.ds(3 * i, 3)],
+            shards,
+            grad_ref.at[:, pl.ds(i * columns, columns)],
+            level,
+            plane_bufs[i],
+        )
+        for i, level in enumerate(levels)
+    ]
     sums = [
-        LineSum(copies, groups, low, own[i], mine[i], line_bufs[i]) for i, low in enumerate(lows)
+        LineSum(copies, groups, source, part, mine[i], line_bufs[i])
+        for i, (source, part) in enumerate(zip(parts + list(levels), list(own) + list(levels)))
     ]
-    last = LineSum(copies, groups, level, level, mine[-1], line_bufs[-1])
-    stages[0]()
-    stages[1]()
-    for part in range(PARTS):
-        for one in sums:
-            one.run(part, 0)
+    early, halves = sums[: counts[0]], sums[counts[0] :]
+    for stages in planes:
+        stages[0]()
+        stages[1]()
+    for one in early:
+        one.all(0)
+    small_copies = [go(small_a.at[me], small_a.at[me], where) for where in plane]
     swaps = [go(source, target, partner) for source, target in zip(ready, other[n:])]
-    small_copies = [go(small_a.at[me], small_a.at[me], where) for where in plane]
     for copy in loads:
         copy.wait()
+    planes[0][2]()
+    planes[1][2]()
+    for one in early:
+        one.all(1, 0, one.count // 2)
+    planes[0][3]()
+    halves[0].all(0)
     finish(small_copies)
     small_b[group] = sum(small_a[k] for k in range(shards))
     small_copies = [go(small_b.at[group], small_b.at[group], where) for where in line]
-    for part in range(PARTS // 2):
-        for one in sums:
-            one.run(part, 1)
-    stages[2]()
-    for part in range(PARTS // 2):
-        for one in sums:
-            one.run(part + PARTS // 2, 1)
-            one.run(part, 2)
+    for one in early:
+        one.all(1, one.count // 2)
+        one.all(2, 0, one.count // 2)
+    planes[1][3]()
+    halves[1].all(0)
+    for one in early:
+        one.all(2, one.count // 2)
     finish(small_copies)
     small_c[core] = sum(small_b[k] for k in range(groups))
     small_copies = [go(small_c.at[core], small_c.at[core], partner)]
-    stages[3]()
-    for part in range(PARTS):
-        last.run(part, 0)
-    for part in range(PARTS // 2, PARTS):
-        for one in sums:
-            one.run(part, 2)
-    for part in range(PARTS):
-        last.run(part, 1)
-        if part >= 2:
-            last.run(part - 2, 2)
-    for part in range(PARTS - 2, PARTS):
-        last.run(part, 2)
-    for part in range(PARTS):
-        for one in sums:
-            one.run(part, 3)
-    swaps += [go(mine[i], other[i], partner) for i in range(counts[0])]
-    for part in range(PARTS):
-        last.run(part, 3)
-    swaps.append(go(mine[-1], other[n - 1], partner))
+    halves[0].all(1)
+    halves[1].all(1)
+    halves[0].all(2)
+    stores = []
+
+    def hand(i):
+        sums[i].all(3)
+        swaps.append(go(mine[i], other[i], partner))
+        stores.append(pltpu.make_async_copy(mine[i], mine_out[i], load.at[6 + counts[0] + i]))
+        stores[-1].start()
+
+    for i in range(counts[0]):
+        hand(i)
+    halves[1].all(2)
+    hand(counts[0])
+    hand(counts[0] + 1)
     finish(small_copies)
     total_ref[...] = small_c[0] + small_c[1]
     finish(swaps)
-
-
-def finish_sums(grad, length, smalls, rows, lows, ready, shards, groups):
-    level = (grad.shape[0] // shards, grad.shape[1])
-    shapes = [low.shape for low in lows] + [level]
+    for store in stores:
+        store.wait()
+
+
+def finish_sums(grad, length, smalls, rows, lows, skip, ready, shards, groups):
+    level = (grad.shape[0] // shards, grad.shape[1] // 2)
+    shapes = [(low.shape[0] - (0 if i else skip), low.shape[1]) for i, low in enumerate(lows)]
+    shapes += [level] * 2
     others = shapes + [one.shape for one in ready]
     vmem = pl.BlockSpec(memory_space=pltpu.VMEM)
     hbm = pl.BlockSpec(memory_space=pltpu.HBM)
-    scratch = [pltpu.VMEM(level, LOW)] + plane_buffers(shards, level)
-    scratch += [pltpu.VMEM(shape, LOW) for shape in shapes[:-1]]
+    scratch = [pltpu.VMEM(shape, LOW) for shape in shapes + [level] * 2 + shapes[: len(lows)]]
+    for _ in range(2):
+        scratch += plane_buffers(shards, level)
     for shape in shapes:
         scratch += LineSum.buffers(groups, shape)
-    count = 6 + 2 * shards + len(shapes) * LineSum.copies(groups) + len(others) + groups
+    count = 2 * max(6, shards) + sum(LineSum.copies(groups, shape) for shape in shapes)
+    count += len(others) + shards + groups
     small = (8, max(one.shape[1] for one in smalls))
     outs = pl.pallas_call(
-        partial(finish_kernel, shards, groups, (len(lows), len(ready)), rows),
+        partial(finish_kernel, shards, groups, (len(lows), len(ready)), rows, skip),
         out_shape=[jax.ShapeDtypeStruct(shape, LOW) for shape in shapes + others]
         + [jax.ShapeDtypeStruct(small, F32)],
         in_specs=[pl.BlockSpec(memory_space=pltpu.SMEM)]
         + [vmem] * len(smalls)
         + [hbm] * (1 + len(lows) + len(ready)),
-        out_specs=[vmem] * (len(shapes) + len(shapes)) + [hbm] * len(ready) + [vmem],
+        out_specs=[hbm] * (len(shapes) + len(others)) + [vmem],
         scratch_shapes=scratch
-        + [pltpu.VMEM((count,) + small, F32) for count in (shards, groups, 2)]
+        + [pltpu.VMEM((size,) + small, F32) for size in (shards, groups, 2)]
         + [pltpu.SemaphoreType.DMA((count,)), pltpu.SemaphoreType.DMA((count,))]
-        + [pltpu.SemaphoreType.DMA((3 + len(lows),))],
+        + [pltpu.SemaphoreType.DMA((6 + len(lows) + len(shapes),))],
         compiler_params=pltpu.CompilerParams(
-            collective_id=1, has_side_effects=True, vmem_limit_bytes=56 << 20
+            collective_id=1, has_side_effects=True, vmem_limit_bytes=62 << 20
         ),
         name="finish",
     )(length, *smalls, grad, *lows, *ready)
@@ -899,7 +935,7 @@
         scratch_shapes=side.scratch(),
         cost_estimate=pl.CostEstimate(flops=flops, bytes_accessed=1 << 24, transcendentals=0),
         compiler_params=pltpu.CompilerParams(
-            collective_id=5, has_side_effects=True, vmem_limit_bytes=56 << 20
+            collective_id=5, has_side_effects=True, vmem_limit_bytes=62 << 20
         ),
         name="attend_back",
     )(queries, keys, values, douts, *sources)
@@ -1201,62 +1237,75 @@
 
 
 def dout_kernel(
-    per_slot, width, lens_ref, own_ref, other_ref, att_ref, w_ref, do_ref, grad_ref, acc_ref
+    per_slot, width, own_ref, other_ref, att_ref, w_ref, do_ref, grad_out,
+    acc_ref, give, hold, send, recv, store,
 ):
     step = pl.program_id(0)
     block = own_ref.shape[0]
+    me, group, core = place()
 
     @pl.when(step == 0)
     def _():
+        meet([device(me, group, 1 - core)])
         acc_ref[...] = jnp.zeros(acc_ref.shape, F32)
 
-    @pl.when(is_live(lens_ref, step, per_slot, block))
-    def _():
-        d_attn = jnp.where(step < per_slot, own_ref[...], other_ref[...])
-        lane = lax.broadcasted_iota(jnp.int32, (block, LANES), 1)
-        att = att_ref[...]
-        acc_ref[...] += tn(att, d_attn)
-        for tile in range(att.shape[1] // LANES):
-            lanes = slice(tile * LANES, (tile + 1) * LANES)
-            if tile % 2 == 0:
-                pair = nt(d_attn, w_ref[tile * LANES : (tile + 2) * LANES, :])
-            dout = pair[:, (tile % 2) * LANES : (tile % 2 + 1) * LANES].astype(LOW).astype(F32)
-            delta = -head_sum(dout * att[:, lanes].astype(F32), width)
-            for head, (values, column) in enumerate(
-                ((dout, pltpu.roll(delta, width, 1)), (pltpu.roll(dout, width, 1), delta))
-            ):
-                high, rest = two_parts(column)
-                column = jnp.where(
-                    lane == width, high, jnp.where(lane == width + 1, rest, jnp.zeros_like(rest))
-                )
-                do_ref[:, pl.ds((2 * tile + head) * LANES, LANES)] = jnp.where(
-                    lane < width, values.astype(LOW), column
-                )
-
-    @pl.when(jnp.logical_not(is_live(lens_ref, step, per_slot, block)))
-    def _():
-        do_ref[...] = jnp.zeros(do_ref.shape, LOW)
+    d_attn = jnp.where(step < per_slot, own_ref[...], other_ref[...])
+    lane = lax.broadcasted_iota(jnp.int32, (block, LANES), 1)
+    att = att_ref[...]
+    acc_ref[...] += tn(att, d_attn)
+    for tile in range(att.shape[1] // LANES):
+        lanes = slice(tile * LANES, (tile + 1) * LANES)
+        if tile % 2 == 0:
+            pair = nt(d_attn, w_ref[tile * LANES : (tile + 2) * LANES, :])
+        dout = pair[:, (tile % 2) * LANES : (tile % 2 + 1) * LANES].astype(LOW).astype(F32)
+        delta = -head_sum(dout * att[:, lanes].astype(F32), width)
+        for head, (values, column) in enumerate(
+            ((dout, pltpu.roll(delta, width, 1)), (pltpu.roll(dout, width, 1), delta))
+        ):
+            high, rest = two_parts(column)
+            column = jnp.where(
+                lane == width, high, jnp.where(lane == width + 1, rest, jnp.zeros_like(rest))
+            )
+            do_ref[:, pl.ds((2 * tile + head) * LANES, LANES)] = jnp.where(
+                lane < width, values.astype(LOW), column
+            )
 
     @pl.when(step == pl.num_programs(0) - 1)
     def _():
-        grad_ref[...] = acc_ref[...].astype(LOW)
+        rows, columns = give.shape
+        theirs = pl.ds(pl.multiple_of((1 - core) * columns, columns), columns)
+        give[...] = acc_ref[:, theirs].astype(LOW)
+        mine = pl.ds(pl.multiple_of(core * columns, columns), columns)
+        goal = at_rows(hold, core * rows, rows)
+        hold[pl.ds(pl.multiple_of(core * rows, rows), rows), :] = acc_ref[:, mine].astype(LOW)
+        copy = Copies(send, recv)(give, goal, device(me, group, 1 - core))
+        copy.start()
+        copy.wait_send()
+        copy.wait_recv()
+        local = pltpu.make_async_copy(hold, grad_out, store.at[0])
+        local.start()
+        local.wait()
 
 
 def qkv_back_kernel(
-    per_slot, counts, width, scale, dq_ref, dk_ref, dv_ref, raw_ref, normed_ref, w_ref, gh_ref,
-    cos_ref, sin_ref, x_ref, dresid_ref, ga_ref, out_ref, grad_ref, gain_ref, sums_ref,
-    acc_ref, low_ref, give, got, send, recv,
+    per_slot, counts, width, scale, side, dq_ref, dk_ref, dv_ref, raw_ref, normed_ref, w_ref, gh_ref,
+    cos_ref, sin_ref, x_ref, dresid_ref, ga_ref, *refs,
 ):
     step = pl.program_id(0)
     block = dq_ref.shape[0]
     q_tiles, kv_tiles = counts
     me, group, core = place()
     partner = device(me, group, 1 - core)
-    parts = Blocks(Copies(send, recv), partner, per_slot, block, give, got)
+    count = len(side.plane_shapes) + len(side.line_shapes)
+    sources, refs = take(refs, count)
+    (out_ref, grad_ref, gain_ref, sums_ref), refs = take(refs, 4)
+    totals, refs = take(refs, count)
+    (acc_ref, low_ref, give, got), bufs = take(refs, 4)
+    copies, end = side.run(step, sources, totals, bufs)
+    parts = Blocks(copies, partner, per_slot, block, give, got)
 
     @pl.when(step == 0)
     def _():
-        meet([partner])
         acc_ref[...] = jnp.zeros(acc_ref.shape, F32)
         gain_ref[...] = jnp.zeros(gain_ref.shape, F32)
         sums_ref[...] = jnp.zeros(sums_ref.shape, F32)
@@ -1311,11 +1360,13 @@
     def _():
         grad_ref[...] = acc_ref[...].astype(LOW)
         parts.end(False, False)
-
-
-def assemble_kernel(chunks, half, folds, widths, *refs):
+        end()
+
+
+def assemble_kernel(chunks, half, folds, head_width, model_width, *refs):
     parts, refs = take(refs, 4 * chunks)
-    pairs, (gate_ref, up_ref, down_ref, *outs) = take(refs, 4)
+    pairs, refs = take(refs, 6)
+    small_ref, gate_ref, up_ref, down_ref, *outs, ga_ref, gm_ref, rest_ref = refs
     first = lax.rem(lax.axis_index("rep"), 2) == 0
 
     def sides(mine, other):
@@ -1337,12 +1388,34 @@
                 down_ref[chunk * folds + fold, :, side * columns : (side + 1) * columns] = values[
                     :, fold * columns : (fold + 1) * columns
                 ].astype(F32)
-    columns = [pairs[0].shape[1], widths[0], widths[1], widths[1]]
-    starts = [0, 0, widths[0], widths[0] + widths[1]]
-    for ref, width, start, k in zip(outs, columns, starts, (0, 2, 2, 2)):
+    starts = [0, 0, 0, outs[2].shape[1] // 2]
+    for ref, k, start in zip(outs, (0, 2, 4, 4), starts):
+        width = ref.shape[1] // 2
         mine, other = (one[:, start : start + width] for one in pairs[k : k + 2])
         for side, values in enumerate(sides(mine, other)):
             ref[:, side * width : (side + 1) * width] = values.astype(F32)
+
+    @pl.when(pl.program_id(0) == 0)
+    def _():
+        me = lax.axis_index("shard")
+        width = ga_ref.shape[1]
+        here = pl.ds(pl.multiple_of(me * width, width), width)
+        ga_ref[...] = small_ref[0:1, here]
+        gm_ref[...] = small_ref[1:2, here]
+        rest_ref[...] = jnp.zeros(rest_ref.shape, F32)
+        lane = lax.broadcasted_iota(jnp.int32, (1, LANES), 1)
+        count = small_ref[7:8, 0:1] * model_width
+        roots = jnp.zeros((1, LANES), F32)
+        for k in range(3):
+            total = jnp.sum(small_ref[2 + k : 3 + k, :], axis=1, keepdims=True)
+            roots = jnp.where(lane == k, jnp.sqrt(total / count), roots)
+        rest_ref[0:1, :] = roots
+        size = head_width * width // model_width
+        for k in range(2):
+            gains = jnp.broadcast_to(small_ref[5 + k : 6 + k, :LANES], (8, LANES))
+            gains += pltpu.roll(gains, head_width, 1)
+            gains = pltpu.roll(gains, lax.rem(LANES - me * size, LANES), 1)
+            rest_ref[1 + k : 2 + k, :] = gains[0:1, :]
 
 
 class Rows:
@@ -1385,7 +1458,7 @@
             cost_estimate=pl.CostEstimate(
                 flops=flops, bytes_accessed=1 << 24, transcendentals=0
             ),
-            compiler_params=pltpu.CompilerParams(vmem_limit_bytes=60 << 20),
+            compiler_params=pltpu.CompilerParams(vmem_limit_bytes=62 << 20),
             name=name,
         )(self.lens, *args)
 
@@ -1461,7 +1534,7 @@
             in_specs=[hbm] * 3,
             out_specs=[vmem] * 2,
             scratch_shapes=[pltpu.SemaphoreType.DMA((chunks * (2 * half_shards + folds),))],
-            compiler_params=pltpu.CompilerParams(vmem_limit_bytes=32 << 20),
+            compiler_params=pltpu.CompilerParams(vmem_limit_bytes=62 << 20),
             name="pack",
         )(w_gate, w_up, w_down)
     else:
@@ -1587,16 +1660,10 @@
             flops=2 * full * q_half * width_all, bytes_accessed=1 << 24, transcendentals=0
         ),
         compiler_params=pltpu.CompilerParams(
-            collective_id=6, has_side_effects=True, vmem_limit_bytes=40 << 20
+            collective_id=6, has_side_effects=True, vmem_limit_bytes=62 << 20
         ),
         name="out",
     )(lengths, attended, w_o, x_own, gain_m)
-
-    def across(grad_rows):
-        half = grad_rows.shape[1] // 2
-        mine = lax.dynamic_slice_in_dim(grad_rows, core * half, half, axis=1)
-        other = core_swap(lax.dynamic_slice_in_dim(grad_rows, (1 - core) * half, half, axis=1))
-        return ordered(mine, other, 0)
 
     sums = []
     ff_grads, ff_levels, ff_totals = [], [], []
@@ -1666,20 +1733,30 @@
         ff_totals += rest[1:]
     output, d_resid, d_attn, sums_b, d_attn_other = sums
 
-    d_heads, grad_out = over.call(
-        "dout",
-        partial(dout_kernel, over.per_slot, head_width),
-        2,
-        [over.early(width_all), over.late(width_all), over.both(q_half), over.fixed(w_o.shape)],
-        [over.both(2 * q_half), over.fixed(w_o.shape)],
-        [((full, 2 * q_half), LOW), (w_o.shape, LOW)],
-        [pltpu.VMEM(w_o.shape, F32)],
-        4 * full * q_half * width_all,
-        d_attn, d_attn_other, attended, w_o,
-    )
-    grad_out = across(grad_out)
+    o_shape = w_o.shape
+    d_heads, grad_out = pl.pallas_call(
+        partial(dout_kernel, n, head_width),
+        out_shape=[
+            jax.ShapeDtypeStruct((full, 2 * q_half), LOW),
+            jax.ShapeDtypeStruct((2 * o_shape[0], d_half), LOW),
+        ],
+        grid=(2 * n,),
+        in_specs=[first_rows, last_rows, pl.BlockSpec((block, q_half), lambda i: (i, 0))]
+        + [held(o_shape)],
+        out_specs=[pl.BlockSpec((block, 2 * q_half), lambda i: (i, 0)), hbm],
+        scratch_shapes=[pltpu.VMEM(o_shape, F32), pltpu.VMEM((o_shape[0], d_half), LOW)]
+        + [pltpu.VMEM((2 * o_shape[0], d_half), LOW)]
+        + [pltpu.SemaphoreType.DMA((1,))] * 3,
+        cost_estimate=pl.CostEstimate(
+            flops=4 * full * q_half * width_all, bytes_accessed=1 << 24, transcendentals=0
+        ),
+        compiler_params=pltpu.CompilerParams(
+            collective_id=8, has_side_effects=True, vmem_limit_bytes=62 << 20
+        ),
+        name="dout",
+    )(d_attn, d_attn_other, attended, w_o)
     o_level = (d_rows, d_half)
-    d_query, d_key, d_value, ff_level, out_level, ff_total = attend_back(
+    d_query, d_key, d_value, ff_level, ff_total = attend_back(
         queries,
         keys,
         values,
@@ -1687,37 +1764,41 @@
         rows,
         head_width,
         block,
-        Side(shards, groups, [level_shape, o_level], [level_shape]),
-        [ff_grads[-1], grad_out, ff_levels[-1]],
+        Side(shards, groups, [level_shape], [level_shape]),
+        [ff_grads[-1], ff_levels[-1]],
     )
     ff_totals.append(ff_total)
+    top_shape = (d_rows, 2 * units)
+    side = Side(shards, groups, [o_level], [top_shape], n)
     turned = pl.BlockSpec((block, LANES), lambda i: (lax.rem(i, n), 0))
-    input_grad, grad_qkv, gain_sums, sums_c = pl.pallas_call(
-        partial(qkv_back_kernel, n, counts, head_width, scale),
+    input_grad, grad_qkv, gain_sums, sums_c, out_level, ff_top = pl.pallas_call(
+        partial(qkv_back_kernel, n, counts, head_width, scale, side),
         out_shape=[
             jax.ShapeDtypeStruct((rows, width_all), LOW),
             jax.ShapeDtypeStruct(w_qkv.shape, LOW),
             jax.ShapeDtypeStruct((8, LANES), F32),
             jax.ShapeDtypeStruct(eight, F32),
-        ],
+        ]
+        + side.outs(),
         grid=(2 * n,),
         in_specs=[other_first(q_half), other_first(2 * kv_half), other_first(2 * kv_half)]
         + [other_first(qk), other_first(width_all), held(w_qkv.shape), held(gain_h.shape)]
-        + [turned, turned, last_rows, last_rows, held(gain_a.shape)],
+        + [turned, turned, last_rows, last_rows, held(gain_a.shape), hbm, hbm],
         out_specs=[last_rows, held(w_qkv.shape)]
-        + [pl.BlockSpec((8, LANES), lambda i: (0, 0)), sums_spec],
+        + [pl.BlockSpec((8, LANES), lambda i: (0, 0)), sums_spec, hbm, hbm],
         scratch_shapes=[pltpu.VMEM(w_qkv.shape, F32), pltpu.VMEM((block, total), LOW)]
         + [pltpu.VMEM((2 * block, width_all), LOW), slot_rows]
-        + [pltpu.SemaphoreType.DMA((n,))] * 2,
+        + side.scratch(),
         cost_estimate=pl.CostEstimate(
             flops=4 * full * width_all * total, bytes_accessed=1 << 24, transcendentals=0
         ),
         compiler_params=pltpu.CompilerParams(
-            collective_id=7, has_side_effects=True, vmem_limit_bytes=48 << 20
+            collective_id=7, has_side_effects=True, vmem_limit_bytes=62 << 20
         ),
         name="qkv_back",
     )(
-        d_query, d_key, d_value, raw, normed_a, w_qkv, gain_h, cosine, sine, x_own, d_resid, gain_a
+        d_query, d_key, d_value, raw, normed_a, w_qkv, gain_h, cosine, sine, x_own, d_resid, gain_a,
+        grad_out, ff_level,
     )
     mine, other, small = finish_sums(
         grad_qkv,
@@ -1725,67 +1806,66 @@
         [sums_a, sums_b, sums_c, gain_sums],
         [(2, 0), (1, 1), (0, 0), (0, 1), (1, 0), (3, 0), (3, 1)],
         [ff_level, out_level],
-        ff_totals,
+        d_rows,
+        ff_totals + [ff_top],
         shards,
         groups,
     )
-    total_ga, total_gm = small[0], small[1]
-    total_gh = small[5:7, :LANES].reshape(2, -1, head_width).sum(1)
-    totals = jnp.concatenate([small[2:5].sum(1), small[7, :1]])
-    statistics = jnp.sqrt(totals[:3] / (totals[3] * width_all))
-    me = lax.axis_index("shard")
-
-    def own_piece(vector):
-        size = vector.shape[0] // shards
-        return lax.dynamic_slice_in_dim(vector, me * size, size)
-
-    ff_mine = ff_totals + [mine[0]]
-    ff_other = list(other[3:]) + [other[0]]
-
     wide = (d_rows, shards * ff_rows)
     shapes = [wide, wide, (chunks * folds, piece // folds, width_all)]
     shapes += [w.shape for w in (w_out, w_query, w_key, w_value)]
+    shapes += [(1, d_rows), (1, d_rows), (8, LANES)]
     top = d_rows // 8
     low_rows = piece // folds // 8
 
-    def blocks(part):
-        return [
-            pl.BlockSpec((top, part.shape[1]), lambda i: (i, 0)),
-            pl.BlockSpec((low_rows, part.shape[1]), lambda i: (8 * top // low_rows + i, 0)),
-        ]
-
     def whole(part):
         return pl.BlockSpec((top, part.shape[1]), lambda i: (i, 0))
 
-    parts = [one for pair in zip(ff_mine, ff_other) for one in pair for _ in range(2)]
-    specs = [one for pair in zip(ff_mine, ff_other) for part in pair for one in blocks(part)]
-    pairs = [mine[1], other[1], mine[2], other[2]]
-    grad_gate, grad_up, grad_down, grad_out, grad_query, grad_key, grad_value = pl.pallas_call(
-        partial(assemble_kernel, chunks, half_shards, folds, (q_half, kv_half)),
+    def low(part, skip):
+        return pl.BlockSpec((low_rows, part.shape[1]), lambda i: (skip // low_rows + i, 0))
+
+    parts, specs = [], []
+    for chunk in range(chunks):
+        for total, rest in (
+            (ff_totals[chunk], ff_totals[chunk]) if chunk < chunks - 1 else (ff_top, mine[0]),
+            (other[4 + chunk], other[4 + chunk]) if chunk < chunks - 1 else (other[-1], other[0]),
+        ):
+            parts += [total, rest]
+            specs += [whole(total), low(rest, d_rows if chunk < chunks - 1 else 0)]
+    pairs = [one for pair in zip(mine[1:4], other[1:4]) for one in pair]
+    small_specs = [pl.BlockSpec(shape, lambda i: (0, 0)) for shape in shapes[7:]]
+    (
+        grad_gate, grad_up, grad_down, grad_out, grad_query, grad_key, grad_value,
+        grad_ga, grad_gm, rest,
+    ) = pl.pallas_call(
+        partial(assemble_kernel, chunks, half_shards, folds, head_width, width_all),
         out_shape=[jax.ShapeDtypeStruct(shape, F32) for shape in shapes],
         grid=(8,),
-        in_specs=specs + [whole(part) for part in pairs],
+        in_specs=specs
+        + [whole(part) for part in pairs]
+        + [pl.BlockSpec(small.shape, lambda i: (0, 0))],
         out_specs=[pl.BlockSpec((top, shape[1]), lambda i: (i, 0)) for shape in shapes[:2]]
         + [pl.BlockSpec((shapes[2][0], low_rows, width_all), lambda i: (0, i, 0))]
-        + [pl.BlockSpec((top, shape[1]), lambda i: (i, 0)) for shape in shapes[3:]],
-        compiler_params=pltpu.CompilerParams(vmem_limit_bytes=48 << 20),
+        + [pl.BlockSpec((top, shape[1]), lambda i: (i, 0)) for shape in shapes[3:7]]
+        + small_specs,
+        compiler_params=pltpu.CompilerParams(vmem_limit_bytes=62 << 20),
         name="assemble",
-    )(*parts, *pairs)
+    )(*parts, *pairs, small)
     return (
         output[None],
         input_grad[None],
-        own_piece(total_ga),
+        grad_ga.reshape(-1),
         grad_query,
         grad_key,
         grad_value,
-        own_piece(total_gh[0]),
-        own_piece(total_gh[1]),
+        rest[1, :head_rows],
+        rest[2, :head_rows],
         grad_out,
-        own_piece(total_gm),
+        grad_gm.reshape(-1),
         grad_gate,
         grad_up,
         grad_down.reshape(w_down.shape),
-        statistics,
+        rest[0, :3],
     )
 
 

time: 526 us -> 492 us (0.935)
  local copies, waits for them, and re-layouts: 34.8 us -> 11.9 us
  Pallas kernels: 455 us -> 448 us
    pallas_call x2 -> x3, Pallas kernels: 33.5 us -> 68.8 us  [the longest x1 39.2 us: local(): pl.pallas_call(partial(qkv_back_kernel, n, counts, head_width, scale, sid...]
    pallas_call x1, Pallas kernels: 74.1 us -> 50.9 us  [finish_sums(): pl.pallas_call(partial(finish_kernel, shards, groups, (len(lows), len(rea...]
    unnamed x68 -> x14, local copies, waits for them, and re-layouts: 25 us -> 4.86 us
    pallas_call x2 -> x1, Pallas kernels: 36.5 us -> 17 us  [call(): pl.pallas_call(kernel, out_shape=[jax.ShapeDtypeStruct(shape, kind) for s...]
    pallas_call x1, Pallas kernels: 25.4 us -> 16.7 us  [attend(): pl.pallas_call(partial(attend_kernel, block, width), out_shape=(jax.Shape...]
    pallas_call x3, Pallas kernels: 157 us -> 165 us  [local(): pl.pallas_call(partial(ffn_kernel, n, shards, bool(sums), last, side, 0 i...]
  transfers between devices with their start and end apart: 5 -> 4, of which waited for: 1 -> 1; matrix products, arithmetic and copies ran while one was open for 2% -> 2% of each run, Pallas kernels for 41% -> 43%
where the time goes in v2:
time: 492 us; the launch traced here: 485 us
  Pallas kernels  448 us (91%)
  between operations  15.1 us (3%)
  local copies, waits for them, and re-layouts  11.9 us (2%)
  other arithmetic  5.27 us (1%)
    pallas_call x3, Pallas kernels, local(): pl.pallas_call(partial(ffn_kernel, n, shards, bool(sums), last, side, 0 i...  165 us
    pallas_call x1, Pallas kernels, attend_back(): pl.pallas_call(partial(attend_back_kernel, block, width, side), out_shape...  56 us
    pallas_call x1, Pallas kernels, local(): pl.pallas_call(partial(gather_kernel, shards, wide_parts, tall_parts, (6,...  54.8 us
    pallas_call x1, Pallas kernels, finish_sums(): pl.pallas_call(partial(finish_kernel, shards, groups, (len(lows), len(rea...  50.9 us
    pallas_call x1, Pallas kernels, local(): pl.pallas_call(partial(qkv_back_kernel, n, counts, head_width, scale, sid...  39.2 us
    pallas_call x1, Pallas kernels, local(): pl.pallas_call(partial(dout_kernel, n, head_width), out_shape=[jax.ShapeD...  18.9 us
    pallas_call x1, Pallas kernels, call(): pl.pallas_call(kernel, out_shape=[jax.ShapeDtypeStruct(shape, kind) for s...  17 us
    pallas_call x1, Pallas kernels, attend(): pl.pallas_call(partial(attend_kernel, block, width), out_shape=(jax.Shape...  16.7 us
  transfers between devices with their start and end apart: 4, of which 1 were waited for; matrix products, arithmetic and copies ran while one was open for 2% of the time, Pallas kernels for 43%

profile of v2, /device:TPU:0, one launch (start us, length us, event | category | flops | bytes accessed | tf_op | source)
XLA Modules:
  0.0 485.2 jit_solution(7017511150321307921)
XLA Ops:
  7.2 0.0 all-gather.7.cloned.1.call-start
  7.2 4.0 pack.1
  11.2 0.0 copy-start
  11.3 0.0 all-gather.7.cloned.1.call-update
  11.3 0.0 all-gather.5.cloned.1.call-start
  11.3 0.5 collective-permute-start
  12.5 0.3 copy-done
  12.9 1.6 bitcast_select_fusion.g_own
  14.4 0.5 collective-permute-start.1
  14.9 0.0 copy-done.2
  14.9 0.0 copy-done.3
  14.9 0.1 fusion.10
  15.0 0.0 copy-done.4
  15.0 0.0 copy-done.5
  15.0 0.6 fusion.7.refs_4_
  15.6 54.8 %gather.1 = (bf16[1024,1024]{1,0:T(8,128)(2,1)}, bf16[512,1024]{1,0:T(8,128)(2,1)}, bf16[4,16,256]{2,1,0:T(8,128)(2,1)}, bf16[1024,1024]{1,0:T(8,128)(2,1)}) custom-call(bf16[256,1024]{1,0:T(8,128)(2,1)} %refs_0_.3, bf16[256,512]{1,0:T(8,128)(2,1)} %refs_1_.3, bf16[256,512]{1,0:T(8,128)(2,1)} %refs_2_.4, bf16[256,1024]{1,0:T(8,128)(2,1)} %refs_3_.1, ...), custom_call_target="tpu_custom_call" | custom-call | tf_op jit(solution)/shard_map/gather/pallas_call | solution.py:1579
  70.4 0.9 slice_reduce_fusion.1
  71.3 0.1 convert_element_type.40
  71.4 0.1 convert_element_type.41
  71.5 0.7 tile.32.gh_ref
  72.1 0.8 fusion.11
  72.9 0.6 convert.5.ga_ref
  73.6 0.6 fusion.2
  74.2 1.0 copy.29.sin_ref
  75.2 1.0 copy.28.cos_ref
  76.2 0.0 collective-permute-done
  76.2 1.2 pad_add_fusion.lens_ref
  77.5 17.0 %qkv.1 = (bf16[2048,1024]{1,0:T(8,128)(2,1)}, f32[2048,768]{1,0:T(8,128)}, bf16[2048,1024]{1,0:T(8,128)(2,1)}, bf16[2048,512]{1,0:T(8,128)(2,1)}, bf16[2048,512]{1,0:T(8,128)(2,1)}) custom-call(s32[2]{0:T(128)} %pad_add_fusion.lens_ref, bf16[1024,1024]{1,0:T(8,128)(2,1)} %bitcast.25, bf16[1024,1024]{1,0:T(8,128)(2,1)} %get-tuple-element.84.other_ref, ...), custom_call_target="tpu_custom_call" | custom-call | flops 4294967296 | bytes 16777216 | tf_op jit(solution)/shard_map/qkv/pallas_call | solution.py:1448
  94.4 16.7 %attend.1 = (bf16[2048,512]{1,0:T(8,128)(2,1)}, bf16[2048,1024]{1,0:T(8,128)(2,1)}) custom-call(s32[2]{0:T(128)} %pad_add_fusion.lens_ref, bf16[2048,1024]{1,0:T(8,128)(2,1)} %get-tuple-element.87.q_ref, bf16[2048,512]{1,0:T(8,128)(2,1)} %get-tuple-element.88.k_ref, bf16[2048,512]{1,0:T(8,128)(2,1)} %get-tuple-element.89.v_ref), custom_call_target="tpu_custom_call" | custom-call | flops 8589934592 | bytes 8388608 | tf_op jit(solution)/shard_map/attend/pallas_call | solution.py:898
  111.1 0.0 all-gather.5.cloned.1.call-update
  111.2 0.6 convert.6.gain_ref.refs_4_
  111.8 15.1 %out.1 = (f32[1024,1024]{1,0:T(8,128)}, bf16[1024,1024]{1,0:T(8,128)(2,1)}, f32[8,1024]{1,0:T(8,128)}, bf16[1024,1024]{1,0:T(8,128)(2,1)}) custom-call(s32[1]{0:T(128)} %copy.34.length_ref.refs_2_, bf16[2048,512]{1,0:T(8,128)(2,1)} %get-tuple-element.91.att_ref, bf16[512,1024]{1,0:T(8,128)(2,1)} %get-tuple-element.92.w_ref, bf16[1024,1024]{1,0:T(8,128)(2,1)} %bitcast.26, ...), custom_call_target="tpu_custom_call" | custom-call | flops 2147483648 | bytes 16777216 | tf_op jit(solution)/shard_map/out/pallas_call | solution.py:1645
  126.8 0.0 collective-permute-done.1.g_other
  126.8 3.9 all-gather.7.cloned.1.call-done
  130.7 56.2 %ffn.3 = (f32[2048,1024]{1,0:T(8,128)}, f32[2048,1024]{1,0:T(8,128)}, bf16[1536,1536]{1,0:T(8,128)(2,1)}) custom-call(bf16[1024,1024]{1,0:T(8,128)(2,1)} %get-tuple-element.93.x_own, bf16[1024,1024]{1,0:T(8,128)(2,1)} %get-tuple-element.94.x_other, bf16[1024,1024]{1,0:T(8,128)(2,1)} %bitcast_select_fusion.g_own, ...), custom_call_target="tpu_custom_call" | custom-call | flops 28991029248 | bytes 33554432 | tf_op jit(solution)/shard_map/ffn/pallas_call | solution.py:1702
  186.9 49.8 %ffn.4 = (f32[2048,1024]{1,0:T(8,128)}, f32[2048,1024]{1,0:T(8,128)}, bf16[1536,1536]{1,0:T(8,128)(2,1)}, bf16[384,1536]{1,0:T(8,128)(2,1)}) custom-call(bf16[1024,1024]{1,0:T(8,128)(2,1)} %get-tuple-element.93.x_own, bf16[1024,1024]{1,0:T(8,128)(2,1)} %get-tuple-element.94.x_other, bf16[1024,1024]{1,0:T(8,128)(2,1)} %bitcast_select_fusion.g_own, ...), custom_call_target="tpu_custom_call" | custom-call | flops 28991029248 | bytes 33554432 | tf_op jit(solution)/shard_map/ffn/pallas_call | solution.py:1702
  236.7 0.0 all-gather.5.cloned.1.call-done
  236.7 58.7 %ffn.5 = (bf16[1024,1024]{1,0:T(8,128)(2,1)}, f32[1024,1024]{1,0:T(8,128)}, bf16[1024,1024]{1,0:T(8,128)(2,1)}, f32[8,1024]{1,0:T(8,128)}, bf16[1024,1024]{1,0:T...) custom-call(bf16[1024,1024]{1,0:T(8,128)(2,1)} %get-tuple-element.93.x_own, ...), custom_call_target="tpu_custom_call" | custom-call | flops 28991029248 | bytes 33554432 | tf_op jit(solution)/shard_map/ffn/pallas_call | solution.py:1702
  295.5 18.9 %dout.1 = (bf16[2048,1024]{1,0:T(8,128)(2,1)}, bf16[1024,512]{1,0:T(8,128)(2,1)}) custom-call(bf16[1024,1024]{1,0:T(8,128)(2,1)} %get-tuple-element.107.own_ref, bf16[1024,1024]{1,0:T(8,128)(2,1)} %get-tuple-element.108.other_ref, bf16[2048,512]{1,0:T(8,128)(2,1)} %get-tuple-element.91.att_ref, bf16[512,1024]{1,0:T(8,128)(2,1)} %get-tuple-element.92.w_ref), custom_call_target="tpu_custom_call" | custom-call | flops 4294967296 | bytes 16777216 | tf_op jit(solution)/shard_map/dout/pallas_call | solution.py:1737
  314.3 56.0 %attend_back.1 = (f32[2048,512]{1,0:T(8,128)}, f32[2048,512]{1,0:T(8,128)}, f32[2048,512]{1,0:T(8,128)}, bf16[384,1536]{1,0:T(8,128)(2,1)}, bf16[384,1536]{1,0:T(8,128)(2,1)}) custom-call(bf16[2048,1024]{1,0:T(8,128)(2,1)} %get-tuple-element.106.q_ref, bf16[2048,512]{1,0:T(8,128)(2,1)} %get-tuple-element.88.k_ref, ...), custom_call_target="tpu_custom_call" | custom-call | flops 21474836480 | bytes 16777216 | tf_op jit(solution)/shard_map/attend_back/pallas_call | solution.py:922
  370.3 39.2 %qkv_back.1 = (bf16[1024,1024]{1,0:T(8,128)(2,1)}, bf16[1024,1024]{1,0:T(8,128)(2,1)}, f32[8,128]{1,0:T(8,128)}, f32[8,1024]{1,0:T(8,128)}, bf16[256,512]{1,0:T(8,128)(2,1)}, /*index=5*/bf16[256,1536]{1,0:T(8,128)(2,1)}) custom-call(f32[2048,512]{1,0:T(8,128)} %get-tuple-element.112.dq_ref, f32[2048,512]{1,0:T(8,128)} %get-tuple-element.113.dk_ref, ...), custom_call_target="tpu_custom_call" | custom-call | flops 8589934592 | bytes 16777216 | tf_op jit(solution)/shard_map/qkv_back/pallas_call | solution.py:1774
  409.5 50.9 %finish.1 = (bf16[128,1536]{1,0:T(8,128)(2,1)}, bf16[256,512]{1,0:T(8,128)(2,1)}, bf16[256,512]{1,0:T(8,128)(2,1)}, bf16[256,512]{1,0:T(8,128)(2,1)}, bf16[128,1...) custom-call(s32[1]{0:T(128)} %copy.34.length_ref.refs_2_, ...), custom_call_target="tpu_custom_call" | custom-call | tf_op jit(solution)/shard_map/finish/pallas_call | solution.py:774
  460.4 10.7 %assemble.1 = (f32[256,4608]{1,0:T(8,128)}, f32[256,4608]{1,0:T(8,128)}, f32[9,128,1024]{2,1,0:T(8,128)}, f32[256,1024]{1,0:T(8,128)}, f32[256,1024]{1,0:T(8,128...) custom-call(bf16[384,1536]{1,0:T(8,128)(2,1)} %get-tuple-element.121, ...), custom_call_target="tpu_custom_call" | custom-call | tf_op jit(solution)/shard_map/assemble/pallas_call | solution.py:1840
  471.1 1.3 slice_bitcast_fusion.1
  472.4 1.2 slice_bitcast_fusion
  473.6 3.2 copy.35
  476.9 0.0 copy-done.1
  476.9 1.3 copy.36
  (15 shorter events, 0.2 us)
Async XLA Ops:
  7.2 123.6 %all-gather.7.cloned.1.call-start = ((), (), s32[]{:S(2)}) async-start(), calls=%async_computation.1 | async-start | bytes 11796480 | tf_op jit(solution)/shard_map/all_gather | solution.py:1556
  11.2 1.6 copy-start
  11.3 225.4 %all-gather.5.cloned.1.call-start = ((), (), s32[]{:S(2)}) async-start(), calls=%async_computation | async-start | bytes 5898240 | tf_op jit(solution)/shard_map/all_gather | solution.py:1629
  11.3 64.9 %collective-permute-start = (s32[1]{0:T(128)}, s32[1]{0:T(128)}, u32[]{:S(2)}, u32[]{:S(2)}) collective-permute-start(s32[1]{0:T(128)} %param.15), channel_id=1, source_target_pairs={{0,4},{4,0},{8,12},{12,8},{16,20},{20,16},{24,28},{28,24},{1,5},{5... | collective-permute-start | bytes 20 | tf_op jit(solution)/shard_map/ppermute | solution.py:46
  12.8 2.1 copy-start.2
  12.8 2.1 copy-start.3
  12.8 2.1 copy-start.4
  12.8 2.1 copy-start.5
  14.4 112.4 %collective-permute-start.1 = (bf16[1024,1024]{1,0:T(8,128)(2,1)}, bf16[1024,1024]{1,0:T(8,128)(2,1)}, u32[]{:S(2)}, u32[]{:S(2)}) collective-permute-start(bf16[1024,1024]{1,0:T(8,128)(2,1)} %bitcast_select_fusion.g_own), channel_id=1, source_target_pairs={{0,4},{4,0},{8,12},{12,8},{16,20},{20,16},{24,28},{28,24},{1,5},{5... | collective-permute-start | bytes 6291464 | tf_op jit(solution)/shard_map/ppermute | solution.py:46
  473.6 3.2 copy-start.1
Sparse Core Ops, SparseCore 0:
  11.4 119.2 all-gather.6
  132.6 57.0 all-gather.4

commit v3 on v2

--- a/solution.py
+++ b/solution.py
@@ -542,16 +542,14 @@
             for stages in planes:
                 stages[2]()
 
-        plan = {
-            0: [begin],
-            1: [load_done, of_lines(0, 1)],
-            2: [of_lines(1, 1)],
-            3: [of_lines(2, 1), of_lines(3, 1), merge, of_lines(0, 2), of_lines(1, 2)],
-            4: [of_lines(4, 1), of_lines(2, 2), of_lines(3, 2)],
-            5: [of_lines(5, 1), of_lines(6, 1), of_lines(4, 2)],
-            6: [of_lines(7, 1), of_lines(5, 2), of_lines(6, 2)],
-            7: [of_lines(7, 2)],
-        }
+        received = {1: [0], 2: [1], 3: [2, 3], 4: [4], 5: [5, 6], 6: [7]}
+        given = {3: [0, 1], 4: [2, 3], 5: [4], 6: [5, 6], 7: [7]}
+        plan = {0: [begin]}
+        for when in range(1, 8):
+            plan[when] = [load_done] if when == 1 else []
+            plan[when] += [of_lines(part, 1) for part in received.get(when, [])]
+            plan[when] += [merge] if when == 3 else []
+            plan[when] += [of_lines(part, 2) for part in given.get(when, [])]
         for when, stages in plan.items():
 
             @pl.when(step == when)
@@ -797,6 +795,10 @@
     return high, (column - high.astype(F32)).astype(LOW)
 
 
+def below(ref, here, heads):
+    return jnp.concatenate([ref[here, pl.ds(h * LANES, LANES)] for h in range(heads)], axis=0)
+
+
 def attend_kernel(block, width, lens_ref, q_ref, k_ref, v_ref, att_ref, qx_ref):
     rows = q_ref.shape[0]
     heads = q_ref.shape[1] // LANES
@@ -848,37 +850,35 @@
     rows = q_ref.shape[0]
     heads = q_ref.shape[1] // LANES
     lane = lax.broadcasted_iota(jnp.int32, (block, LANES), 1)
-    keep = lax.broadcasted_iota(jnp.int32, (block, block), 0) <= lax.broadcasted_iota(
-        jnp.int32, (block, block), 1
+    shape = (block, heads * block)
+    keep = lax.broadcasted_iota(jnp.int32, shape, 0) <= lax.rem(
+        lax.broadcasted_iota(jnp.int32, shape, 1), block
     )
     dk_ref[...] = jnp.zeros(dk_ref.shape, F32)
     dv_ref[...] = jnp.zeros(dv_ref.shape, F32)
     for step in range(rows // block):
         start = step * block
         here = pl.ds(start, block)
-        parts = []
-        for head in range(heads):
-            lanes = pl.ds(head * LANES, LANES)
-            query = q_ref[here, lanes]
-            dout = do_ref[here, lanes]
-
-            def one(keys, masked):
-                key, value = k_ref[keys, :], v_ref[keys, :]
-                probs = jnp.exp(nt(key, query))
-                if masked:
-                    probs = jnp.where(keep, probs, 0.0)
-                dscores = (probs * nt(value, dout)).astype(LOW)
-                dv_ref[keys, :] += nn(probs.astype(LOW), dout)
-                dk_ref[keys, :] += nn(dscores, query)
-                return tn(dscores, key)
-
-            dquery = one(here, True)
-            if step:
-                dquery += one(pl.ds(0, start), False)
-            parts.append(dquery)
+        query, dout = below(q_ref, here, heads), below(do_ref, here, heads)
+
+        def one(keys, masked):
+            key, value = k_ref[keys, :], v_ref[keys, :]
+            probs = jnp.exp(nt(key, query))
+            if masked:
+                probs = jnp.where(keep, probs, 0.0)
+            dscores = (probs * nt(value, dout)).astype(LOW)
+            dv_ref[keys, :] += nn(probs.astype(LOW), dout)
+            dk_ref[keys, :] += nn(dscores, query)
+            return tn(dscores, key)
+
+        dquery = one(here, True)
+        if step:
+            dquery += one(pl.ds(0, start), False)
         for pair in range(heads // 2):
+            first = dquery[2 * pair * block : (2 * pair + 1) * block]
+            second = dquery[(2 * pair + 1) * block : (2 * pair + 2) * block]
             dq_ref[here, pl.ds(pair * LANES, LANES)] = jnp.where(
-                lane < width, parts[2 * pair], pltpu.roll(parts[2 * pair + 1], width, 1)
+                lane < width, first, pltpu.roll(second, width, 1)
             )
     pl.when(grid_step == pl.num_programs(0) * pl.num_programs(1) - 1)(end)
 
@@ -1366,7 +1366,7 @@
 def assemble_kernel(chunks, half, folds, head_width, model_width, *refs):
     parts, refs = take(refs, 4 * chunks)
     pairs, refs = take(refs, 6)
-    small_ref, gate_ref, up_ref, down_ref, *outs, ga_ref, gm_ref, rest_ref = refs
+    small_ref, gate_ref, up_ref, down_ref, *outs, ga_ref, gm_ref, stat_ref, gq_ref, gk_ref = refs
     first = lax.rem(lax.axis_index("rep"), 2) == 0
 
     def sides(mine, other):
@@ -1402,20 +1402,19 @@
         here = pl.ds(pl.multiple_of(me * width, width), width)
         ga_ref[...] = small_ref[0:1, here]
         gm_ref[...] = small_ref[1:2, here]
-        rest_ref[...] = jnp.zeros(rest_ref.shape, F32)
         lane = lax.broadcasted_iota(jnp.int32, (1, LANES), 1)
         count = small_ref[7:8, 0:1] * model_width
         roots = jnp.zeros((1, LANES), F32)
         for k in range(3):
             total = jnp.sum(small_ref[2 + k : 3 + k, :], axis=1, keepdims=True)
             roots = jnp.where(lane == k, jnp.sqrt(total / count), roots)
-        rest_ref[0:1, :] = roots
-        size = head_width * width // model_width
-        for k in range(2):
+        stat_ref[...] = roots[:, : stat_ref.shape[1]]
+        size = gq_ref.shape[1]
+        for k, ref in enumerate((gq_ref, gk_ref)):
             gains = jnp.broadcast_to(small_ref[5 + k : 6 + k, :LANES], (8, LANES))
             gains += pltpu.roll(gains, head_width, 1)
             gains = pltpu.roll(gains, lax.rem(LANES - me * size, LANES), 1)
-            rest_ref[1 + k : 2 + k, :] = gains[0:1, :]
+            ref[...] = gains[0:1, :size]
 
 
 class Rows:
@@ -1814,7 +1813,7 @@
     wide = (d_rows, shards * ff_rows)
     shapes = [wide, wide, (chunks * folds, piece // folds, width_all)]
     shapes += [w.shape for w in (w_out, w_query, w_key, w_value)]
-    shapes += [(1, d_rows), (1, d_rows), (8, LANES)]
+    shapes += [(1, d_rows), (1, d_rows), (1, 3), (1, head_rows), (1, head_rows)]
     top = d_rows // 8
     low_rows = piece // folds // 8
 
@@ -1836,7 +1835,7 @@
     small_specs = [pl.BlockSpec(shape, lambda i: (0, 0)) for shape in shapes[7:]]
     (
         grad_gate, grad_up, grad_down, grad_out, grad_query, grad_key, grad_value,
-        grad_ga, grad_gm, rest,
+        grad_ga, grad_gm, statistics, grad_gq, grad_gk,
     ) = pl.pallas_call(
         partial(assemble_kernel, chunks, half_shards, folds, head_width, width_all),
         out_shape=[jax.ShapeDtypeStruct(shape, F32) for shape in shapes],
@@ -1858,14 +1857,14 @@
         grad_query,
         grad_key,
         grad_value,
-        rest[1, :head_rows],
-        rest[2, :head_rows],
+        grad_gq.reshape(-1),
+        grad_gk.reshape(-1),
         grad_out,
         grad_gm.reshape(-1),
         grad_gate,
         grad_up,
         grad_down.reshape(w_down.shape),
-        rest[0, :3],
+        statistics.reshape(-1),
     )
 
 

time: 492 us -> 483 us (0.982)
  Pallas kernels: 448 us -> 437 us
where the time goes in v3:
time: 483 us; the launch traced here: 474 us
  Pallas kernels  437 us (90%)
  between operations  15.1 us (3%)
  local copies, waits for them, and re-layouts  9.47 us (2%)
  waiting for transfers between devices  5.53 us (1%)
  other arithmetic  5.26 us (1%)
    pallas_call x3, Pallas kernels, local(): pl.pallas_call(partial(ffn_kernel, n, shards, bool(sums), last, side, 0 i...  161 us
    pallas_call x1, Pallas kernels, local(): pl.pallas_call(partial(gather_kernel, shards, wide_parts, tall_parts, (6,...  54.8 us
    pallas_call x1, Pallas kernels, attend_back(): pl.pallas_call(partial(attend_back_kernel, block, width, side), out_shape...  53.1 us
    pallas_call x1, Pallas kernels, finish_sums(): pl.pallas_call(partial(finish_kernel, shards, groups, (len(lows), len(rea...  49.1 us
    pallas_call x1, Pallas kernels, local(): pl.pallas_call(partial(qkv_back_kernel, n, counts, head_width, scale, sid...  38.4 us
    pallas_call x1, Pallas kernels, local(): pl.pallas_call(partial(dout_kernel, n, head_width), out_shape=[jax.ShapeD...  18.9 us
    pallas_call x1, Pallas kernels, call(): pl.pallas_call(kernel, out_shape=[jax.ShapeDtypeStruct(shape, kind) for s...  17.3 us
    pallas_call x1, Pallas kernels, local(): pl.pallas_call(partial(out_kernel, n), out_shape=[jax.ShapeDtypeStruct((r...  15.1 us
  transfers between devices with their start and end apart: 4, of which 1 were waited for; matrix products, arithmetic and copies ran while one was open for 2% of the time, Pallas kernels for 43%

profile of v3, /device:TPU:0, one launch (start us, length us, event | category | flops | bytes accessed | tf_op | source)
XLA Modules:
  0.0 473.6 jit_solution(17291450972701430850)
XLA Ops:
  7.2 0.0 all-gather.7.cloned.1.call-start
  7.2 4.0 pack.1
  11.2 0.0 copy-start
  11.3 0.0 all-gather.7.cloned.1.call-update
  11.3 0.0 all-gather.5.cloned.1.call-start
  11.3 0.5 collective-permute-start
  12.5 0.3 copy-done
  12.8 0.0 copy-start.2
  12.8 1.6 bitcast_select_fusion.g_own
  14.4 0.5 collective-permute-start.1
  14.9 0.0 copy-done.2
  14.9 0.0 copy-done.3
  14.9 0.1 fusion.10
  15.0 0.0 copy-done.4
  15.0 0.0 copy-done.5
  15.0 0.6 fusion.7.refs_4_
  15.6 54.8 %gather.1 = (bf16[1024,1024]{1,0:T(8,128)(2,1)}, bf16[512,1024]{1,0:T(8,128)(2,1)}, bf16[4,16,256]{2,1,0:T(8,128)(2,1)}, bf16[1024,1024]{1,0:T(8,128)(2,1)}) custom-call(bf16[256,1024]{1,0:T(8,128)(2,1)} %refs_0_.3, bf16[256,512]{1,0:T(8,128)(2,1)} %refs_1_.3, bf16[256,512]{1,0:T(8,128)(2,1)} %refs_2_.4, bf16[256,1024]{1,0:T(8,128)(2,1)} %refs_3_.1, ...), custom_call_target="tpu_custom_call" | custom-call | tf_op jit(solution)/shard_map/gather/pallas_call | solution.py:1578
  70.4 0.9 slice_reduce_fusion.1
  71.3 0.1 convert_element_type.40
  71.4 0.1 convert_element_type.41
  71.5 0.7 tile.32.gh_ref
  72.2 0.8 fusion.11
  73.0 0.6 convert.5.ga_ref
  73.6 0.6 fusion.2
  74.2 1.0 copy.29.sin_ref
  75.2 1.0 copy.28.cos_ref
  76.2 0.0 collective-permute-done
  76.2 1.2 pad_add_fusion.lens_ref
  77.4 17.3 %qkv.1 = (bf16[2048,1024]{1,0:T(8,128)(2,1)}, f32[2048,768]{1,0:T(8,128)}, bf16[2048,1024]{1,0:T(8,128)(2,1)}, bf16[2048,512]{1,0:T(8,128)(2,1)}, bf16[2048,512]{1,0:T(8,128)(2,1)}) custom-call(s32[2]{0:T(128)} %pad_add_fusion.lens_ref, bf16[1024,1024]{1,0:T(8,128)(2,1)} %bitcast.22, bf16[1024,1024]{1,0:T(8,128)(2,1)} %get-tuple-element.86.other_ref, ...), custom_call_target="tpu_custom_call" | custom-call | flops 4294967296 | bytes 16777216 | tf_op jit(solution)/shard_map/qkv/pallas_call | solution.py:1447
  94.7 14.9 %attend.1 = (bf16[2048,512]{1,0:T(8,128)(2,1)}, bf16[2048,1024]{1,0:T(8,128)(2,1)}) custom-call(s32[2]{0:T(128)} %pad_add_fusion.lens_ref, bf16[2048,1024]{1,0:T(8,128)(2,1)} %get-tuple-element.89.q_ref, bf16[2048,512]{1,0:T(8,128)(2,1)} %get-tuple-element.90.k_ref, bf16[2048,512]{1,0:T(8,128)(2,1)} %get-tuple-element.91.v_ref), custom_call_target="tpu_custom_call" | custom-call | flops 8589934592 | bytes 8388608 | tf_op jit(solution)/shard_map/attend/pallas_call | solution.py:898
  109.6 0.0 all-gather.5.cloned.1.call-update
  109.6 0.6 convert.6.gain_ref.refs_4_
  110.2 15.1 %out.1 = (f32[1024,1024]{1,0:T(8,128)}, bf16[1024,1024]{1,0:T(8,128)(2,1)}, f32[8,1024]{1,0:T(8,128)}, bf16[1024,1024]{1,0:T(8,128)(2,1)}) custom-call(s32[1]{0:T(128)} %copy.34.length_ref.refs_2_, bf16[2048,512]{1,0:T(8,128)(2,1)} %get-tuple-element.93.att_ref, bf16[512,1024]{1,0:T(8,128)(2,1)} %get-tuple-element.94.w_ref, bf16[1024,1024]{1,0:T(8,128)(2,1)} %bitcast.23, ...), custom_call_target="tpu_custom_call" | custom-call | flops 2147483648 | bytes 16777216 | tf_op jit(solution)/shard_map/out/pallas_call | solution.py:1644
  125.3 0.0 collective-permute-done.1.g_other
  125.3 5.5 %all-gather.7.cloned.1.call-done = bf16[3072,1536]{1,0:T(8,128)(2,1)} async-done(((bf16[768,1536]{1,0:T(8,128)(2,1)}), bf16[3072,1536]{1,0:T(8,128)(2,1)}) %all-gather.7.cloned.1.call-update) | async-done | bytes 9437200 | tf_op jit(solution)/shard_map/all_gather | solution.py:1555
  130.7 48.8 %ffn.3 = (f32[2048,1024]{1,0:T(8,128)}, f32[2048,1024]{1,0:T(8,128)}, bf16[1536,1536]{1,0:T(8,128)(2,1)}) custom-call(bf16[1024,1024]{1,0:T(8,128)(2,1)} %get-tuple-element.95.x_own, bf16[1024,1024]{1,0:T(8,128)(2,1)} %get-tuple-element.96.x_other, bf16[1024,1024]{1,0:T(8,128)(2,1)} %bitcast_select_fusion.g_own, ...), custom_call_target="tpu_custom_call" | custom-call | flops 28991029248 | bytes 33554432 | tf_op jit(solution)/shard_map/ffn/pallas_call | solution.py:1701
  179.6 51.5 %ffn.4 = (f32[2048,1024]{1,0:T(8,128)}, f32[2048,1024]{1,0:T(8,128)}, bf16[1536,1536]{1,0:T(8,128)(2,1)}, bf16[384,1536]{1,0:T(8,128)(2,1)}) custom-call(bf16[1024,1024]{1,0:T(8,128)(2,1)} %get-tuple-element.95.x_own, bf16[1024,1024]{1,0:T(8,128)(2,1)} %get-tuple-element.96.x_other, bf16[1024,1024]{1,0:T(8,128)(2,1)} %bitcast_select_fusion.g_own, ...), custom_call_target="tpu_custom_call" | custom-call | flops 28991029248 | bytes 33554432 | tf_op jit(solution)/shard_map/ffn/pallas_call | solution.py:1701
  231.1 0.0 all-gather.5.cloned.1.call-done
  231.1 60.6 %ffn.5 = (bf16[1024,1024]{1,0:T(8,128)(2,1)}, f32[1024,1024]{1,0:T(8,128)}, bf16[1024,1024]{1,0:T(8,128)(2,1)}, f32[8,1024]{1,0:T(8,128)}, bf16[1024,1024]{1,0:T...) custom-call(bf16[1024,1024]{1,0:T(8,128)(2,1)} %get-tuple-element.95.x_own, ...), custom_call_target="tpu_custom_call" | custom-call | flops 28991029248 | bytes 33554432 | tf_op jit(solution)/shard_map/ffn/pallas_call | solution.py:1701
  291.7 18.9 %dout.1 = (bf16[2048,1024]{1,0:T(8,128)(2,1)}, bf16[1024,512]{1,0:T(8,128)(2,1)}) custom-call(bf16[1024,1024]{1,0:T(8,128)(2,1)} %get-tuple-element.109.own_ref, bf16[1024,1024]{1,0:T(8,128)(2,1)} %get-tuple-element.110.other_ref, bf16[2048,512]{1,0:T(8,128)(2,1)} %get-tuple-element.93.att_ref, bf16[512,1024]{1,0:T(8,128)(2,1)} %get-tuple-element.94.w_ref), custom_call_target="tpu_custom_call" | custom-call | flops 4294967296 | bytes 16777216 | tf_op jit(solution)/shard_map/dout/pallas_call | solution.py:1736
  310.6 53.1 %attend_back.1 = (f32[2048,512]{1,0:T(8,128)}, f32[2048,512]{1,0:T(8,128)}, f32[2048,512]{1,0:T(8,128)}, bf16[384,1536]{1,0:T(8,128)(2,1)}, bf16[384,1536]{1,0:T(8,128)(2,1)}) custom-call(bf16[2048,1024]{1,0:T(8,128)(2,1)} %get-tuple-element.108.q_ref, bf16[2048,512]{1,0:T(8,128)(2,1)} %get-tuple-element.90.k_ref, ...), custom_call_target="tpu_custom_call" | custom-call | flops 21474836480 | bytes 16777216 | tf_op jit(solution)/shard_map/attend_back/pallas_call | solution.py:922
  363.7 38.4 %qkv_back.1 = (bf16[1024,1024]{1,0:T(8,128)(2,1)}, bf16[1024,1024]{1,0:T(8,128)(2,1)}, f32[8,128]{1,0:T(8,128)}, f32[8,1024]{1,0:T(8,128)}, bf16[256,512]{1,0:T(8,128)(2,1)}, /*index=5*/bf16[256,1536]{1,0:T(8,128)(2,1)}) custom-call(f32[2048,512]{1,0:T(8,128)} %get-tuple-element.114.dq_ref, f32[2048,512]{1,0:T(8,128)} %get-tuple-element.115.dk_ref, ...), custom_call_target="tpu_custom_call" | custom-call | flops 8589934592 | bytes 16777216 | tf_op jit(solution)/shard_map/qkv_back/pallas_call | solution.py:1773
  402.1 49.1 %finish.1 = (bf16[128,1536]{1,0:T(8,128)(2,1)}, bf16[256,512]{1,0:T(8,128)(2,1)}, bf16[256,512]{1,0:T(8,128)(2,1)}, bf16[256,512]{1,0:T(8,128)(2,1)}, bf16[128,1...) custom-call(s32[1]{0:T(128)} %copy.34.length_ref.refs_2_, ...), custom_call_target="tpu_custom_call" | custom-call | tf_op jit(solution)/shard_map/finish/pallas_call | solution.py:772
  451.2 10.8 %assemble.1 = (f32[256,4608]{1,0:T(8,128)}, f32[256,4608]{1,0:T(8,128)}, f32[9,128,1024]{2,1,0:T(8,128)}, f32[256,1024]{1,0:T(8,128)}, f32[256,1024]{1,0:T(8,128...) custom-call(bf16[384,1536]{1,0:T(8,128)(2,1)} %get-tuple-element.123, ...), custom_call_target="tpu_custom_call" | custom-call | tf_op jit(solution)/shard_map/assemble/pallas_call | solution.py:1839
  462.0 0.0 copy-start.1
  462.0 3.2 copy.35
  465.3 0.0 copy-done.1
  465.3 1.3 copy.36
  (13 shorter events, 0.2 us)
Async XLA Ops:
  7.2 123.6 %all-gather.7.cloned.1.call-start = ((), (), s32[]{:S(2)}) async-start(), calls=%async_computation.1 | async-start | bytes 11796480 | tf_op jit(solution)/shard_map/all_gather | solution.py:1555
  11.2 1.6 copy-start
  11.3 219.8 %all-gather.5.cloned.1.call-start = ((), (), s32[]{:S(2)}) async-start(), calls=%async_computation | async-start | bytes 5898240 | tf_op jit(solution)/shard_map/all_gather | solution.py:1628
  11.3 64.9 %collective-permute-start = (s32[1]{0:T(128)}, s32[1]{0:T(128)}, u32[]{:S(2)}, u32[]{:S(2)}) collective-permute-start(s32[1]{0:T(128)} %param.15), channel_id=1, source_target_pairs={{0,4},{4,0},{8,12},{12,8},{16,20},{20,16},{24,28},{28,24},{1,5},{5... | collective-permute-start | bytes 20 | tf_op jit(solution)/shard_map/ppermute | solution.py:46
  12.8 2.1 copy-start.2
  12.8 2.1 copy-start.3
  12.8 2.1 copy-start.4
  12.8 2.1 copy-start.5
  14.4 110.8 %collective-permute-start.1 = (bf16[1024,1024]{1,0:T(8,128)(2,1)}, bf16[1024,1024]{1,0:T(8,128)(2,1)}, u32[]{:S(2)}, u32[]{:S(2)}) collective-permute-start(bf16[1024,1024]{1,0:T(8,128)(2,1)} %bitcast_select_fusion.g_own), channel_id=1, source_target_pairs={{0,4},{4,0},{8,12},{12,8},{16,20},{20,16},{24,28},{28,24},{1,5},{5... | collective-permute-start | bytes 6291464 | tf_op jit(solution)/shard_map/ppermute | solution.py:46
  462.0 3.2 copy-start.1
Sparse Core Ops, SparseCore 0:
  11.4 119.2 all-gather.6
  132.6 59.8 all-gather.4
